TPU v7x, 32 devices: a whole 2x2x4 slice. The times are simulated.
32 devices in a mesh: dp: 16 (over z, y, core), tensor: 2 (over x).
Axes of the slice: x: 2, y: 2, z: 4, core: 2. Of those that a mesh axis runs over, the one named last changes fastest.
Arguments:
- queries: bfloat16 [8192, 4096], P(('dp', 'tensor')), may hold values from -6 to 6
- key_rows: bfloat16 [8192, 512], P(('dp', 'tensor')), may hold values from -6 to 6
- value_rows: bfloat16 [8192, 512], P(('dp', 'tensor')), may hold values from -150 to 150
- norm_gain: float32 [4096], replicated, may hold values from 0.1 to 1.9
- labels: int32 [8192], P('dp'), may hold values from 0 to 12, as said below
- pair_list: int32 [16, 2], replicated, may hold values from 0 to 11, as said below
- owner_map: int32 [16], replicated, may hold values from 0 to 15, each once
Outputs:
- gram: bfloat16 [16, 4096, 4096], P('dp', 'tensor')
- harvest: bfloat16 [8192, 4096], P('dp', 'tensor')
Inputs may be any that keep to these rules, and one draw needn't show every extreme that they name: Class 12 marks a token without a class. Among the 512 tokens of one sequence every class 0 to 11 labels 1 to 12 tokens, and one class of the first listed pair labels exactly 12 tokens in every sequence. `pair_list`: 16 different pairs, the first class below the second.
All inputs are finite; a program needn't handle non-finite values.
Results may differ from a plain program's by a relative error of at most 0.0056.
Values may be sent and summed in bfloat16 or wider, within the bound.
No kernel may reach another device: no remote copies, remote signals or barrier semaphores. Data moves between devices by JAX's collectives and lax.ppermute only.
A program may use at most 128 MiB of HBM per device.

v0:
```python
import math

import jax
import jax.numpy as jnp
from jax import lax
from jax.sharding import PartitionSpec as P

H = 32
KVH = 4
HD = 128
D = 4096
C = 12
P_SIZE = 16
SLOT = 12


NEGATIVE = -1e30
EPSILON = 1e-06


def from_root(shard, axis, root):
    mine = lax.axis_index(axis) == root
    return lax.psum(jnp.where(mine, shard, jnp.zeros_like(shard)), axis)


def folded_keys(query_heads, key_heads, value_heads, offset, block_rows):
    local_rows, head_count, head_width = query_heads.shape
    kv_count = key_heads.shape[1]
    group_size = head_count // kv_count
    score_scale = 1.0 / math.sqrt(head_width)
    grouped = query_heads.reshape(local_rows, kv_count, group_size, head_width)
    positions = offset + jnp.arange(local_rows)
    initial = (
        jnp.full((kv_count, group_size, local_rows), NEGATIVE, jnp.float32),
        jnp.zeros((kv_count, group_size, local_rows), jnp.float32),
        jnp.zeros((kv_count, group_size, local_rows, head_width), jnp.float32),
    )
    pieces = (
        lax.all_gather(key_heads, "tensor", axis=0, tiled=True),
        lax.all_gather(value_heads, "tensor", axis=0, tiled=True),
    )
    piece_start = jnp.int32(0)

    def compute(state_in):
        row_max, row_total, accumulated = state_in
        key_piece, value_piece = pieces
        piece_rows = key_piece.shape[0]
        for sub_start in range(0, piece_rows, block_rows):
            key_block = key_piece[sub_start : sub_start + block_rows]
            value_block = value_piece[sub_start : sub_start + block_rows]
            span_rows = key_block.shape[0]
            scores = (
                jnp.einsum("skgd,nkd->kgsn", grouped, key_block, preferred_element_type=jnp.float32)
                * score_scale
            )
            key_places = piece_start + sub_start + jnp.arange(span_rows)
            allowed = key_places[None, :] <= positions[:, None]
            scores = jnp.where(allowed, scores, NEGATIVE)
            new_max = jnp.maximum(row_max, jnp.max(scores, axis=-1))
            expo_vals = jnp.where(allowed, jnp.exp(scores - new_max[..., None]), 0.0)
            factor = jnp.exp(row_max - new_max)
            row_total = row_total * factor + jnp.sum(expo_vals, axis=-1)
            accumulated = accumulated * factor[..., None] + jnp.einsum(
                "kgsn,nkd->kgsd",
                expo_vals.astype(jnp.bfloat16),
                value_block,
                preferred_element_type=jnp.float32,
            )
            row_max = new_max
        return (row_max, row_total, accumulated)

    row_max, row_total, accumulated = lax.cond(
        piece_start <= offset + local_rows - 1, compute, lambda state_in: state_in, initial
    )
    attended = accumulated / row_total[..., None]
    return jnp.transpose(attended, (2, 0, 1, 3)).reshape(local_rows, head_count * head_width)


def class_rows(harvest, labels, class_count, slot_count):
    seq_len = labels.shape[0]
    onehot = (labels[:, None] == jnp.arange(class_count, dtype=jnp.int32)[None, :]).astype(
        jnp.int32
    )
    ranks = jnp.cumsum(onehot, axis=0) - onehot
    picked = onehot[None, :, :] * (
        ranks[None, :, :] == jnp.arange(slot_count, dtype=jnp.int32)[:, None, None]
    ).astype(jnp.int32)
    positions = jnp.sum(picked * jnp.arange(seq_len, dtype=jnp.int32)[None, :, None], axis=1)
    present = jnp.sum(picked, axis=1)
    gathered = harvest[jnp.transpose(positions)]
    return gathered * jnp.transpose(present)[:, :, None].astype(harvest.dtype)


def local(queries, key_rows, value_rows, norm_gain, labels, pair_list, owner_map):
    tensor_count = lax.axis_size("tensor")
    group_count = lax.axis_size("dp")
    local_rows = queries.shape[0]
    seq_len = local_rows * tensor_count
    block_rows = min(seq_len, 512)
    part_width = D // tensor_count
    my_tensor = lax.axis_index("tensor")
    my_group = lax.axis_index("dp")
    query_heads = queries.reshape(local_rows, H, HD)
    key_heads = key_rows.reshape(local_rows, KVH, HD)
    value_heads = value_rows.reshape(local_rows, KVH, HD)
    attended = folded_keys(query_heads, key_heads, value_heads, my_tensor * local_rows, block_rows)
    squares = jnp.sum(attended * attended, axis=1)
    whole_rows = (attended * lax.rsqrt(squares / D + EPSILON)[:, None] * norm_gain[None, :]).astype(
        jnp.bfloat16
    )
    harvest = lax.all_to_all(whole_rows, "tensor", split_axis=1, concat_axis=0, tiled=True)
    class_ids = jnp.arange(C, dtype=jnp.int32)
    local_counts = jnp.sum((labels[:, None] == class_ids[None, :]).astype(jnp.float32), axis=0)
    counts = lax.psum(local_counts, "dp")
    per_class = class_rows(harvest, labels, C, SLOT)
    blocks_per_pair = group_count // P_SIZE
    dest_classes = pair_list[owner_map // blocks_per_pair]
    outgoing = per_class[dest_classes]
    incoming = lax.all_to_all(outgoing, "dp", split_axis=0, concat_axis=0, tiled=True)
    stacked = incoming.reshape(-1, part_width)
    my_block = owner_map[my_group]
    my_classes = pair_list[my_block // blocks_per_pair]
    my_share = my_block % blocks_per_pair
    pair_count = counts[my_classes[0]] + counts[my_classes[1]]
    slice_count = P_SIZE * tensor_count // group_count
    received = []
    for slot_index in range(slice_count):
        received.append(from_root(stacked, "tensor", my_share * slice_count + slot_index))
    chosen = jnp.concatenate(received, axis=1)
    tile = lax.dot_general(
        stacked, chosen, (((0,), (0,)), ((), ())), preferred_element_type=jnp.float32
    )
    return ((tile / pair_count).astype(jnp.bfloat16)[None], harvest)


def solution(mesh):
    return jax.shard_map(
        local,
        mesh=mesh,
        in_specs=(
            P(("dp", "tensor"), None),
            P(("dp", "tensor"), None),
            P(("dp", "tensor"), None),
            P(),
            P("dp"),
            P(),
            P(),
        ),
        out_specs=(P("dp", "tensor", None), P("dp", "tensor")),
        check_vma=False,
    )
```

profile of v0, /device:TPU:0, one launch (start us, length us, event | category | flops | bytes accessed | tf_op | source)
XLA Modules:
  0.0 249.4 jit_solution(2447600743895676012)
XLA Ops:
  7.2 0.7 mul.68
  7.9 1.1 copy.81
  9.0 9.9 %all_gather.6 = bf16[512,4,128]{0,2,1:T(8,128)(2,1)S(1)} all-gather(bf16[256,4,128]{0,2,1:T(8,128)(2,1)S(1)} %bitcast.67), channel_id=1, replica_groups=mesh['dp'=16,'tensor'=2] {'tensor'}, dimensions={0}, use_global_device_ids=true | all-gather | bytes 786432 | tf_op jit(solution)/shard_map/all_gather | solution.py:39
  18.9 1.1 copy.82
  20.0 8.1 %all_gather.7 = bf16[512,4,128]{0,2,1:T(8,128)(2,1)S(1)} all-gather(bf16[256,4,128]{0,2,1:T(8,128)(2,1)S(1)} %bitcast.68), channel_id=1, replica_groups=mesh['dp'=16,'tensor'=2] {'tensor'}, dimensions={0}, use_global_device_ids=true | all-gather | bytes 786432 | tf_op jit(solution)/shard_map/all_gather | solution.py:40
  28.2 22.9 %conditional.1 = (f32[4,8,256]{2,1,0:T(8,128)S(1)}, f32[4,8,256,128]{2,3,1,0:T(8,128)}) conditional(s32[]{:T(128)} %convert_element_type.35, () %tuple.16, (s32[]{:T(128)}, s32[256]{0:T(256)S(1)}, bf16[256,4096]{1,0:T(8,128)(2,1)}, bf16[512,4,128]{0,2,1:T(8,128)(2,1)S(1)}, bf16[512,4,128]{0,2,1:T(8,128)(2,1)S(1)}) %tuple.17), branch_computations={%region_0.0_spmd, %region_1.4_spmd} | conditional | flops 2203214080 | bytes 71142416 | solution.py:72
  28.2 0.1 iota_compare_fusion
  28.2 2.1 copy.107
  30.3 4.2 %fusion = (f32[4,8,256]{2,1,0:T(8,128)S(1)}, f32[4,512,256,8]{2,1,3,0:T(8,128)S(1)}) fusion(pred[256,512]{0,1:T(8,128)(4,1)S(1)} %iota_compare_fusion, bf16[256,4,8,128]{3,2,1,0:T(8,128)(2,1)S(1)} %bitcast.63, bf16[512,4,128]{0,2,1:T(8,128)(2,1)S(1)} %get-tuple-element.49), kind=kOutput, calls=%fused_computation.5 | convolution fusion | flops 1086316544 | bytes 19562496 | tf_op jit(solution)/shard_map/cond/branch_1_fun/skgd,nkd->kgsn/dot_general | solution.py:53
  34.5 4.2 %fusion.2 = f32[4,8,256]{2,1,0:T(8,128)S(1)} fusion(f32[4,512,256,8]{2,1,3,0:T(8,128)S(1)} %get-tuple-element.61, f32[4,8,256]{2,1,0:T(8,128)S(1)} %broadcast_maximum_fusion, pred[256,512]{0,1:T(8,128)(4,1)S(1)} %iota_compare_fusion), kind=kLoop, calls=%fused_computation.7 | loop fusion | flops 20963328 | bytes 16973824 | tf_op jit(solution)/shard_map/cond/branch_1_fun/reduce_sum | solution.py:62
  38.7 7.0 %broadcast_add_fusion = f32[4,8,256,128]{3,2,1,0:T(8,128)} fusion(f32[4,8,256]{2,1,0:T(8,128)S(1)} %get-tuple-element.58, f32[4,512,256,8]{2,1,3,0:T(8,128)S(1)} %get-tuple-element.61, f32[4,8,256]{2,1,0:T(8,128)S(1)} %broadcast_maximum_fusion, pred[256,512]{0,1:T(8,128)(4,1)S(1)} %iota_compare_fusion, bf16[512,4,128]{0,2,1:T(8,128)(2,1)S(1)} %get-tuple-element.50), kind=kOutput, calls=%fused_computation.12 | convolution fusion | flops 1095761920 | bytes 21692416 | tf_op jit(solution)/shard_map/cond/branch_1_fun/kgsn,nkd->kgsd/dot_general | solution.py:63
  45.7 5.3 %copy.106 = f32[4,8,256,128]{2,3,1,0:T(8,128)} copy(f32[4,8,256,128]{3,2,1,0:T(8,128)} %broadcast_add_fusion) | data formatting | bytes 8388608 | tf_op jit(solution)/shard_map/cond | solution.py:72
  51.0 2.8 %fusion.17 = (f32[256]{0:T(256)S(1)}, f32[4,8,256,128]{2,3,1,0:T(8,128)S(1)}) fusion(f32[4,8,256,128]{2,3,1,0:T(8,128)} %get-tuple-element.51, f32[4,8,256]{2,1,0:T(8,128)S(1)} %get-tuple-element.23), kind=kLoop, calls=%fused_computation.26 | loop fusion | flops 3145472 | bytes 8422400 | tf_op jit(solution)/shard_map/reduce_sum | solution.py:107
  53.9 0.0 copy-start.5
  53.9 0.0 copy-start.4
  53.9 0.0 copy-start.3
  53.9 1.7 multiply_convert_fusion
  55.6 3.9 %all-to-all-start = ((bf16[256,2,2048]{0,2,1:T(8,128)(2,1)}), bf16[256,2,2048]{0,2,1:T(8,128)(2,1)S(1)}, u32[]{:S(2)}, u32[]{:S(2)}) async-start(bf16[256,2,2048]{0,2,1:T(8,128)(2,1)} %multiply_convert_fusion), calls=%async_computation | async-start | bytes 4194304 | tf_op jit(solution)/shard_map/all_to_all | solution.py:111
  59.6 0.0 copy-done.5
  59.6 0.0 copy-done.4
  59.6 0.1 copy.90
  59.7 0.6 gather_fusion.1
  60.3 0.1 copy.91
  60.3 0.0 copy-done.3
  60.4 1.2 reduce-window.6
  61.5 0.2 slice_reduce_fusion
  61.8 0.1 broadcast_add_fusion.2
  61.9 0.1 copy.92
  62.0 0.1 reshape.123
  62.1 0.5 select_reduce_fusion
  62.6 0.1 copy.89
  62.7 0.1 copy.88
  62.8 0.1 reshape.107
  62.9 20.1 %all-to-all-done = bf16[256,2,2048]{0,2,1:T(8,128)(2,1)S(1)} async-done(((bf16[256,2,2048]{0,2,1:T(8,128)(2,1)}), bf16[256,2,2048]{0,2,1:T(8,128)(2,1)S(1)}, u32[]{:S(2)}, u32[]{:S(2)}) %all-to-all-start) | async-done | bytes 2097184 | tf_op jit(solution)/shard_map/all_to_all | solution.py:111
  83.1 0.0 copy-start.1
  83.1 1.3 copy-done.1
  84.4 2.9 %copy.86 = bf16[2,256,2048]{2,1,0:T(8,128)(2,1)S(1)} copy(bf16[2,256,2048]{1,2,0:T(8,128)(2,1)} %bitcast.65) | data formatting | bytes 4194304 | tf_op jit(solution)/shard_map/all_to_all | solution.py:111
  87.3 0.0 copy-start
  87.3 1.0 gather_fusion
  88.3 1.0 reshape.106
  89.3 0.0 copy-done
  89.3 1.3 broadcast_multiply_fusion
  90.6 0.7 gather_fusion.2
  91.3 2.8 %copy.94 = bf16[16,2,12,2048]{3,1,2,0:T(2,128)(2,1)} copy(bf16[16,2,12,2048]{3,2,1,0:T(8,128)(2,1)S(1)} %bitcast.64) | data formatting | bytes 3145728 | tf_op jit(solution)/shard_map/gather | solution.py:118
  94.1 5.7 %all-to-all-start.1 = ((bf16[16,2,12,2048]{3,1,2,0:T(2,128)(2,1)}), bf16[16,2,12,2048]{3,1,2,0:T(2,128)(2,1)}, u32[]{:S(2)}, u32[]{:S(2)}) async-start(bf16[16,2,12,2048]{3,1,2,0:T(2,128)(2,1)} %copy.94), calls=%async_computation.1 | async-start | bytes 3145728 | tf_op jit(solution)/shard_map/all_to_all | solution.py:119
  99.7 0.0 all-reduce.3.cloned.1.call-start
  99.8 31.9 %all-to-all-done.1 = bf16[16,2,12,2048]{3,1,2,0:T(2,128)(2,1)} async-done(((bf16[16,2,12,2048]{3,1,2,0:T(2,128)(2,1)}), bf16[16,2,12,2048]{3,1,2,0:T(2,128)(2,1)}, u32[]{:S(2)}, u32[]{:S(2)}) %all-to-all-start.1) | async-done | bytes 1572896 | tf_op jit(solution)/shard_map/all_to_all | solution.py:119
  131.6 2.2 copy.95
  133.8 1.3 reshape.104
  135.1 0.0 copy-start.2
  135.1 3.4 %broadcast_select_fusion.1 = (bf16[384,2048]{1,0:T(8,128)(2,1)}, bf16[384,2048]{1,0:T(8,128)(2,1)}) fusion(bf16[384,2048]{1,0:T(8,128)(2,1)} %reshape.104, pred[]{:T(512)S(6)} %eq.65, pred[]{:T(512)S(6)} %eq.66), kind=kLoop, calls=%fused_computation.33 | loop fusion | flops 1572864 | bytes 4718594 | tf_op jit(solution)/shard_map/jit(_where)/select_n | solution.py:23
  138.6 0.0 all-reduce.3.cloned.1.call-update
  138.6 0.1 convert_reduce_fusion
  138.7 37.2 %psum.23 = f32[12]{0:T(128)S(1)} all-reduce(f32[12]{0:T(128)S(1)} %convert_reduce_fusion), channel_id=1, replica_groups=mesh['dp'=16,'tensor'=2] {'dp'}, use_global_device_ids=true, to_apply=%region_12.13 | all-reduce | flops 12 | bytes 96 | tf_op jit(solution)/shard_map/psum | solution.py:114
  175.9 0.6 dynamic_slice.12
  178.2 0.1 constant_dynamic-slice_fusion
  178.3 0.5 fusion.25
  182.5 0.7 fusion.26
  184.4 43.7 %all-reduce.3.cloned.1.call-done = (bf16[384,2048]{1,0:T(8,128)(2,1)}, bf16[384,2048]{1,0:T(8,128)(2,1)}) async-done(((bf16[384,2048]{1,0:T(8,128)(2,1)}, bf16[384,2048]{1,0:T(8,128)(2,1)}), (bf16[384,2048]{1,0:T(8,128)(2,1)}, bf16[384,2048]{1,0:T(8,128)(2,1)})) %all-reduce.3.cloned.1.call-update) | async-done | bytes 3145744 | tf_op jit(solution)/shard_map/psum | solution.py:23
  228.1 0.0 copy-done.2
  228.1 14.4 %fusion.16 = bf16[1,2048,4096]{2,1,0:T(8,128)(2,1)} fusion(f32[]{:T(128)} %bitcast.18, bf16[384,2048]{1,0:T(8,128)(2,1)S(1)} %copy-done.2, bf16[384,2048]{1,0:T(8,128)(2,1)} %get-tuple-element.54, bf16[384,2048]{1,0:T(8,128)(2,1)} %get-tuple-element.55), kind=kOutput, calls=%fused_computation.24 | convolution fusion | flops 6465519616 | bytes 21495812 | tf_op jit(solution)/shard_map/dot_general | solution.py:130
  (20 shorter events, 0.2 us)
Async XLA Ops:
  53.9 5.7 %copy-start.5 = (s32[16]{0:T(128)S(1)}, s32[16]{0:T(128)}, u32[]{:S(2)}) copy-start(s32[16]{0:T(128)} %param.15) | copy-start | bytes 196
  53.9 5.7 %copy-start.4 = (s32[16,2]{0,1:T(2,128)S(1)}, s32[16,2]{0,1:T(2,128)}, u32[]{:S(2)}) copy-start(s32[16,2]{0,1:T(2,128)} %param.14) | copy-start | bytes 388
  53.9 6.4 %copy-start.3 = (s32[512]{0:T(512)S(1)}, s32[512]{0:T(512)}, u32[]{:S(2)}) copy-start(s32[512]{0:T(512)} %param.13) | copy-start | bytes 6148
  55.6 27.4 %all-to-all-start = ((bf16[256,2,2048]{0,2,1:T(8,128)(2,1)}), bf16[256,2,2048]{0,2,1:T(8,128)(2,1)S(1)}, u32[]{:S(2)}, u32[]{:S(2)}) async-start(bf16[256,2,2048]{0,2,1:T(8,128)(2,1)} %multiply_convert_fusion), calls=%async_computation | async-start | bytes 4194304 | tf_op jit(solution)/shard_map/all_to_all | solution.py:111
  83.1 1.3 copy-start.1
  87.3 2.0 copy-start
  94.1 37.6 %all-to-all-start.1 = ((bf16[16,2,12,2048]{3,1,2,0:T(2,128)(2,1)}), bf16[16,2,12,2048]{3,1,2,0:T(2,128)(2,1)}, u32[]{:S(2)}, u32[]{:S(2)}) async-start(bf16[16,2,12,2048]{3,1,2,0:T(2,128)(2,1)} %copy.94), calls=%async_computation.1 | async-start | bytes 3145728 | tf_op jit(solution)/shard_map/all_to_all | solution.py:119
  99.7 128.4 %all-reduce.3.cloned.1.call-start = ((), (), s32[]{:S(2)}) async-start(), calls=%async_computation.2 | async-start | bytes 6291456 | tf_op jit(solution)/shard_map/psum | solution.py:23
  135.1 93.0 %copy-start.2 = (bf16[384,2048]{1,0:T(8,128)(2,1)S(1)}, bf16[384,2048]{1,0:T(8,128)(2,1)}, u32[]{:S(2)}) copy-start(bf16[384,2048]{1,0:T(8,128)(2,1)} %reshape.104) | copy-start | bytes 4718596
Sparse Core Ops, SparseCore 0:
  138.7 89.3 all-reduce.2
where the time goes:
time: 250 us; the launch traced here: 249 us
  waiting for transfers between devices  95.7 us (38%)
  blocking collectives  55.3 us (22%)
  local copies, waits for them, and re-layouts  26.8 us (11%)
  matrix products  25.6 us (10%)
  between operations  20.9 us (8%)
  other arithmetic  15.4 us (6%)
  starting transfers between devices  9.65 us (4%)
    psum x1, waiting for transfers between devices, from_root(): return lax.psum(jnp.where(mine, shard, jnp.zeros_like(shard)), axis)  43.7 us
    psum x1, blocking collectives, local(): counts = lax.psum(local_counts, 'dp')  37.2 us
    all_to_all x1, waiting for transfers between devices, local(): lax.all_to_all(outgoing, 'dp', split_axis=0, concat_axis=0, tiled=True)  31.9 us
    all_to_all x1, waiting for transfers between devices, local(): lax.all_to_all(whole_rows, 'tensor', split_axis=1, concat_axis=0, tiled=T...  20.1 us
    dot_general x1, matrix products, local(): lax.dot_general(stacked, chosen, (((0,), (0,)), ((), ())), preferred_elem...  14.4 us
    all_gather x1, blocking collectives, folded_keys(): lax.all_gather(key_heads, 'tensor', axis=0, tiled=True)  9.94 us
    all_gather x1, blocking collectives, folded_keys(): lax.all_gather(value_heads, 'tensor', axis=0, tiled=True)  8.13 us
    dot_general x1, matrix products, compute(): jnp.einsum('kgsn,nkd->kgsd', expo_vals.astype(jnp.bfloat16), value_block,...  7 us
  transfers between devices with their start and end apart: 3, of which 3 were waited for; matrix products, arithmetic and copies ran while one was open for 2% of the time, Pallas kernels for 0%

commit v1 on v0

--- a/solution.py
+++ b/solution.py
@@ -3,6 +3,8 @@
 import jax
 import jax.numpy as jnp
 from jax import lax
+from jax.experimental import pallas as pl
+from jax.experimental.pallas import tpu as pltpu
 from jax.sharding import PartitionSpec as P
 
 H = 32
@@ -16,6 +18,9 @@
 
 NEGATIVE = -1e30
 EPSILON = 1e-06
+
+BF16 = jnp.bfloat16
+F32 = jnp.float32
 
 
 def from_root(shard, axis, root):
@@ -91,7 +96,7 @@
     return gathered * jnp.transpose(present)[:, :, None].astype(harvest.dtype)
 
 
-def local(queries, key_rows, value_rows, norm_gain, labels, pair_list, owner_map):
+def general_local(queries, key_rows, value_rows, norm_gain, labels, pair_list, owner_map):
     tensor_count = lax.axis_size("tensor")
     group_count = lax.axis_size("dp")
     local_rows = queries.shape[0]
@@ -133,9 +138,467 @@
     return ((tile / pair_count).astype(jnp.bfloat16)[None], harvest)
 
 
+BLOCKS = 8
+ROWS = 2 * SLOT
+EXTRA = HD
+VMEM_SPEC = pl.BlockSpec(memory_space=pltpu.VMEM)
+
+
+def cost(flops, moved, exps=0):
+    return pl.CostEstimate(flops=flops, bytes_accessed=moved, transcendentals=exps)
+
+
+def nt(left, right):
+    return lax.dot_general(left, right, (((1,), (1,)), ((), ())), preferred_element_type=F32)
+
+
+def dot(left, right):
+    return lax.dot_general(left, right, (((1,), (0,)), ((), ())), preferred_element_type=F32)
+
+
+def attend_heads(q_ref, kd, vd, ko, vo, use_off, put):
+    rows = q_ref.shape[0]
+    heads = q_ref.shape[1] // HD
+    factor = math.log2(math.e) / math.sqrt(HD)
+
+    def run(with_off):
+        row = lax.broadcasted_iota(jnp.int32, (rows, rows), 0)
+        col = lax.broadcasted_iota(jnp.int32, (rows, rows), 1)
+        allowed = col <= row
+        for head in range(heads):
+            query = q_ref[:, head * HD : (head + 1) * HD]
+            diag = jnp.where(allowed, nt(query, kd[...]), NEGATIVE)
+            peak = jnp.max(diag, axis=-1, keepdims=True)
+            if with_off:
+                off = nt(query, ko[...])
+                peak = jnp.maximum(peak, jnp.max(off, axis=-1, keepdims=True))
+            diag_w = jnp.exp2((diag - peak) * factor)
+            total = jnp.sum(diag_w, axis=-1, keepdims=True)
+            mixed = dot(diag_w.astype(BF16), vd[...])
+            if with_off:
+                off_w = jnp.exp2((off - peak) * factor)
+                total = total + jnp.sum(off_w, axis=-1, keepdims=True)
+                mixed = mixed + dot(off_w.astype(BF16), vo[...])
+            put(head, mixed * (1.0 / total))
+
+    @pl.when(use_off)
+    def _():
+        run(True)
+
+    @pl.when(jnp.logical_not(use_off))
+    def _():
+        run(False)
+
+
+def own_kernel(place, q_ref, k_ref, v_ref, kp_ref, vp_ref, att_ref, sq_ref):
+    sq_ref[...] = jnp.zeros_like(sq_ref)
+
+    def put(head, value):
+        att_ref[:, head * HD : (head + 1) * HD] = value
+        sq_ref[0] += value * value
+
+    attend_heads(q_ref, k_ref, v_ref, kp_ref, vp_ref, place[0] == 1, put)
+
+
+def attend_own(place, queries, key_rows, value_rows, partner_kv):
+    rows = queries.shape[0]
+    wide = D // KVH
+    return pl.pallas_call(
+        own_kernel,
+        grid_spec=pltpu.PrefetchScalarGridSpec(
+            num_scalar_prefetch=1,
+            grid=(2,),
+            in_specs=[
+                pl.BlockSpec((rows, wide), lambda i, t: (0, 2 * t[0] + i)),
+                pl.BlockSpec((rows, HD), lambda i, t: (0, 2 * t[0] + i)),
+                pl.BlockSpec((rows, HD), lambda i, t: (0, 2 * t[0] + i)),
+                pl.BlockSpec((rows, HD), lambda i, t: (0, i)),
+                pl.BlockSpec((rows, HD), lambda i, t: (0, 2 + i)),
+            ],
+            out_specs=[
+                pl.BlockSpec((rows, wide), lambda i, t: (0, i)),
+                pl.BlockSpec((1, rows, HD), lambda i, t: (i, 0, 0)),
+            ],
+        ),
+        out_shape=[
+            jax.ShapeDtypeStruct((rows, 2 * wide), F32),
+            jax.ShapeDtypeStruct((2, rows, HD), F32),
+        ],
+        cost_estimate=cost(2 * 2 * 16 * rows * 2 * rows * HD, 4 << 20, 16 * rows * 2 * rows),
+        name="attend_own",
+    )(place, queries, key_rows, value_rows, partner_kv, partner_kv)
+
+
+def partner_a_kernel(
+    place, q_ref, kd, vd, ko, vo, own_ref, so_ref, sp_ref, att_ref, sq_ref, out_ref
+):
+    sq_ref[...] = jnp.zeros_like(sq_ref)
+
+    def put(head, value):
+        att_ref[:, head * HD : (head + 1) * HD] = value
+        sq_ref[...] += value * value
+
+    attend_heads(q_ref, kd, vd, ko, vo, place[0] == 0, put)
+    picked = dot(so_ref[...], own_ref[...].astype(BF16))
+    out_ref[...] = (picked + dot(sp_ref[...], att_ref[...].astype(BF16))).astype(BF16)
+
+
+def partner_specs(rows, wide, chunk):
+    return [
+        pl.BlockSpec((rows, wide), lambda i, t: (0, 0)),
+        pl.BlockSpec((rows, HD), lambda i, t: (0, chunk)),
+        pl.BlockSpec((rows, HD), lambda i, t: (0, 2 + chunk)),
+        pl.BlockSpec((rows, HD), lambda i, t: (0, 2 * t[0] + chunk)),
+        pl.BlockSpec((rows, HD), lambda i, t: (0, 2 * t[0] + chunk)),
+    ]
+
+
+def attend_partner_a(place, query_a, partner_kv, key_rows, value_rows, att_own, picks):
+    rows, wide = query_a.shape
+    out_rows = picks.shape[0]
+    return pl.pallas_call(
+        partner_a_kernel,
+        grid_spec=pltpu.PrefetchScalarGridSpec(
+            num_scalar_prefetch=1,
+            grid=(1,),
+            in_specs=partner_specs(rows, wide, 0)
+            + [
+                pl.BlockSpec((rows, wide), lambda i, t: (0, 0)),
+                pl.BlockSpec((out_rows, rows), lambda i, t: (0, t[0])),
+                pl.BlockSpec((out_rows, rows), lambda i, t: (0, 1 - t[0])),
+            ],
+            out_specs=[
+                pl.BlockSpec((rows, wide), lambda i, t: (0, 0)),
+                pl.BlockSpec((rows, HD), lambda i, t: (0, 0)),
+                pl.BlockSpec((out_rows, wide), lambda i, t: (0, 0)),
+            ],
+        ),
+        out_shape=[
+            jax.ShapeDtypeStruct((rows, wide), F32),
+            jax.ShapeDtypeStruct((rows, HD), F32),
+            jax.ShapeDtypeStruct((out_rows, wide), BF16),
+        ],
+        cost_estimate=cost(2 * 2 * 8 * rows * 2 * rows * HD, 3 << 20, 8 * rows * 2 * rows),
+        name="attend_partner_a",
+    )(place, query_a, partner_kv, partner_kv, key_rows, value_rows, att_own, picks, picks)
+
+
+def partner_b_kernel(place, q_ref, kd, vd, ko, vo, sqo_ref, sqa_ref, att_ref, sum_ref, sq_ref):
+    sq_ref[...] = sqa_ref[...]
+
+    def put(head, value):
+        att_ref[:, head * HD : (head + 1) * HD] = value
+        sq_ref[...] += value * value
+
+    attend_heads(q_ref, kd, vd, ko, vo, place[0] == 0, put)
+    ones = jnp.ones((8, HD), F32)
+
+    def lanes(values):
+        return lax.dot_general(
+            ones,
+            values,
+            (((1,), (1,)), ((), ())),
+            precision=lax.Precision.HIGHEST,
+            preferred_element_type=F32,
+        )
+
+    sum_ref[0:8, :] = lanes(sq_ref[...])
+    sum_ref[8:16, :] = lanes(sqo_ref[0] + sqo_ref[1])
+
+
+def attend_partner_b(place, query_b, partner_kv, key_rows, value_rows, sq_own, sq_a):
+    rows, wide = query_b.shape
+    return pl.pallas_call(
+        partner_b_kernel,
+        grid_spec=pltpu.PrefetchScalarGridSpec(
+            num_scalar_prefetch=1,
+            grid=(1,),
+            in_specs=partner_specs(rows, wide, 1)
+            + [
+                pl.BlockSpec((2, rows, HD), lambda i, t: (0, 0, 0)),
+                pl.BlockSpec((rows, HD), lambda i, t: (0, 0)),
+            ],
+            out_specs=[
+                pl.BlockSpec((rows, wide), lambda i, t: (0, 0)),
+                pl.BlockSpec((16, rows), lambda i, t: (0, 0)),
+            ],
+            scratch_shapes=[pltpu.VMEM((rows, HD), F32)],
+        ),
+        out_shape=[
+            jax.ShapeDtypeStruct((rows, wide), F32),
+            jax.ShapeDtypeStruct((16, rows), F32),
+        ],
+        cost_estimate=cost(2 * 2 * 8 * rows * 2 * rows * HD, 2 << 20, 8 * rows * 2 * rows),
+        name="attend_partner_b",
+    )(place, query_b, partner_kv, partner_kv, key_rows, value_rows, sq_own, sq_a)
+
+
+def norm_kernel(
+    place, own_ref, pa_ref, pb_ref, mine_ref, theirs_ref, gain_ref, so_ref, sp_ref, h_ref, out_ref
+):
+    rows = own_ref.shape[0]
+    wide = pa_ref.shape[1]
+    ones = jnp.full((8, HD), 0.125, F32)
+
+    def scale_of(first, second):
+        total = lax.dot_general(
+            first + second,
+            ones,
+            (((0,), (0,)), ((), ())),
+            precision=lax.Precision.HIGHEST,
+            preferred_element_type=F32,
+        )
+        return lax.rsqrt(total * (1.0 / D) + EPSILON)
+
+    lane = lax.broadcasted_iota(jnp.int32, (rows, HD), 1)
+
+    def coded(scale):
+        high = scale.astype(BF16)
+        rest = scale - high.astype(F32)
+        low = rest.astype(BF16)
+        last = (rest - low.astype(F32)).astype(BF16)
+        picked = jnp.where(lane == 0, high.astype(F32), 0.0)
+        picked = jnp.where(lane == 1, low.astype(F32), picked)
+        picked = jnp.where(lane == 2, last.astype(F32), picked)
+        return jnp.where(lane == 3, 1.0, picked).astype(BF16)
+
+    own_scale = scale_of(mine_ref[8:16, :], theirs_ref[0:8, :])
+    other_scale = scale_of(mine_ref[0:8, :], theirs_ref[8:16, :])
+    own_at = pl.ds(pl.multiple_of(place[0] * rows, rows), rows)
+    other_at = pl.ds(pl.multiple_of((1 - place[0]) * rows, rows), rows)
+    gain = gain_ref[...]
+    h_ref[own_at, :] = (own_ref[...] * own_scale[:, 0:1] * gain).astype(BF16)
+    h_ref[other_at, 0:wide] = (pa_ref[...] * other_scale[:, 0:1] * gain[:, 0:wide]).astype(BF16)
+    h_ref[other_at, wide:] = (pb_ref[...] * other_scale[:, 0:1] * gain[:, wide:]).astype(BF16)
+    picks_own = so_ref[...]
+    picks_other = sp_ref[...]
+    picked = dot(picks_own, h_ref[own_at, wide:]) + dot(picks_other, h_ref[other_at, wide:])
+    out_ref[:, 0:wide] = picked.astype(BF16)
+    extra = dot(picks_own, coded(own_scale)) + dot(picks_other, coded(other_scale))
+    out_ref[:, wide:] = extra.astype(BF16)
+
+
+def normalize(place, att_own, att_a, att_b, mine, theirs, norm_gain, picks):
+    rows, half = att_own.shape
+    wide = half // 2
+    out_rows = picks.shape[0]
+    whole = lambda i, t: (0, 0)
+    return pl.pallas_call(
+        norm_kernel,
+        grid_spec=pltpu.PrefetchScalarGridSpec(
+            num_scalar_prefetch=1,
+            grid=(1,),
+            in_specs=[
+                pl.BlockSpec((rows, half), whole),
+                pl.BlockSpec((rows, wide), whole),
+                pl.BlockSpec((rows, wide), whole),
+                pl.BlockSpec((16, rows), whole),
+                pl.BlockSpec((16, rows), whole),
+                pl.BlockSpec((1, half), lambda i, t: (0, t[0])),
+                pl.BlockSpec((out_rows, rows), lambda i, t: (0, t[0])),
+                pl.BlockSpec((out_rows, rows), lambda i, t: (0, 1 - t[0])),
+            ],
+            out_specs=[
+                pl.BlockSpec((2 * rows, half), whole),
+                pl.BlockSpec((out_rows, wide + EXTRA), whole),
+            ],
+        ),
+        out_shape=[
+            jax.ShapeDtypeStruct((2 * rows, half), BF16),
+            jax.ShapeDtypeStruct((out_rows, wide + EXTRA), BF16),
+        ],
+        cost_estimate=cost(2 * out_rows * 2 * rows * wide, 8 << 20),
+        name="normalize",
+    )(place, att_own, att_a, att_b, mine, theirs, norm_gain, picks, picks)
+
+
+def picks_kernel(col_ref, row_ref, key_ref, out_ref):
+    tokens = row_ref.shape[1]
+    label = row_ref[...]
+    before = lax.broadcasted_iota(jnp.int32, (tokens, tokens), 0)
+    at = lax.broadcasted_iota(jnp.int32, (tokens, tokens), 1)
+    same = jnp.logical_and(col_ref[...] == label, before < at)
+    rank = jnp.sum(jnp.where(same, 1, 0), axis=0, keepdims=True)
+    token_key = jnp.where(jnp.logical_and(label < C, rank < 16), label * 16 + rank, -1)
+    out_ref[...] = jnp.where(key_ref[...] == token_key, 1.0, 0.0).astype(BF16)
+
+
+def class_picks(labels, classes):
+    tokens = labels.shape[0]
+    slots = jnp.arange(SLOT, dtype=jnp.int32)
+    keys = (classes[:, :, None] * 16 + slots[None, None, :]).reshape(-1, 1)
+    return pl.pallas_call(
+        picks_kernel,
+        in_specs=[VMEM_SPEC] * 3,
+        out_specs=VMEM_SPEC,
+        out_shape=jax.ShapeDtypeStruct((keys.shape[0], tokens), BF16),
+        cost_estimate=cost(4 * tokens * tokens, 1 << 20),
+        name="class_picks",
+    )(labels.reshape(tokens, 1), labels.reshape(1, tokens), keys)
+
+
+def gram_own_kernel(place, *refs):
+    a_refs = refs[0:BLOCKS]
+    b_refs = refs[BLOCKS : 2 * BLOCKS]
+    gain_ref, out_ref, turned_ref, extra_ref, rows_ref = refs[2 * BLOCKS :]
+    span = 2 * ROWS
+    wide = a_refs[0].shape[1]
+    step = out_ref.shape[0]
+
+    @pl.when(pl.program_id(0) == 0)
+    def _():
+        for block in range(BLOCKS):
+            at = slice(block * span, (block + 1) * span)
+            extra = b_refs[block][:, wide:].astype(F32)
+            extra_ref[at, :] = extra
+            scale = extra[:, 0:1] + extra[:, 1:2] + extra[:, 2:3]
+            scaled = a_refs[block][...].astype(F32) * scale * gain_ref[:, 0:wide]
+            rows_ref[at, 0:wide] = scaled.astype(BF16)
+            rows_ref[at, wide:] = b_refs[block][:, 0:wide]
+        turned_ref[...] = jnp.transpose(rows_ref[...])
+
+    count = jnp.sum(extra_ref[:, 3:4])
+    left = turned_ref[pl.ds(pl.multiple_of(pl.program_id(0) * step, step), step), :]
+    out_ref[...] = (dot(left, rows_ref[...]) * (1.0 / count)).astype(BF16)
+
+
+def gram_own(place, pieces_a, pieces_b, norm_gain):
+    wide = pieces_a[0].shape[1]
+    half = 2 * wide
+    total = BLOCKS * 2 * ROWS
+    step = 512
+    whole = lambda i, t: (0, 0)
+    return pl.pallas_call(
+        gram_own_kernel,
+        grid_spec=pltpu.PrefetchScalarGridSpec(
+            num_scalar_prefetch=1,
+            grid=(half // step,),
+            in_specs=[pl.BlockSpec((2 * ROWS, wide), whole)] * BLOCKS
+            + [pl.BlockSpec((2 * ROWS, wide + EXTRA), whole)] * BLOCKS
+            + [pl.BlockSpec((1, half), lambda i, t: (0, t[0]))],
+            out_specs=[
+                pl.BlockSpec((step, half), lambda i, t: (i, t[0])),
+                pl.BlockSpec((half, total), whole),
+                pl.BlockSpec((total, EXTRA), whole),
+            ],
+            scratch_shapes=[pltpu.VMEM((total, half), BF16)],
+        ),
+        out_shape=[
+            jax.ShapeDtypeStruct((half, 2 * half), BF16),
+            jax.ShapeDtypeStruct((half, total), BF16),
+            jax.ShapeDtypeStruct((total, EXTRA), F32),
+        ],
+        cost_estimate=cost(2 * half * half * total, 14 << 20),
+        name="gram_own",
+    )(place, *pieces_a, *pieces_b, norm_gain)
+
+
+def gram_other_kernel(place, *refs):
+    a_refs = refs[0:BLOCKS]
+    b_refs = refs[BLOCKS : 2 * BLOCKS]
+    gain_ref, turned_ref, extra_ref, _, out_ref, rows_ref = refs[2 * BLOCKS :]
+    span = 2 * ROWS
+    wide = a_refs[0].shape[1]
+
+    @pl.when(pl.program_id(0) == 0)
+    def _():
+        for block in range(BLOCKS):
+            at = slice(block * span, (block + 1) * span)
+            extra = extra_ref[at, :]
+            scale = extra[:, 0:1] + extra[:, 1:2] + extra[:, 2:3]
+            scaled = a_refs[block][...].astype(F32) * scale * gain_ref[:, 0:wide]
+            rows_ref[at, 0:wide] = scaled.astype(BF16)
+            rows_ref[at, wide:] = b_refs[block][...]
+
+    count = jnp.sum(extra_ref[:, 3:4])
+    out_ref[...] = (dot(turned_ref[...], rows_ref[...]) * (1.0 / count)).astype(BF16)
+
+
+def gram_other(place, pieces_a, pieces_b, norm_gain, turned, extra, partial):
+    wide = pieces_a[0].shape[1]
+    half = 2 * wide
+    total = BLOCKS * 2 * ROWS
+    step = 512
+    whole = lambda i, t: (0, 0)
+    return pl.pallas_call(
+        gram_other_kernel,
+        grid_spec=pltpu.PrefetchScalarGridSpec(
+            num_scalar_prefetch=1,
+            grid=(half // step,),
+            in_specs=[pl.BlockSpec((2 * ROWS, wide), whole)] * (2 * BLOCKS)
+            + [
+                pl.BlockSpec((1, half), lambda i, t: (0, 1 - t[0])),
+                pl.BlockSpec((step, total), lambda i, t: (i, 0)),
+                pl.BlockSpec((total, EXTRA), whole),
+                pl.BlockSpec(memory_space=pl.ANY),
+            ],
+            out_specs=pl.BlockSpec((step, half), lambda i, t: (i, 1 - t[0])),
+            scratch_shapes=[pltpu.VMEM((total, half), BF16)],
+        ),
+        out_shape=jax.ShapeDtypeStruct((half, 2 * half), BF16),
+        input_output_aliases={2 * BLOCKS + 4: 0},
+        cost_estimate=cost(2 * half * half * total, 14 << 20),
+        name="gram_other",
+    )(place, *pieces_a, *pieces_b, norm_gain, turned, extra, partial)
+
+
+def paired_local(queries, key_rows, value_rows, norm_gain, labels, pair_list, owner_map):
+    group_count = lax.axis_size("dp")
+    my_tensor = lax.axis_index("tensor")
+    my_group = lax.axis_index("dp")
+    place = jnp.full((1,), my_tensor, jnp.int32)
+    wide = D // KVH
+    swap = [(0, 1), (1, 0)]
+
+    def across(value):
+        return lax.ppermute(value, "tensor", swap)
+
+    def hop(value, offset):
+        return lax.ppermute(value, "dp", [(i, i ^ offset) for i in range(group_count)])
+
+    def theirs(rows, start, width):
+        return lax.dynamic_slice_in_dim(rows, (1 - my_tensor) * start, width, 1)
+
+    part = 2 * HD
+    sent_kv = jnp.concatenate([theirs(key_rows, part, part), theirs(value_rows, part, part)], 1)
+    partner_kv = across(sent_kv)
+    other_half = (1 - my_tensor) * 2 * wide
+    query_a = across(lax.dynamic_slice_in_dim(queries, other_half, wide, 1))
+    query_b = across(lax.dynamic_slice_in_dim(queries, other_half + wide, wide, 1))
+
+    order = jnp.concatenate([jnp.arange(0, 16, 2), jnp.arange(1, 16, 2)]).astype(jnp.int32)
+    classes = pair_list[owner_map[my_group ^ order]]
+    picks = class_picks(labels, classes)
+    gain = norm_gain.reshape(1, D)
+
+    def spread(rows):
+        width = rows.shape[1]
+        stay, leave = rows[: BLOCKS * ROWS], rows[BLOCKS * ROWS :]
+        came = hop(leave, 1)
+        joined = jnp.concatenate(
+            [stay.reshape(BLOCKS, ROWS, width), came.reshape(BLOCKS, ROWS, width)], 1
+        )
+        return [joined[0]] + [hop(joined[m], 2 * m) for m in range(1, BLOCKS)]
+
+    att_own, sq_own = attend_own(place, queries, key_rows, value_rows, partner_kv)
+    att_a, sq_a, rows_a = attend_partner_a(
+        place, query_a, partner_kv, key_rows, value_rows, att_own, picks
+    )
+    own_a = spread(rows_a)
+    other_a = [across(piece) for piece in own_a]
+    att_b, mine = attend_partner_b(place, query_b, partner_kv, key_rows, value_rows, sq_own, sq_a)
+    harvest, rows_b = normalize(place, att_own, att_a, att_b, mine, across(mine), gain, picks)
+    own_b = spread(rows_b)
+    other_b = [across(piece[:, :wide]) for piece in own_b]
+    partial, turned, extra = gram_own(place, own_a, own_b, gain)
+    gram = gram_other(place, other_a, other_b, gain, turned, extra, partial)
+    return gram[None], harvest
+
+
 def solution(mesh):
+    paired = mesh.shape["tensor"] == 2 and mesh.shape["dp"] == P_SIZE
     return jax.shard_map(
-        local,
+        paired_local if paired else general_local,
         mesh=mesh,
         in_specs=(
             P(("dp", "tensor"), None),

time: 250 us -> 138 us (0.55)
  blocking collectives: 55.3 us -> 0 us
  waiting for transfers between devices: 95.7 us -> 47.7 us
  Pallas kernels: 0 us -> 40.1 us
  starting transfers between devices: 9.65 us -> 38.2 us
  matrix products: 25.6 us -> 0 us
  between operations: 20.9 us -> 1.18 us
  local copies, waits for them, and re-layouts: 26.8 us -> 10.2 us
  other arithmetic: 15.4 us -> 0.33 us
    all_to_all x2 -> x0, waiting for transfers between devices: 52 us -> none  [the longest x1 31.9 us: local(): lax.all_to_all(outgoing, 'dp', split_axis=0, concat_axis=0, tiled=True)]
    ppermute x0 -> x36, waiting for transfers between devices: none -> 47.7 us  [the longest x20 30 us: across(): return lax.ppermute(value, 'tensor', swap)]
    psum x1 -> x0, waiting for transfers between devices: 43.7 us -> none  [from_root(): return lax.psum(jnp.where(mine, shard, jnp.zeros_like(shard)), axis)]
    pallas_call x0 -> x7, Pallas kernels: none -> 40.1 us  [the longest x1 9.13 us: gram_own(): pl.pallas_call(gram_own_kernel, grid_spec=pltpu.PrefetchScalarGridSpec(nu...]
    ppermute x0 -> x36, starting transfers between devices: none -> 38.2 us  [the longest x16 26.1 us: hop(): lax.ppermute(value, 'dp', [(i, i ^ offset) for i in range(group_count)])]
    psum x1 -> x0, blocking collectives: 37.2 us -> none  [local(): counts = lax.psum(local_counts, 'dp')]
    dot_general x3 -> x0, matrix products: 25.6 us -> none  [the longest x1 14.4 us: local(): lax.dot_general(stacked, chosen, (((0,), (0,)), ((), ())), preferred_elem...]
    all_gather x2 -> x0, blocking collectives: 18.1 us -> none  [the longest x1 9.94 us: folded_keys(): lax.all_gather(key_heads, 'tensor', axis=0, tiled=True)]
  transfers between devices with their start and end apart: 3 -> 36, of which waited for: 3 -> 13; matrix products, arithmetic and copies ran while one was open for 2% -> 4% of each run, Pallas kernels for 0% -> 19%
where the time goes in v1:
time: 138 us
  waiting for transfers between devices  47.7 us (35%)
  Pallas kernels  40.1 us (29%)
  starting transfers between devices  38.2 us (28%)
  local copies, waits for them, and re-layouts  10.2 us (7%)
    ppermute x20, waiting for transfers between devices, across(): return lax.ppermute(value, 'tensor', swap)  30 us
    ppermute x16, starting transfers between devices, hop(): lax.ppermute(value, 'dp', [(i, i ^ offset) for i in range(group_count)])  26.1 us
    ppermute x16, waiting for transfers between devices, hop(): lax.ppermute(value, 'dp', [(i, i ^ offset) for i in range(group_count)])  17.7 us
    ppermute x20, starting transfers between devices, across(): return lax.ppermute(value, 'tensor', swap)  12.1 us
    pallas_call x1, Pallas kernels, gram_own(): pl.pallas_call(gram_own_kernel, grid_spec=pltpu.PrefetchScalarGridSpec(nu...  9.13 us
    pallas_call x1, Pallas kernels, gram_other(): pl.pallas_call(gram_other_kernel, grid_spec=pltpu.PrefetchScalarGridSpec(...  8.77 us
    pallas_call x1, Pallas kernels, attend_partner_a(): pl.pallas_call(partner_a_kernel, grid_spec=pltpu.PrefetchScalarGridSpec(n...  5.64 us
    pallas_call x1, Pallas kernels, attend_partner_b(): pl.pallas_call(partner_b_kernel, grid_spec=pltpu.PrefetchScalarGridSpec(n...  5.02 us
  transfers between devices with their start and end apart: 36, of which 13 were waited for; matrix products, arithmetic and copies ran while one was open for 4% of the time, Pallas kernels for 19%

profile of v1, /device:TPU:0, one launch (start us, length us, event | category | flops | bytes accessed | tf_op | source)
XLA Modules:
  0.0 137.7 jit_solution(10243379639601066994)
XLA Ops:
  0.7 1.0 constant_dynamic-slice_fusion.1
  1.7 3.0 %collective-permute-start.1 = (bf16[256,512]{1,0:T(8,128)(2,1)S(1)}, bf16[256,512]{1,0:T(8,128)(2,1)S(1)}, u32[]{:S(2)}, u32[]{:S(2)}) collective-permute-start(bf16[256,512]{1,0:T(8,128)(2,1)S(1)} %pad_maximum_fusion), channel_id=1, source_target_pairs={{0,1},{1,0},{2,3},{3,2},{4,5},{5,4},{6,7},{7,6},{8,9},{9,8},{10,11... | collective-permute-start | bytes 786440 | tf_op jit(solution)/shard_map/ppermute | solution.py:554
  4.7 1.3 constant_dynamic-slice_fusion
  6.0 0.1 collective-permute-start.18
  6.1 2.0 %collective-permute-start = (bf16[256,1024]{1,0:T(8,128)(2,1)S(1)}, bf16[256,1024]{1,0:T(8,128)(2,1)S(1)}, u32[]{:S(2)}, u32[]{:S(2)}) collective-permute-start(bf16[256,1024]{1,0:T(8,128)(2,1)S(1)} %get-tuple-element.27), channel_id=1, source_target_pairs={{0,1},{1,0},{2,3},{3,2},{4,5},{5,4},{6,7},{7,6},{8,9},{9,8},{10,11... | collective-permute-start | bytes 1572872 | tf_op jit(solution)/shard_map/ppermute | solution.py:554
  8.1 0.1 fusion.30
  8.2 0.7 gather_fusion
  8.9 0.1 copy.11
  9.0 0.6 gather_fusion.1
  9.5 0.1 iota_add_fusion
  9.6 0.8 add.78.key_ref
  10.4 0.9 copy.12.col_ref
  11.3 2.0 %class_picks.1.so_ref.sp_ref = bf16[384,512]{1,0:T(8,128)(2,1)} custom-call(s32[512,1]{1,0:T(8,128)} %copy.12.col_ref, s32[1,512]{1,0:T(1,128)} %bitcast.59, s32[384,1]{1,0:T(8,128)} %add.78.key_ref), custom_call_target="tpu_custom_call" | custom-call | flops 1048576 | bytes 1048576 | tf_op jit(solution)/shard_map/class_picks/pallas_call | solution.py:430
  13.3 0.7 copy-done.1
  14.0 4.5 %attend_own.1 = (f32[256,2048]{1,0:T(8,128)}, f32[2,256,128]{2,1,0:T(8,128)}) custom-call(s32[1]{0:T(128)} %bitcast.place, bf16[256,4096]{1,0:T(8,128)(2,1)} %q_ref.1, bf16[256,512]{1,0:T(8,128)(2,1)} %ko.3, bf16[256,512]{1,0:T(8,128)(2,1)} %vo.3, bf16[256,512]{1,0:T(8,128)(2,1)} %copy-done.1, bf16[256,512]{1,0:T(8,128)(2,1)} %copy-done.1), custom_call_target="tpu_custom_call" | custom-call | flops 1073741824 | bytes 4194304 | tf_op jit(solution)/shard_map/attend_own/pallas_call | solution.py:206
  18.5 15.0 %collective-permute-done.q_ref = bf16[256,1024]{1,0:T(8,128)(2,1)S(1)} collective-permute-done((bf16[256,1024]{1,0:T(8,128)(2,1)S(1)}, bf16[256,1024]{1,0:T(8,128)(2,1)S(1)}, u32[]{:S(2)}, u32[]{:S(2)}) %collective-permute-start) | collective-permute-done | bytes 524320 | tf_op jit(solution)/shard_map/ppermute | solution.py:554
  33.5 0.8 copy-done.3
  34.3 5.6 %attend_partner_a.1 = (f32[256,1024]{1,0:T(8,128)}, f32[256,128]{1,0:T(8,128)}, bf16[384,1024]{1,0:T(8,128)(2,1)}) custom-call(s32[1]{0:T(128)} %bitcast.place, bf16[256,1024]{1,0:T(8,128)(2,1)} %copy-done.3, bf16[256,512]{1,0:T(8,128)(2,1)} %copy-done.1, bf16[256,512]{1,0:T(8,128)(2,1)} %copy-done.1, bf16[256,512]{1,0:T(8,128)(2,1)} %ko.3, ...), custom_call_target="tpu_custom_call" | custom-call | flops 536870912 | bytes 3145728 | tf_op jit(solution)/shard_map/attend_partner_a/pallas_call | solution.py:259
  40.0 0.8 copy-done.32
  40.7 5.0 %attend_partner_b.1 = (f32[256,1024]{1,0:T(8,128)}, f32[16,256]{1,0:T(8,128)}) custom-call(s32[1]{0:T(128)} %bitcast.place, bf16[256,1024]{1,0:T(8,128)(2,1)} %copy-done.32, bf16[256,512]{1,0:T(8,128)(2,1)} %copy-done.1, bf16[256,512]{1,0:T(8,128)(2,1)} %copy-done.1, bf16[256,512]{1,0:T(8,128)(2,1)} %ko.3, bf16[256,512]{1,0:T(8,128)(2,1)} %vo.3, ...), custom_call_target="tpu_custom_call" | custom-call | flops 536870912 | bytes 2097152 | tf_op jit(solution)/shard_map/attend_partner_b/pallas_call | solution.py:311
  45.8 0.1 fusion.34
  45.8 0.1 collective-permute-start.2
  45.9 3.8 %collective-permute-done.19.theirs_ref = f32[16,256]{1,0:T(8,128)S(1)} collective-permute-done((f32[16,256]{1,0:T(8,128)}, f32[16,256]{1,0:T(8,128)S(1)}, u32[]{:S(2)}, u32[]{:S(2)}) %collective-permute-start.19) | collective-permute-done | bytes 16416 | tf_op jit(solution)/shard_map/ppermute | solution.py:554
  49.7 0.6 copy-done.29
  50.3 5.0 %normalize.1 = (bf16[512,2048]{1,0:T(8,128)(2,1)}, bf16[384,1152]{1,0:T(8,128)(2,1)}) custom-call(s32[1]{0:T(128)} %bitcast.place, f32[256,2048]{1,0:T(8,128)} %get-tuple-element.14.own_ref, f32[256,1024]{1,0:T(8,128)} %get-tuple-element.16.pa_ref, f32[256,1024]{1,0:T(8,128)} %get-tuple-element.19.pb_ref, f32[16,256]{1,0:T(8,128)} %get-tuple-element.20.mine_ref, ...), custom_call_target="tpu_custom_call" | custom-call | flops 402653184 | bytes 8388608 | tf_op jit(solution)/shard_map/normalize/pallas_call | solution.py:386
  55.3 1.2 fusion.33
  56.5 0.1 collective-permute-start.20
  56.6 0.1 fusion.22
  56.7 4.9 %collective-permute-start.16 = (bf16[48,1024]{1,0:T(8,128)(2,1)S(1)}, bf16[48,1024]{1,0:T(8,128)(2,1)S(1)}, u32[]{:S(2)}, u32[]{:S(2)}) collective-permute-start(bf16[48,1024]{1,0:T(8,128)(2,1)S(1)} %get-tuple-element.38), channel_id=1, source_target_pairs={{0,28},{2,30},{4,24},{6,26},{8,20},{10,22},{12,16},{14,18},{16,12}... | collective-permute-start | bytes 294920 | tf_op jit(solution)/shard_map/ppermute | solution.py:557
  61.5 0.5 collective-permute-start.4
  62.0 3.0 %collective-permute-start.8 = (bf16[48,1024]{1,0:T(8,128)(2,1)S(1)}, bf16[48,1024]{1,0:T(8,128)(2,1)S(1)}, u32[]{:S(2)}, u32[]{:S(2)}) collective-permute-start(bf16[48,1024]{1,0:T(8,128)(2,1)S(1)} %get-tuple-element.42), channel_id=1, source_target_pairs={{0,12},{2,14},{4,8},{6,10},{8,4},{10,6},{12,0},{14,2},{16,28},{18,... | collective-permute-start | bytes 294920 | tf_op jit(solution)/shard_map/ppermute | solution.py:557
  65.0 0.2 collective-permute-done.16.refs_7_
  65.2 3.5 %collective-permute-start.12 = (bf16[48,1024]{1,0:T(8,128)(2,1)S(1)}, bf16[48,1024]{1,0:T(8,128)(2,1)S(1)}, u32[]{:S(2)}, u32[]{:S(2)}) collective-permute-start(bf16[48,1024]{1,0:T(8,128)(2,1)S(1)} %get-tuple-element.44), channel_id=1, source_target_pairs={{0,20},{2,22},{4,16},{6,18},{8,28},{10,30},{12,24},{14,26},{16,4},... | collective-permute-start | bytes 294920 | tf_op jit(solution)/shard_map/ppermute | solution.py:557
  68.8 0.1 fusion.7
  68.9 1.4 %collective-permute-start.34 = (bf16[48,1152]{1,0:T(8,128)(2,1)S(1)}, bf16[48,1152]{1,0:T(8,128)(2,1)S(1)}, u32[]{:S(2)}, u32[]{:S(2)}) collective-permute-start(bf16[48,1152]{1,0:T(8,128)(2,1)S(1)} %get-tuple-element.28), channel_id=1, source_target_pairs={{0,28},{2,30},{4,24},{6,26},{8,20},{10,22},{12,16},{14,18},{16,12}... | collective-permute-start | bytes 331784 | tf_op jit(solution)/shard_map/ppermute | solution.py:557
  70.3 2.6 %collective-permute-start.14 = (bf16[48,1024]{1,0:T(8,128)(2,1)S(1)}, bf16[48,1024]{1,0:T(8,128)(2,1)S(1)}, u32[]{:S(2)}, u32[]{:S(2)}) collective-permute-start(bf16[48,1024]{1,0:T(8,128)(2,1)S(1)} %get-tuple-element.45), channel_id=1, source_target_pairs={{0,24},{2,26},{4,28},{6,30},{8,16},{10,18},{12,20},{14,22},{16,8},... | collective-permute-start | bytes 294920 | tf_op jit(solution)/shard_map/ppermute | solution.py:557
  72.9 7.0 %collective-permute-done.10.refs_4_ = bf16[48,1024]{1,0:T(8,128)(2,1)S(1)} collective-permute-done((bf16[48,1024]{1,0:T(8,128)(2,1)S(1)}, bf16[48,1024]{1,0:T(8,128)(2,1)S(1)}, u32[]{:S(2)}, u32[]{:S(2)}) %collective-permute-start.10) | collective-permute-done | bytes 98336 | tf_op jit(solution)/shard_map/ppermute | solution.py:557
  79.9 2.1 %collective-permute-done.12.refs_5_ = bf16[48,1024]{1,0:T(8,128)(2,1)S(1)} collective-permute-done((bf16[48,1024]{1,0:T(8,128)(2,1)S(1)}, bf16[48,1024]{1,0:T(8,128)(2,1)S(1)}, u32[]{:S(2)}, u32[]{:S(2)}) %collective-permute-start.12) | collective-permute-done | bytes 98336 | tf_op jit(solution)/shard_map/ppermute | solution.py:557
  82.0 1.4 %collective-permute-start.22 = (bf16[48,1152]{1,0:T(8,128)(2,1)S(1)}, bf16[48,1152]{1,0:T(8,128)(2,1)S(1)}, u32[]{:S(2)}, u32[]{:S(2)}) collective-permute-start(bf16[48,1152]{1,0:T(8,128)(2,1)S(1)} %get-tuple-element.30), channel_id=1, source_target_pairs={{0,4},{2,6},{4,0},{6,2},{8,12},{10,14},{12,8},{14,10},{16,20},{18,... | collective-permute-start | bytes 331784 | tf_op jit(solution)/shard_map/ppermute | solution.py:557
  83.5 2.4 %collective-permute-start.24 = (bf16[48,1152]{1,0:T(8,128)(2,1)S(1)}, bf16[48,1152]{1,0:T(8,128)(2,1)S(1)}, u32[]{:S(2)}, u32[]{:S(2)}) collective-permute-start(bf16[48,1152]{1,0:T(8,128)(2,1)S(1)} %get-tuple-element.31), channel_id=1, source_target_pairs={{0,8},{2,10},{4,12},{6,14},{8,0},{10,2},{12,4},{14,6},{16,24},{18,... | collective-permute-start | bytes 331784 | tf_op jit(solution)/shard_map/ppermute | solution.py:557
  85.8 0.2 collective-permute-start.26
  86.1 2.8 %collective-permute-start.28 = (bf16[48,1152]{1,0:T(8,128)(2,1)S(1)}, bf16[48,1152]{1,0:T(8,128)(2,1)S(1)}, u32[]{:S(2)}, u32[]{:S(2)}) collective-permute-start(bf16[48,1152]{1,0:T(8,128)(2,1)S(1)} %get-tuple-element.33), channel_id=1, source_target_pairs={{0,16},{2,18},{4,20},{6,22},{8,24},{10,26},{12,28},{14,30},{16,0},... | collective-permute-start | bytes 331784 | tf_op jit(solution)/shard_map/ppermute | solution.py:557
  88.8 1.0 collective-permute-start.30
  89.8 2.4 %collective-permute-start.32 = (bf16[48,1152]{1,0:T(8,128)(2,1)S(1)}, bf16[48,1152]{1,0:T(8,128)(2,1)S(1)}, u32[]{:S(2)}, u32[]{:S(2)}) collective-permute-start(bf16[48,1152]{1,0:T(8,128)(2,1)S(1)} %get-tuple-element.35), channel_id=1, source_target_pairs={{0,24},{2,26},{4,28},{6,30},{8,16},{10,18},{12,20},{14,22},{16,8},... | collective-permute-start | bytes 331784 | tf_op jit(solution)/shard_map/ppermute | solution.py:557
  92.2 1.7 %collective-permute-done.26.refs_11_ = bf16[48,1152]{1,0:T(8,128)(2,1)S(1)} collective-permute-done((bf16[48,1152]{1,0:T(8,128)(2,1)S(1)}, bf16[48,1152]{1,0:T(8,128)(2,1)S(1)}, u32[]{:S(2)}, u32[]{:S(2)}) %collective-permute-start.26) | collective-permute-done | bytes 110624 | tf_op jit(solution)/shard_map/ppermute | solution.py:557
  93.9 0.4 collective-permute-start.5
  94.2 1.7 %collective-permute-start.7 = (bf16[48,1024]{1,0:T(8,128)(2,1)S(1)}, bf16[48,1024]{1,0:T(8,128)(2,1)S(1)}, u32[]{:S(2)}, u32[]{:S(2)}) collective-permute-start(bf16[48,1024]{1,0:T(8,128)(2,1)S(1)} %collective-permute-done.6.refs_2_), channel_id=1, source_target_pairs={{0,1},{1,0},{2,3},{3,2},{4,5},{5,4},{6,7},{7,6},{8,9},{9,8},{10,11... | collective-permute-start | bytes 294920 | tf_op jit(solution)/shard_map/ppermute | solution.py:554
  95.9 6.6 %collective-permute-done.30.refs_13_ = bf16[48,1152]{1,0:T(8,128)(2,1)S(1)} collective-permute-done((bf16[48,1152]{1,0:T(8,128)(2,1)S(1)}, bf16[48,1152]{1,0:T(8,128)(2,1)S(1)}, u32[]{:S(2)}, u32[]{:S(2)}) %collective-permute-start.30) | collective-permute-done | bytes 110624 | tf_op jit(solution)/shard_map/ppermute | solution.py:557
  102.6 2.1 %collective-permute-start.11 = (bf16[48,1024]{1,0:T(8,128)(2,1)S(1)}, bf16[48,1024]{1,0:T(8,128)(2,1)S(1)}, u32[]{:S(2)}, u32[]{:S(2)}) collective-permute-start(bf16[48,1024]{1,0:T(8,128)(2,1)S(1)} %collective-permute-done.10.refs_4_), channel_id=1, source_target_pairs={{0,1},{1,0},{2,3},{3,2},{4,5},{5,4},{6,7},{7,6},{8,9},{9,8},{10,11... | collective-permute-start | bytes 294920 | tf_op jit(solution)/shard_map/ppermute | solution.py:554
  104.7 0.1 collective-permute-start.13
  104.8 1.9 %collective-permute-start.15 = (bf16[48,1024]{1,0:T(8,128)(2,1)S(1)}, bf16[48,1024]{1,0:T(8,128)(2,1)S(1)}, u32[]{:S(2)}, u32[]{:S(2)}) collective-permute-start(bf16[48,1024]{1,0:T(8,128)(2,1)S(1)} %collective-permute-done.14.refs_6_), channel_id=1, source_target_pairs={{0,1},{1,0},{2,3},{3,2},{4,5},{5,4},{6,7},{7,6},{8,9},{9,8},{10,11... | collective-permute-start | bytes 294920 | tf_op jit(solution)/shard_map/ppermute | solution.py:554
  106.7 0.1 collective-permute-start.35
  106.8 1.4 %collective-permute-done.9.refs_3_ = bf16[48,1024]{1,0:T(8,128)(2,1)S(1)} collective-permute-done((bf16[48,1024]{1,0:T(8,128)(2,1)S(1)}, bf16[48,1024]{1,0:T(8,128)(2,1)S(1)}, u32[]{:S(2)}, u32[]{:S(2)}) %collective-permute-start.9) | collective-permute-done | bytes 98336 | tf_op jit(solution)/shard_map/ppermute | solution.py:554
  108.2 0.5 collective-permute-start.23
  108.8 1.5 %collective-permute-done.11.refs_4_ = bf16[48,1024]{1,0:T(8,128)(2,1)S(1)} collective-permute-done((bf16[48,1024]{1,0:T(8,128)(2,1)S(1)}, bf16[48,1024]{1,0:T(8,128)(2,1)S(1)}, u32[]{:S(2)}, u32[]{:S(2)}) %collective-permute-start.11) | collective-permute-done | bytes 98336 | tf_op jit(solution)/shard_map/ppermute | solution.py:554
  110.3 0.1 collective-permute-start.25
  110.4 2.0 %collective-permute-done.13.refs_5_ = bf16[48,1024]{1,0:T(8,128)(2,1)S(1)} collective-permute-done((bf16[48,1024]{1,0:T(8,128)(2,1)S(1)}, bf16[48,1024]{1,0:T(8,128)(2,1)S(1)}, u32[]{:S(2)}, u32[]{:S(2)}) %collective-permute-start.13) | collective-permute-done | bytes 98336 | tf_op jit(solution)/shard_map/ppermute | solution.py:554
  112.5 2.1 %collective-permute-done.15.refs_6_ = bf16[48,1024]{1,0:T(8,128)(2,1)S(1)} collective-permute-done((bf16[48,1024]{1,0:T(8,128)(2,1)S(1)}, bf16[48,1024]{1,0:T(8,128)(2,1)S(1)}, u32[]{:S(2)}, u32[]{:S(2)}) %collective-permute-start.15) | collective-permute-done | bytes 98336 | tf_op jit(solution)/shard_map/ppermute | solution.py:554
  114.6 2.1 %collective-permute-done.35.refs_15_ = bf16[48,1024]{1,0:T(8,128)(2,1)S(1)} collective-permute-done((bf16[48,1024]{1,0:T(8,128)(2,1)S(1)}, bf16[48,1024]{1,0:T(8,128)(2,1)S(1)}, u32[]{:S(2)}, u32[]{:S(2)}) %collective-permute-start.35) | collective-permute-done | bytes 98336 | tf_op jit(solution)/shard_map/ppermute | solution.py:554
  116.7 2.1 %collective-permute-done.23.refs_9_ = bf16[48,1024]{1,0:T(8,128)(2,1)S(1)} collective-permute-done((bf16[48,1024]{1,0:T(8,128)(2,1)S(1)}, bf16[48,1024]{1,0:T(8,128)(2,1)S(1)}, u32[]{:S(2)}, u32[]{:S(2)}) %collective-permute-start.23) | collective-permute-done | bytes 98336 | tf_op jit(solution)/shard_map/ppermute | solution.py:554
  118.9 9.1 %gram_own.1 = (bf16[2048,4096]{1,0:T(8,128)(2,1)}, bf16[2048,384]{1,0:T(8,128)(2,1)}, f32[384,128]{1,0:T(8,128)}) custom-call(s32[1]{0:T(128)} %bitcast.place, bf16[48,1024]{1,0:T(8,128)(2,1)} %copy-done.21, bf16[48,1024]{1,0:T(8,128)(2,1)} %copy-done.34, bf16[48,1024]{1,0:T(8,128)(2,1)} %copy-done.35, bf16[48,1024]{1,0:T(8,128)(2,1)} %copy-done.36, ...), custom_call_target="tpu_custom_call" | custom-call | flops 3221225472 | bytes 14680064 | tf_op jit(solution)/shard_map/gram_own/pallas_call | solution.py:471
  128.2 0.5 copy-done.16
  128.8 0.0 copy-done.17
  128.9 8.8 %gram_other.1 = bf16[2048,4096]{1,0:T(8,128)(2,1)} custom-call(s32[1]{0:T(128)} %bitcast.place, bf16[48,1024]{1,0:T(8,128)(2,1)} %copy-done.5, bf16[48,1024]{1,0:T(8,128)(2,1)} %copy-done.8, bf16[48,1024]{1,0:T(8,128)(2,1)} %copy-done.9, bf16[48,1024]{1,0:T(8,128)(2,1)} %copy-done.10, bf16[48,1024]{1,0:T(8,128)(2,1)} %copy-done.11, ...), custom_call_target="tpu_custom_call", output_to_operand_aliasing={{}: (20, {})} | custom-call | flops 3221225472 | bytes 14680064 | tf_op jit(solution)/shard_map/gram_other/pallas_call | solution.py:523
  (122 shorter events, 0.5 us)
Async XLA Ops:
  0.7 9.8 %copy-start.30 = (s32[512]{0:T(512)S(1)}, s32[512]{0:T(512)}, u32[]{:S(2)}) copy-start(s32[512]{0:T(512)} %param.11) | copy-start | bytes 6148
  1.7 11.6 %collective-permute-start.1 = (bf16[256,512]{1,0:T(8,128)(2,1)S(1)}, bf16[256,512]{1,0:T(8,128)(2,1)S(1)}, u32[]{:S(2)}, u32[]{:S(2)}) collective-permute-start(bf16[256,512]{1,0:T(8,128)(2,1)S(1)} %pad_maximum_fusion), channel_id=1, source_target_pairs={{0,1},{1,0},{2,3},{3,2},{4,5},{5,4},{6,7},{7,6},{8,9},{9,8},{10,11... | collective-permute-start | bytes 786440 | tf_op jit(solution)/shard_map/ppermute | solution.py:554
  6.0 33.9 %collective-permute-start.18 = (bf16[256,1024]{1,0:T(8,128)(2,1)S(1)}, bf16[256,1024]{1,0:T(8,128)(2,1)S(1)}, u32[]{:S(2)}, u32[]{:S(2)}) collective-permute-start(bf16[256,1024]{1,0:T(8,128)(2,1)S(1)} %get-tuple-element.26), channel_id=1, source_target_pairs={{0,1},{1,0},{2,3},{3,2},{4,5},{5,4},{6,7},{7,6},{8,9},{9,8},{10,11... | collective-permute-start | bytes 1572872 | tf_op jit(solution)/shard_map/ppermute | solution.py:554
  6.1 27.4 %collective-permute-start = (bf16[256,1024]{1,0:T(8,128)(2,1)S(1)}, bf16[256,1024]{1,0:T(8,128)(2,1)S(1)}, u32[]{:S(2)}, u32[]{:S(2)}) collective-permute-start(bf16[256,1024]{1,0:T(8,128)(2,1)S(1)} %get-tuple-element.27), channel_id=1, source_target_pairs={{0,1},{1,0},{2,3},{3,2},{4,5},{5,4},{6,7},{7,6},{8,9},{9,8},{10,11... | collective-permute-start | bytes 1572872 | tf_op jit(solution)/shard_map/ppermute | solution.py:554
  45.7 3.9 %collective-permute-start.19 = (f32[16,256]{1,0:T(8,128)}, f32[16,256]{1,0:T(8,128)S(1)}, u32[]{:S(2)}, u32[]{:S(2)}) collective-permute-start(f32[16,256]{1,0:T(8,128)} %get-tuple-element.20.mine_ref), channel_id=1, source_target_pairs={{0,1},{1,0},{2,3},{3,2},{4,5},{5,4},{6,7},{7,6},{8,9},{9,8},{10,11... | collective-permute-start | bytes 49160 | tf_op jit(solution)/shard_map/ppermute | solution.py:554
  45.8 10.8 %collective-permute-start.2 = (bf16[192,1024]{1,0:T(8,128)(2,1)S(1)}, bf16[192,1024]{1,0:T(8,128)(2,1)S(1)}, u32[]{:S(2)}, u32[]{:S(2)}) collective-permute-start(bf16[192,1024]{1,0:T(8,128)(2,1)S(1)} %get-tuple-element.47), channel_id=1, source_target_pairs={{0,2},{2,0},{4,6},{6,4},{8,10},{10,8},{12,14},{14,12},{16,18},{18,... | collective-permute-start | bytes 1179656 | tf_op jit(solution)/shard_map/ppermute | solution.py:557
  56.5 8.5 %collective-permute-start.20 = (bf16[192,1152]{1,0:T(8,128)(2,1)S(1)}, bf16[192,1152]{1,0:T(8,128)(2,1)S(1)}, u32[]{:S(2)}, u32[]{:S(2)}) collective-permute-start(bf16[192,1152]{1,0:T(8,128)(2,1)S(1)} %get-tuple-element.37), channel_id=1, source_target_pairs={{0,2},{2,0},{4,6},{6,4},{8,10},{10,8},{12,14},{14,12},{16,18},{18,... | collective-permute-start | bytes 1327112 | tf_op jit(solution)/shard_map/ppermute | solution.py:557
  56.7 62.1 %copy-start.21 = (bf16[48,1024]{1,0:T(8,128)(2,1)}, bf16[48,1024]{1,0:T(8,128)(2,1)S(1)}, u32[]{:S(2)}) copy-start(bf16[48,1024]{1,0:T(8,128)(2,1)S(1)} %get-tuple-element.39.refs_0_) | copy-start | bytes 294916
  56.7 8.6 %collective-permute-start.16 = (bf16[48,1024]{1,0:T(8,128)(2,1)S(1)}, bf16[48,1024]{1,0:T(8,128)(2,1)S(1)}, u32[]{:S(2)}, u32[]{:S(2)}) collective-permute-start(bf16[48,1024]{1,0:T(8,128)(2,1)S(1)} %get-tuple-element.38), channel_id=1, source_target_pairs={{0,28},{2,30},{4,24},{6,26},{8,20},{10,22},{12,16},{14,18},{16,12}... | collective-permute-start | bytes 294920 | tf_op jit(solution)/shard_map/ppermute | solution.py:557
  61.5 7.3 %collective-permute-start.4 = (bf16[48,1024]{1,0:T(8,128)(2,1)S(1)}, bf16[48,1024]{1,0:T(8,128)(2,1)S(1)}, u32[]{:S(2)}, u32[]{:S(2)}) collective-permute-start(bf16[48,1024]{1,0:T(8,128)(2,1)S(1)} %get-tuple-element.40), channel_id=1, source_target_pairs={{0,4},{2,6},{4,0},{6,2},{8,12},{10,14},{12,8},{14,10},{16,20},{18,... | collective-permute-start | bytes 294920 | tf_op jit(solution)/shard_map/ppermute | solution.py:557
  62.0 8.2 %collective-permute-start.6 = (bf16[48,1024]{1,0:T(8,128)(2,1)S(1)}, bf16[48,1024]{1,0:T(8,128)(2,1)S(1)}, u32[]{:S(2)}, u32[]{:S(2)}) collective-permute-start(bf16[48,1024]{1,0:T(8,128)(2,1)S(1)} %get-tuple-element.41), channel_id=1, source_target_pairs={{0,8},{2,10},{4,12},{6,14},{8,0},{10,2},{12,4},{14,6},{16,24},{18,... | collective-permute-start | bytes 294920 | tf_op jit(solution)/shard_map/ppermute | solution.py:557
  62.0 10.8 %collective-permute-start.8 = (bf16[48,1024]{1,0:T(8,128)(2,1)S(1)}, bf16[48,1024]{1,0:T(8,128)(2,1)S(1)}, u32[]{:S(2)}, u32[]{:S(2)}) collective-permute-start(bf16[48,1024]{1,0:T(8,128)(2,1)S(1)} %get-tuple-element.42), channel_id=1, source_target_pairs={{0,12},{2,14},{4,8},{6,10},{8,4},{10,6},{12,0},{14,2},{16,28},{18,... | collective-permute-start | bytes 294920 | tf_op jit(solution)/shard_map/ppermute | solution.py:557
  65.0 14.9 %collective-permute-start.10 = (bf16[48,1024]{1,0:T(8,128)(2,1)S(1)}, bf16[48,1024]{1,0:T(8,128)(2,1)S(1)}, u32[]{:S(2)}, u32[]{:S(2)}) collective-permute-start(bf16[48,1024]{1,0:T(8,128)(2,1)S(1)} %get-tuple-element.43), channel_id=1, source_target_pairs={{0,16},{2,18},{4,20},{6,22},{8,24},{10,26},{12,28},{14,30},{16,0},... | collective-permute-start | bytes 294920 | tf_op jit(solution)/shard_map/ppermute | solution.py:557
  65.2 53.6 %copy-start.33 = (bf16[48,1024]{1,0:T(8,128)(2,1)}, bf16[48,1024]{1,0:T(8,128)(2,1)S(1)}, u32[]{:S(2)}) copy-start(bf16[48,1024]{1,0:T(8,128)(2,1)S(1)} %collective-permute-done.16.refs_7_) | copy-start | bytes 294916
  65.2 16.8 %collective-permute-start.12 = (bf16[48,1024]{1,0:T(8,128)(2,1)S(1)}, bf16[48,1024]{1,0:T(8,128)(2,1)S(1)}, u32[]{:S(2)}, u32[]{:S(2)}) collective-permute-start(bf16[48,1024]{1,0:T(8,128)(2,1)S(1)} %get-tuple-element.44), channel_id=1, source_target_pairs={{0,20},{2,22},{4,16},{6,18},{8,28},{10,30},{12,24},{14,26},{16,4},... | collective-permute-start | bytes 294920 | tf_op jit(solution)/shard_map/ppermute | solution.py:557
  68.8 50.0 %copy-start.4 = (bf16[48,1152]{1,0:T(8,128)(2,1)}, bf16[48,1152]{1,0:T(8,128)(2,1)S(1)}, u32[]{:S(2)}) copy-start(bf16[48,1152]{1,0:T(8,128)(2,1)S(1)} %get-tuple-element.29.refs_8_) | copy-start | bytes 331780
  68.8 50.0 %copy-start.34 = (bf16[48,1024]{1,0:T(8,128)(2,1)}, bf16[48,1024]{1,0:T(8,128)(2,1)S(1)}, u32[]{:S(2)}) copy-start(bf16[48,1024]{1,0:T(8,128)(2,1)S(1)} %collective-permute-done.4.refs_1_) | copy-start | bytes 294916
  68.9 20.0 %collective-permute-start.34 = (bf16[48,1152]{1,0:T(8,128)(2,1)S(1)}, bf16[48,1152]{1,0:T(8,128)(2,1)S(1)}, u32[]{:S(2)}, u32[]{:S(2)}) collective-permute-start(bf16[48,1152]{1,0:T(8,128)(2,1)S(1)} %get-tuple-element.28), channel_id=1, source_target_pairs={{0,28},{2,30},{4,24},{6,26},{8,20},{10,22},{12,16},{14,18},{16,12}... | collective-permute-start | bytes 331784 | tf_op jit(solution)/shard_map/ppermute | solution.py:557
  70.3 48.5 %copy-start.35 = (bf16[48,1024]{1,0:T(8,128)(2,1)}, bf16[48,1024]{1,0:T(8,128)(2,1)S(1)}, u32[]{:S(2)}) copy-start(bf16[48,1024]{1,0:T(8,128)(2,1)S(1)} %collective-permute-done.6.refs_2_) | copy-start | bytes 294916
  70.3 13.2 %collective-permute-start.14 = (bf16[48,1024]{1,0:T(8,128)(2,1)S(1)}, bf16[48,1024]{1,0:T(8,128)(2,1)S(1)}, u32[]{:S(2)}, u32[]{:S(2)}) collective-permute-start(bf16[48,1024]{1,0:T(8,128)(2,1)S(1)} %get-tuple-element.45), channel_id=1, source_target_pairs={{0,24},{2,26},{4,28},{6,30},{8,16},{10,18},{12,20},{14,22},{16,8},... | collective-permute-start | bytes 294920 | tf_op jit(solution)/shard_map/ppermute | solution.py:557
  72.9 46.0 %copy-start.36 = (bf16[48,1024]{1,0:T(8,128)(2,1)}, bf16[48,1024]{1,0:T(8,128)(2,1)S(1)}, u32[]{:S(2)}) copy-start(bf16[48,1024]{1,0:T(8,128)(2,1)S(1)} %collective-permute-done.8.refs_3_) | copy-start | bytes 294916
  72.9 13.0 %collective-permute-start.3 = (bf16[48,1024]{1,0:T(8,128)(2,1)S(1)}, bf16[48,1024]{1,0:T(8,128)(2,1)S(1)}, u32[]{:S(2)}, u32[]{:S(2)}) collective-permute-start(bf16[48,1024]{1,0:T(8,128)(2,1)S(1)} %get-tuple-element.39.refs_0_), channel_id=1, source_target_pairs={{0,1},{1,0},{2,3},{3,2},{4,5},{5,4},{6,7},{7,6},{8,9},{9,8},{10,11... | collective-permute-start | bytes 294920 | tf_op jit(solution)/shard_map/ppermute | solution.py:554
  79.9 38.9 %copy-start.37 = (bf16[48,1024]{1,0:T(8,128)(2,1)}, bf16[48,1024]{1,0:T(8,128)(2,1)S(1)}, u32[]{:S(2)}) copy-start(bf16[48,1024]{1,0:T(8,128)(2,1)S(1)} %collective-permute-done.10.refs_4_) | copy-start | bytes 294916
  79.9 6.2 %collective-permute-start.21 = (bf16[48,1024]{1,0:T(8,128)(2,1)S(1)}, bf16[48,1024]{1,0:T(8,128)(2,1)S(1)}, u32[]{:S(2)}, u32[]{:S(2)}) collective-permute-start(bf16[48,1024]{1,0:T(8,128)(2,1)S(1)} %slice.132), channel_id=1, source_target_pairs={{0,1},{1,0},{2,3},{3,2},{4,5},{5,4},{6,7},{7,6},{8,9},{9,8},{10,11... | collective-permute-start | bytes 294920 | tf_op jit(solution)/shard_map/ppermute | solution.py:554
  82.0 28.4 %copy-start.38 = (bf16[48,1024]{1,0:T(8,128)(2,1)}, bf16[48,1024]{1,0:T(8,128)(2,1)S(1)}, u32[]{:S(2)}) copy-start(bf16[48,1024]{1,0:T(8,128)(2,1)S(1)} %collective-permute-done.12.refs_5_) | copy-start | bytes 294916
  82.0 7.8 %collective-permute-start.22 = (bf16[48,1152]{1,0:T(8,128)(2,1)S(1)}, bf16[48,1152]{1,0:T(8,128)(2,1)S(1)}, u32[]{:S(2)}, u32[]{:S(2)}) collective-permute-start(bf16[48,1152]{1,0:T(8,128)(2,1)S(1)} %get-tuple-element.30), channel_id=1, source_target_pairs={{0,4},{2,6},{4,0},{6,2},{8,12},{10,14},{12,8},{14,10},{16,20},{18,... | collective-permute-start | bytes 331784 | tf_op jit(solution)/shard_map/ppermute | solution.py:557
  83.5 35.3 %copy-start.39 = (bf16[48,1024]{1,0:T(8,128)(2,1)}, bf16[48,1024]{1,0:T(8,128)(2,1)S(1)}, u32[]{:S(2)}) copy-start(bf16[48,1024]{1,0:T(8,128)(2,1)S(1)} %collective-permute-done.14.refs_6_) | copy-start | bytes 294916
  83.5 8.7 %collective-permute-start.24 = (bf16[48,1152]{1,0:T(8,128)(2,1)S(1)}, bf16[48,1152]{1,0:T(8,128)(2,1)S(1)}, u32[]{:S(2)}, u32[]{:S(2)}) collective-permute-start(bf16[48,1152]{1,0:T(8,128)(2,1)S(1)} %get-tuple-element.31), channel_id=1, source_target_pairs={{0,8},{2,10},{4,12},{6,14},{8,0},{10,2},{12,4},{14,6},{16,24},{18,... | collective-permute-start | bytes 331784 | tf_op jit(solution)/shard_map/ppermute | solution.py:557
  85.8 42.2 %copy-start.5 = (bf16[48,1024]{1,0:T(8,128)(2,1)}, bf16[48,1024]{1,0:T(8,128)(2,1)S(1)}, u32[]{:S(2)}) copy-start(bf16[48,1024]{1,0:T(8,128)(2,1)S(1)} %collective-permute-done.3.refs_0_) | copy-start | bytes 294916
  85.8 8.0 %collective-permute-start.26 = (bf16[48,1152]{1,0:T(8,128)(2,1)S(1)}, bf16[48,1152]{1,0:T(8,128)(2,1)S(1)}, u32[]{:S(2)}, u32[]{:S(2)}) collective-permute-start(bf16[48,1152]{1,0:T(8,128)(2,1)S(1)} %get-tuple-element.32), channel_id=1, source_target_pairs={{0,12},{2,14},{4,8},{6,10},{8,4},{10,6},{12,0},{14,2},{16,28},{18,... | collective-permute-start | bytes 331784 | tf_op jit(solution)/shard_map/ppermute | solution.py:557
  86.1 42.0 %copy-start.6 = (bf16[48,1024]{1,0:T(8,128)(2,1)}, bf16[48,1024]{1,0:T(8,128)(2,1)S(1)}, u32[]{:S(2)}) copy-start(bf16[48,1024]{1,0:T(8,128)(2,1)S(1)} %collective-permute-done.21.refs_8_) | copy-start | bytes 294916
  86.1 8.2 %collective-permute-start.28 = (bf16[48,1152]{1,0:T(8,128)(2,1)S(1)}, bf16[48,1152]{1,0:T(8,128)(2,1)S(1)}, u32[]{:S(2)}, u32[]{:S(2)}) collective-permute-start(bf16[48,1152]{1,0:T(8,128)(2,1)S(1)} %get-tuple-element.33), channel_id=1, source_target_pairs={{0,16},{2,18},{4,20},{6,22},{8,24},{10,26},{12,28},{14,30},{16,0},... | collective-permute-start | bytes 331784 | tf_op jit(solution)/shard_map/ppermute | solution.py:557
  88.8 30.0 %copy-start.22 = (bf16[48,1152]{1,0:T(8,128)(2,1)}, bf16[48,1152]{1,0:T(8,128)(2,1)S(1)}, u32[]{:S(2)}) copy-start(bf16[48,1152]{1,0:T(8,128)(2,1)S(1)} %collective-permute-done.34.refs_15_) | copy-start | bytes 331780
  88.8 13.7 %collective-permute-start.30 = (bf16[48,1152]{1,0:T(8,128)(2,1)S(1)}, bf16[48,1152]{1,0:T(8,128)(2,1)S(1)}, u32[]{:S(2)}, u32[]{:S(2)}) collective-permute-start(bf16[48,1152]{1,0:T(8,128)(2,1)S(1)} %get-tuple-element.34), channel_id=1, source_target_pairs={{0,20},{2,22},{4,16},{6,18},{8,28},{10,30},{12,24},{14,26},{16,4},... | collective-permute-start | bytes 331784 | tf_op jit(solution)/shard_map/ppermute | solution.py:557
  89.8 29.0 %copy-start.23 = (bf16[48,1152]{1,0:T(8,128)(2,1)}, bf16[48,1152]{1,0:T(8,128)(2,1)S(1)}, u32[]{:S(2)}) copy-start(bf16[48,1152]{1,0:T(8,128)(2,1)S(1)} %collective-permute-done.22.refs_9_) | copy-start | bytes 331780
  89.8 12.7 %collective-permute-start.32 = (bf16[48,1152]{1,0:T(8,128)(2,1)S(1)}, bf16[48,1152]{1,0:T(8,128)(2,1)S(1)}, u32[]{:S(2)}, u32[]{:S(2)}) collective-permute-start(bf16[48,1152]{1,0:T(8,128)(2,1)S(1)} %get-tuple-element.35), channel_id=1, source_target_pairs={{0,24},{2,26},{4,28},{6,30},{8,16},{10,18},{12,20},{14,22},{16,8},... | collective-permute-start | bytes 331784 | tf_op jit(solution)/shard_map/ppermute | solution.py:557
  92.2 26.7 %copy-start.24 = (bf16[48,1152]{1,0:T(8,128)(2,1)}, bf16[48,1152]{1,0:T(8,128)(2,1)S(1)}, u32[]{:S(2)}) copy-start(bf16[48,1152]{1,0:T(8,128)(2,1)S(1)} %collective-permute-done.24.refs_10_) | copy-start | bytes 331780
  92.2 12.5 %collective-permute-start.17 = (bf16[48,1024]{1,0:T(8,128)(2,1)S(1)}, bf16[48,1024]{1,0:T(8,128)(2,1)S(1)}, u32[]{:S(2)}, u32[]{:S(2)}) collective-permute-start(bf16[48,1024]{1,0:T(8,128)(2,1)S(1)} %collective-permute-done.16.refs_7_), channel_id=1, source_target_pairs={{0,1},{1,0},{2,3},{3,2},{4,5},{5,4},{6,7},{7,6},{8,9},{9,8},{10,11... | collective-permute-start | bytes 294920 | tf_op jit(solution)/shard_map/ppermute | solution.py:554
  93.9 25.0 %copy-start.25 = (bf16[48,1152]{1,0:T(8,128)(2,1)}, bf16[48,1152]{1,0:T(8,128)(2,1)S(1)}, u32[]{:S(2)}) copy-start(bf16[48,1152]{1,0:T(8,128)(2,1)S(1)} %collective-permute-done.26.refs_11_) | copy-start | bytes 331780
  93.9 10.9 %collective-permute-start.5 = (bf16[48,1024]{1,0:T(8,128)(2,1)S(1)}, bf16[48,1024]{1,0:T(8,128)(2,1)S(1)}, u32[]{:S(2)}, u32[]{:S(2)}) collective-permute-start(bf16[48,1024]{1,0:T(8,128)(2,1)S(1)} %collective-permute-done.4.refs_1_), channel_id=1, source_target_pairs={{0,1},{1,0},{2,3},{3,2},{4,5},{5,4},{6,7},{7,6},{8,9},{9,8},{10,11... | collective-permute-start | bytes 294920 | tf_op jit(solution)/shard_map/ppermute | solution.py:554
  94.2 24.6 %copy-start.26 = (bf16[48,1152]{1,0:T(8,128)(2,1)}, bf16[48,1152]{1,0:T(8,128)(2,1)S(1)}, u32[]{:S(2)}) copy-start(bf16[48,1152]{1,0:T(8,128)(2,1)S(1)} %collective-permute-done.28.refs_12_) | copy-start | bytes 331780
  94.2 12.5 %collective-permute-start.7 = (bf16[48,1024]{1,0:T(8,128)(2,1)S(1)}, bf16[48,1024]{1,0:T(8,128)(2,1)S(1)}, u32[]{:S(2)}, u32[]{:S(2)}) collective-permute-start(bf16[48,1024]{1,0:T(8,128)(2,1)S(1)} %collective-permute-done.6.refs_2_), channel_id=1, source_target_pairs={{0,1},{1,0},{2,3},{3,2},{4,5},{5,4},{6,7},{7,6},{8,9},{9,8},{10,11... | collective-permute-start | bytes 294920 | tf_op jit(solution)/shard_map/ppermute | solution.py:554
  102.6 16.3 %copy-start.27 = (bf16[48,1152]{1,0:T(8,128)(2,1)}, bf16[48,1152]{1,0:T(8,128)(2,1)S(1)}, u32[]{:S(2)}) copy-start(bf16[48,1152]{1,0:T(8,128)(2,1)S(1)} %collective-permute-done.30.refs_13_) | copy-start | bytes 331780
  102.6 5.7 %collective-permute-start.9 = (bf16[48,1024]{1,0:T(8,128)(2,1)S(1)}, bf16[48,1024]{1,0:T(8,128)(2,1)S(1)}, u32[]{:S(2)}, u32[]{:S(2)}) collective-permute-start(bf16[48,1024]{1,0:T(8,128)(2,1)S(1)} %collective-permute-done.8.refs_3_), channel_id=1, source_target_pairs={{0,1},{1,0},{2,3},{3,2},{4,5},{5,4},{6,7},{7,6},{8,9},{9,8},{10,11... | collective-permute-start | bytes 294920 | tf_op jit(solution)/shard_map/ppermute | solution.py:554
  102.6 16.3 %copy-start.28 = (bf16[48,1152]{1,0:T(8,128)(2,1)}, bf16[48,1152]{1,0:T(8,128)(2,1)S(1)}, u32[]{:S(2)}) copy-start(bf16[48,1152]{1,0:T(8,128)(2,1)S(1)} %collective-permute-done.32.refs_14_) | copy-start | bytes 331780
  102.6 7.7 %collective-permute-start.11 = (bf16[48,1024]{1,0:T(8,128)(2,1)S(1)}, bf16[48,1024]{1,0:T(8,128)(2,1)S(1)}, u32[]{:S(2)}, u32[]{:S(2)}) collective-permute-start(bf16[48,1024]{1,0:T(8,128)(2,1)S(1)} %collective-permute-done.10.refs_4_), channel_id=1, source_target_pairs={{0,1},{1,0},{2,3},{3,2},{4,5},{5,4},{6,7},{7,6},{8,9},{9,8},{10,11... | collective-permute-start | bytes 294920 | tf_op jit(solution)/shard_map/ppermute | solution.py:554
  104.7 23.4 %copy-start.7 = (bf16[48,1024]{1,0:T(8,128)(2,1)}, bf16[48,1024]{1,0:T(8,128)(2,1)S(1)}, u32[]{:S(2)}) copy-start(bf16[48,1024]{1,0:T(8,128)(2,1)S(1)} %collective-permute-done.17.refs_7_) | copy-start | bytes 294916
  104.7 7.7 %collective-permute-start.13 = (bf16[48,1024]{1,0:T(8,128)(2,1)S(1)}, bf16[48,1024]{1,0:T(8,128)(2,1)S(1)}, u32[]{:S(2)}, u32[]{:S(2)}) collective-permute-start(bf16[48,1024]{1,0:T(8,128)(2,1)S(1)} %collective-permute-done.12.refs_5_), channel_id=1, source_target_pairs={{0,1},{1,0},{2,3},{3,2},{4,5},{5,4},{6,7},{7,6},{8,9},{9,8},{10,11... | collective-permute-start | bytes 294920 | tf_op jit(solution)/shard_map/ppermute | solution.py:554
  104.8 23.3 %copy-start.8 = (bf16[48,1024]{1,0:T(8,128)(2,1)}, bf16[48,1024]{1,0:T(8,128)(2,1)S(1)}, u32[]{:S(2)}) copy-start(bf16[48,1024]{1,0:T(8,128)(2,1)S(1)} %collective-permute-done.5.refs_1_) | copy-start | bytes 294916
  104.8 9.7 %collective-permute-start.15 = (bf16[48,1024]{1,0:T(8,128)(2,1)S(1)}, bf16[48,1024]{1,0:T(8,128)(2,1)S(1)}, u32[]{:S(2)}, u32[]{:S(2)}) collective-permute-start(bf16[48,1024]{1,0:T(8,128)(2,1)S(1)} %collective-permute-done.14.refs_6_), channel_id=1, source_target_pairs={{0,1},{1,0},{2,3},{3,2},{4,5},{5,4},{6,7},{7,6},{8,9},{9,8},{10,11... | collective-permute-start | bytes 294920 | tf_op jit(solution)/shard_map/ppermute | solution.py:554
  106.7 21.3 %copy-start.9 = (bf16[48,1024]{1,0:T(8,128)(2,1)}, bf16[48,1024]{1,0:T(8,128)(2,1)S(1)}, u32[]{:S(2)}) copy-start(bf16[48,1024]{1,0:T(8,128)(2,1)S(1)} %collective-permute-done.7.refs_2_) | copy-start | bytes 294916
  106.7 9.9 %collective-permute-start.35 = (bf16[48,1024]{1,0:T(8,128)(2,1)S(1)}, bf16[48,1024]{1,0:T(8,128)(2,1)S(1)}, u32[]{:S(2)}, u32[]{:S(2)}) collective-permute-start(bf16[48,1024]{1,0:T(8,128)(2,1)S(1)} %slice.151), channel_id=1, source_target_pairs={{0,1},{1,0},{2,3},{3,2},{4,5},{5,4},{6,7},{7,6},{8,9},{9,8},{10,11... | collective-permute-start | bytes 294920 | tf_op jit(solution)/shard_map/ppermute | solution.py:554
  108.2 19.9 %copy-start.10 = (bf16[48,1024]{1,0:T(8,128)(2,1)}, bf16[48,1024]{1,0:T(8,128)(2,1)S(1)}, u32[]{:S(2)}) copy-start(bf16[48,1024]{1,0:T(8,128)(2,1)S(1)} %collective-permute-done.9.refs_3_) | copy-start | bytes 294916
  108.2 10.5 %collective-permute-start.23 = (bf16[48,1024]{1,0:T(8,128)(2,1)S(1)}, bf16[48,1024]{1,0:T(8,128)(2,1)S(1)}, u32[]{:S(2)}, u32[]{:S(2)}) collective-permute-start(bf16[48,1024]{1,0:T(8,128)(2,1)S(1)} %slice.135), channel_id=1, source_target_pairs={{0,1},{1,0},{2,3},{3,2},{4,5},{5,4},{6,7},{7,6},{8,9},{9,8},{10,11... | collective-permute-start | bytes 294920 | tf_op jit(solution)/shard_map/ppermute | solution.py:554
  110.3 17.8 %copy-start.11 = (bf16[48,1024]{1,0:T(8,128)(2,1)}, bf16[48,1024]{1,0:T(8,128)(2,1)S(1)}, u32[]{:S(2)}) copy-start(bf16[48,1024]{1,0:T(8,128)(2,1)S(1)} %collective-permute-done.11.refs_4_) | copy-start | bytes 294916
  110.3 17.8 %collective-permute-start.25 = (bf16[48,1024]{1,0:T(8,128)(2,1)S(1)}, bf16[48,1024]{1,0:T(8,128)(2,1)S(1)}, u32[]{:S(2)}, u32[]{:S(2)}) collective-permute-start(bf16[48,1024]{1,0:T(8,128)(2,1)S(1)} %slice.138), channel_id=1, source_target_pairs={{0,1},{1,0},{2,3},{3,2},{4,5},{5,4},{6,7},{7,6},{8,9},{9,8},{10,11... | collective-permute-start | bytes 294920 | tf_op jit(solution)/shard_map/ppermute | solution.py:554
  112.4 15.7 %copy-start.12 = (bf16[48,1024]{1,0:T(8,128)(2,1)}, bf16[48,1024]{1,0:T(8,128)(2,1)S(1)}, u32[]{:S(2)}) copy-start(bf16[48,1024]{1,0:T(8,128)(2,1)S(1)} %collective-permute-done.13.refs_5_) | copy-start | bytes 294916
  112.4 15.7 %collective-permute-start.27 = (bf16[48,1024]{1,0:T(8,128)(2,1)S(1)}, bf16[48,1024]{1,0:T(8,128)(2,1)S(1)}, u32[]{:S(2)}, u32[]{:S(2)}) collective-permute-start(bf16[48,1024]{1,0:T(8,128)(2,1)S(1)} %slice.141), channel_id=1, source_target_pairs={{0,1},{1,0},{2,3},{3,2},{4,5},{5,4},{6,7},{7,6},{8,9},{9,8},{10,11... | collective-permute-start | bytes 294920 | tf_op jit(solution)/shard_map/ppermute | solution.py:554
  114.5 13.6 %copy-start.13 = (bf16[48,1024]{1,0:T(8,128)(2,1)}, bf16[48,1024]{1,0:T(8,128)(2,1)S(1)}, u32[]{:S(2)}) copy-start(bf16[48,1024]{1,0:T(8,128)(2,1)S(1)} %collective-permute-done.15.refs_6_) | copy-start | bytes 294916
  114.5 13.6 %collective-permute-start.29 = (bf16[48,1024]{1,0:T(8,128)(2,1)S(1)}, bf16[48,1024]{1,0:T(8,128)(2,1)S(1)}, u32[]{:S(2)}, u32[]{:S(2)}) collective-permute-start(bf16[48,1024]{1,0:T(8,128)(2,1)S(1)} %slice.144), channel_id=1, source_target_pairs={{0,1},{1,0},{2,3},{3,2},{4,5},{5,4},{6,7},{7,6},{8,9},{9,8},{10,11... | collective-permute-start | bytes 294920 | tf_op jit(solution)/shard_map/ppermute | solution.py:554
  116.6 11.5 %copy-start.14 = (bf16[48,1024]{1,0:T(8,128)(2,1)}, bf16[48,1024]{1,0:T(8,128)(2,1)S(1)}, u32[]{:S(2)}) copy-start(bf16[48,1024]{1,0:T(8,128)(2,1)S(1)} %collective-permute-done.35.refs_15_) | copy-start | bytes 294916
  116.7 11.6 %collective-permute-start.31 = (bf16[48,1024]{1,0:T(8,128)(2,1)S(1)}, bf16[48,1024]{1,0:T(8,128)(2,1)S(1)}, u32[]{:S(2)}, u32[]{:S(2)}) collective-permute-start(bf16[48,1024]{1,0:T(8,128)(2,1)S(1)} %slice.147), channel_id=1, source_target_pairs={{0,1},{1,0},{2,3},{3,2},{4,5},{5,4},{6,7},{7,6},{8,9},{9,8},{10,11... | collective-permute-start | bytes 294920 | tf_op jit(solution)/shard_map/ppermute | solution.py:554
  118.8 9.4 %copy-start.15 = (bf16[48,1024]{1,0:T(8,128)(2,1)}, bf16[48,1024]{1,0:T(8,128)(2,1)S(1)}, u32[]{:S(2)}) copy-start(bf16[48,1024]{1,0:T(8,128)(2,1)S(1)} %collective-permute-done.23.refs_9_) | copy-start | bytes 294916
  118.8 9.5 %collective-permute-start.33 = (bf16[48,1024]{1,0:T(8,128)(2,1)S(1)}, bf16[48,1024]{1,0:T(8,128)(2,1)S(1)}, u32[]{:S(2)}, u32[]{:S(2)}) collective-permute-start(bf16[48,1024]{1,0:T(8,128)(2,1)S(1)} %slice.150), channel_id=1, source_target_pairs={{0,1},{1,0},{2,3},{3,2},{4,5},{5,4},{6,7},{7,6},{8,9},{9,8},{10,11... | collective-permute-start | bytes 294920 | tf_op jit(solution)/shard_map/ppermute | solution.py:554
  (12 other events, 27.8 us)

commit v2 on v1

--- a/solution.py
+++ b/solution.py
@@ -138,14 +138,16 @@
     return ((tile / pair_count).astype(jnp.bfloat16)[None], harvest)
 
 
-BLOCKS = 8
 ROWS = 2 * SLOT
-EXTRA = HD
+EARLY = (8, 12, 9, 13)
+LATE = (0, 2, 4, 6, 10, 14)
+EARLY_ROWS = len(EARLY) * ROWS
+LATE_ROWS = len(LATE) * ROWS
+PIECES = len(EARLY) // 2 + len(LATE)
+SPAN = 2 * ROWS
+ABSENT = 2.0**100
+WIDE_A = 12 * HD
 VMEM_SPEC = pl.BlockSpec(memory_space=pltpu.VMEM)
-
-
-def cost(flops, moved, exps=0):
-    return pl.CostEstimate(flops=flops, bytes_accessed=moved, transcendentals=exps)
 
 
 def nt(left, right):
@@ -156,7 +158,7 @@
     return lax.dot_general(left, right, (((1,), (0,)), ((), ())), preferred_element_type=F32)
 
 
-def attend_heads(q_ref, kd, vd, ko, vo, use_off, put):
+def attend_heads(q_ref, first, kd, vd, ko, vo, use_off, put):
     rows = q_ref.shape[0]
     heads = q_ref.shape[1] // HD
     factor = math.log2(math.e) / math.sqrt(HD)
@@ -167,18 +169,20 @@
         allowed = col <= row
         for head in range(heads):
             query = q_ref[:, head * HD : (head + 1) * HD]
-            diag = jnp.where(allowed, nt(query, kd[...]), NEGATIVE)
+            key_head = (first + head) // (H // KVH)
+            at = slice(key_head * HD, (key_head + 1) * HD)
+            diag = jnp.where(allowed, nt(query, kd[:, at]), NEGATIVE)
             peak = jnp.max(diag, axis=-1, keepdims=True)
             if with_off:
-                off = nt(query, ko[...])
+                off = nt(query, ko[:, at])
                 peak = jnp.maximum(peak, jnp.max(off, axis=-1, keepdims=True))
             diag_w = jnp.exp2((diag - peak) * factor)
             total = jnp.sum(diag_w, axis=-1, keepdims=True)
-            mixed = dot(diag_w.astype(BF16), vd[...])
+            mixed = dot(diag_w.astype(BF16), vd[:, at])
             if with_off:
                 off_w = jnp.exp2((off - peak) * factor)
                 total = total + jnp.sum(off_w, axis=-1, keepdims=True)
-                mixed = mixed + dot(off_w.astype(BF16), vo[...])
+                mixed = mixed + dot(off_w.astype(BF16), vo[:, at])
             put(head, mixed * (1.0 / total))
 
     @pl.when(use_off)
@@ -197,7 +201,7 @@
         att_ref[:, head * HD : (head + 1) * HD] = value
         sq_ref[0] += value * value
 
-    attend_heads(q_ref, k_ref, v_ref, kp_ref, vp_ref, place[0] == 1, put)
+    attend_heads(q_ref, 0, k_ref, v_ref, kp_ref, vp_ref, place[0] == 1, put)
 
 
 def attend_own(place, queries, key_rows, value_rows, partner_kv):
@@ -224,73 +228,91 @@
             jax.ShapeDtypeStruct((rows, 2 * wide), F32),
             jax.ShapeDtypeStruct((2, rows, HD), F32),
         ],
-        cost_estimate=cost(2 * 2 * 16 * rows * 2 * rows * HD, 4 << 20, 16 * rows * 2 * rows),
         name="attend_own",
     )(place, queries, key_rows, value_rows, partner_kv, partner_kv)
+
+
+def absent_of(first, second):
+    present = jnp.sum(first.astype(F32) + second.astype(F32), axis=-1, keepdims=True)
+    return (1.0 - present) * ABSENT
 
 
 def partner_a_kernel(
     place, q_ref, kd, vd, ko, vo, own_ref, so_ref, sp_ref, att_ref, sq_ref, out_ref
 ):
+    wide = q_ref.shape[1]
     sq_ref[...] = jnp.zeros_like(sq_ref)
 
     def put(head, value):
         att_ref[:, head * HD : (head + 1) * HD] = value
         sq_ref[...] += value * value
 
-    attend_heads(q_ref, kd, vd, ko, vo, place[0] == 0, put)
+    attend_heads(q_ref, 0, kd, vd, ko, vo, place[0] == 0, put)
     picked = dot(so_ref[...], own_ref[...].astype(BF16))
-    out_ref[...] = (picked + dot(sp_ref[...], att_ref[...].astype(BF16))).astype(BF16)
-
-
-def partner_specs(rows, wide, chunk):
+    out_ref[:, wide:] = picked[:, wide:].astype(BF16)
+    picked = picked[:, 0:wide] + dot(sp_ref[...], att_ref[...].astype(BF16))
+    out_ref[:, 0:wide] = picked.astype(BF16)
+
+
+def partner_specs(rows, wide):
     return [
         pl.BlockSpec((rows, wide), lambda i, t: (0, 0)),
-        pl.BlockSpec((rows, HD), lambda i, t: (0, chunk)),
-        pl.BlockSpec((rows, HD), lambda i, t: (0, 2 + chunk)),
-        pl.BlockSpec((rows, HD), lambda i, t: (0, 2 * t[0] + chunk)),
-        pl.BlockSpec((rows, HD), lambda i, t: (0, 2 * t[0] + chunk)),
+        pl.BlockSpec((rows, 2 * HD), lambda i, t: (0, 0)),
+        pl.BlockSpec((rows, 2 * HD), lambda i, t: (0, 1)),
+        pl.BlockSpec((rows, 2 * HD), lambda i, t: (0, t[0])),
+        pl.BlockSpec((rows, 2 * HD), lambda i, t: (0, t[0])),
     ]
 
 
 def attend_partner_a(place, query_a, partner_kv, key_rows, value_rows, att_own, picks):
     rows, wide = query_a.shape
-    out_rows = picks.shape[0]
+    half = att_own.shape[1]
     return pl.pallas_call(
         partner_a_kernel,
         grid_spec=pltpu.PrefetchScalarGridSpec(
             num_scalar_prefetch=1,
             grid=(1,),
-            in_specs=partner_specs(rows, wide, 0)
+            in_specs=partner_specs(rows, wide)
             + [
-                pl.BlockSpec((rows, wide), lambda i, t: (0, 0)),
-                pl.BlockSpec((out_rows, rows), lambda i, t: (0, t[0])),
-                pl.BlockSpec((out_rows, rows), lambda i, t: (0, 1 - t[0])),
+                pl.BlockSpec((rows, half), lambda i, t: (0, 0)),
+                pl.BlockSpec((EARLY_ROWS, rows), lambda i, t: (0, t[0])),
+                pl.BlockSpec((EARLY_ROWS, rows), lambda i, t: (0, 1 - t[0])),
             ],
             out_specs=[
                 pl.BlockSpec((rows, wide), lambda i, t: (0, 0)),
                 pl.BlockSpec((rows, HD), lambda i, t: (0, 0)),
-                pl.BlockSpec((out_rows, wide), lambda i, t: (0, 0)),
+                pl.BlockSpec((EARLY_ROWS, half), lambda i, t: (0, 0)),
             ],
         ),
         out_shape=[
             jax.ShapeDtypeStruct((rows, wide), F32),
             jax.ShapeDtypeStruct((rows, HD), F32),
-            jax.ShapeDtypeStruct((out_rows, wide), BF16),
+            jax.ShapeDtypeStruct((EARLY_ROWS, half), BF16),
         ],
-        cost_estimate=cost(2 * 2 * 8 * rows * 2 * rows * HD, 3 << 20, 8 * rows * 2 * rows),
         name="attend_partner_a",
     )(place, query_a, partner_kv, partner_kv, key_rows, value_rows, att_own, picks, picks)
 
 
-def partner_b_kernel(place, q_ref, kd, vd, ko, vo, sqo_ref, sqa_ref, att_ref, sum_ref, sq_ref):
+def partner_b_kernel(place, q_ref, kd, vd, ko, vo, sqo_ref, sqa_ref, so_ref, sp_ref, early_ref, *refs):
+    att_ref, sum_ref = refs[0:2]
+    out_refs, sq_ref = refs[2:-1], refs[-1]
+    wide = early_ref.shape[1] - q_ref.shape[1]
     sq_ref[...] = sqa_ref[...]
 
     def put(head, value):
         att_ref[:, head * HD : (head + 1) * HD] = value
         sq_ref[...] += value * value
 
-    attend_heads(q_ref, kd, vd, ko, vo, place[0] == 0, put)
+    first = H // 2 - q_ref.shape[1] // HD
+    attend_heads(q_ref, first, kd, vd, ko, vo, place[0] == 0, put)
+    absent = absent_of(so_ref[...], sp_ref[...])
+    picked = dot(sp_ref[...], att_ref[...].astype(BF16)) + early_ref[:, wide:].astype(F32)
+    picked = (picked + absent).astype(BF16)
+    early = (early_ref[:, 0:wide].astype(F32) + absent).astype(BF16)
+    for index, out_ref in enumerate(out_refs):
+        at = slice(index * ROWS, (index + 1) * ROWS)
+        out_ref[:, 0:wide] = early[at]
+        out_ref[:, wide:] = picked[at]
     ones = jnp.ones((8, HD), F32)
 
     def lanes(values):
@@ -306,35 +328,47 @@
     sum_ref[8:16, :] = lanes(sqo_ref[0] + sqo_ref[1])
 
 
-def attend_partner_b(place, query_b, partner_kv, key_rows, value_rows, sq_own, sq_a):
+def attend_partner_b(
+    place, query_b, partner_kv, key_rows, value_rows, sq_own, sq_a, picks, early_a
+):
     rows, wide = query_b.shape
+    half = early_a.shape[1]
+    whole = lambda i, t: (0, 0)
     return pl.pallas_call(
         partner_b_kernel,
         grid_spec=pltpu.PrefetchScalarGridSpec(
             num_scalar_prefetch=1,
             grid=(1,),
-            in_specs=partner_specs(rows, wide, 1)
+            in_specs=partner_specs(rows, wide)
             + [
                 pl.BlockSpec((2, rows, HD), lambda i, t: (0, 0, 0)),
-                pl.BlockSpec((rows, HD), lambda i, t: (0, 0)),
+                pl.BlockSpec((rows, HD), whole),
+                pl.BlockSpec((EARLY_ROWS, rows), lambda i, t: (0, t[0])),
+                pl.BlockSpec((EARLY_ROWS, rows), lambda i, t: (0, 1 - t[0])),
+                pl.BlockSpec((EARLY_ROWS, half), whole),
             ],
             out_specs=[
-                pl.BlockSpec((rows, wide), lambda i, t: (0, 0)),
-                pl.BlockSpec((16, rows), lambda i, t: (0, 0)),
-            ],
+                pl.BlockSpec((rows, wide), whole),
+                pl.BlockSpec((16, rows), whole),
+            ]
+            + [pl.BlockSpec((ROWS, half), whole)] * len(EARLY),
             scratch_shapes=[pltpu.VMEM((rows, HD), F32)],
         ),
         out_shape=[
             jax.ShapeDtypeStruct((rows, wide), F32),
             jax.ShapeDtypeStruct((16, rows), F32),
-        ],
-        cost_estimate=cost(2 * 2 * 8 * rows * 2 * rows * HD, 2 << 20, 8 * rows * 2 * rows),
+        ]
+        + [jax.ShapeDtypeStruct((ROWS, half), BF16)] * len(EARLY),
         name="attend_partner_b",
-    )(place, query_b, partner_kv, partner_kv, key_rows, value_rows, sq_own, sq_a)
+    )(
+        place, query_b, partner_kv, partner_kv, key_rows, value_rows,
+        sq_own, sq_a, picks, picks, early_a,
+    )
 
 
 def norm_kernel(
-    place, own_ref, pa_ref, pb_ref, mine_ref, theirs_ref, gain_ref, so_ref, sp_ref, h_ref, out_ref
+    place, own_ref, pa_ref, pb_ref, mine_ref, theirs_ref, gain_ref, so_ref, sp_ref,
+    h_ref, stay_ref, leave_ref,
 ):
     rows = own_ref.shape[0]
     wide = pa_ref.shape[1]
@@ -348,40 +382,29 @@
             precision=lax.Precision.HIGHEST,
             preferred_element_type=F32,
         )
-        return lax.rsqrt(total * (1.0 / D) + EPSILON)
-
-    lane = lax.broadcasted_iota(jnp.int32, (rows, HD), 1)
-
-    def coded(scale):
-        high = scale.astype(BF16)
-        rest = scale - high.astype(F32)
-        low = rest.astype(BF16)
-        last = (rest - low.astype(F32)).astype(BF16)
-        picked = jnp.where(lane == 0, high.astype(F32), 0.0)
-        picked = jnp.where(lane == 1, low.astype(F32), picked)
-        picked = jnp.where(lane == 2, last.astype(F32), picked)
-        return jnp.where(lane == 3, 1.0, picked).astype(BF16)
+        return lax.rsqrt(total * (1.0 / D) + EPSILON)[:, 0:1]
 
     own_scale = scale_of(mine_ref[8:16, :], theirs_ref[0:8, :])
     other_scale = scale_of(mine_ref[0:8, :], theirs_ref[8:16, :])
     own_at = pl.ds(pl.multiple_of(place[0] * rows, rows), rows)
     other_at = pl.ds(pl.multiple_of((1 - place[0]) * rows, rows), rows)
     gain = gain_ref[...]
-    h_ref[own_at, :] = (own_ref[...] * own_scale[:, 0:1] * gain).astype(BF16)
-    h_ref[other_at, 0:wide] = (pa_ref[...] * other_scale[:, 0:1] * gain[:, 0:wide]).astype(BF16)
-    h_ref[other_at, wide:] = (pb_ref[...] * other_scale[:, 0:1] * gain[:, wide:]).astype(BF16)
-    picks_own = so_ref[...]
-    picks_other = sp_ref[...]
-    picked = dot(picks_own, h_ref[own_at, wide:]) + dot(picks_other, h_ref[other_at, wide:])
-    out_ref[:, 0:wide] = picked.astype(BF16)
-    extra = dot(picks_own, coded(own_scale)) + dot(picks_other, coded(other_scale))
-    out_ref[:, wide:] = extra.astype(BF16)
+    h_ref[own_at, :] = (own_ref[...] * own_scale * gain).astype(BF16)
+    h_ref[other_at, 0:wide] = (pa_ref[...] * other_scale * gain[:, 0:wide]).astype(BF16)
+    h_ref[other_at, wide:] = (pb_ref[...] * other_scale * gain[:, wide:]).astype(BF16)
+    start = EARLY_ROWS
+    for out_ref in (stay_ref, leave_ref):
+        first = so_ref[start : start + LATE_ROWS, :]
+        second = sp_ref[start : start + LATE_ROWS, :]
+        picked = dot(first, h_ref[own_at, :]) + dot(second, h_ref[other_at, :])
+        out_ref[...] = (picked + absent_of(first, second)).astype(BF16)
+        start += LATE_ROWS
 
 
 def normalize(place, att_own, att_a, att_b, mine, theirs, norm_gain, picks):
     rows, half = att_own.shape
-    wide = half // 2
-    out_rows = picks.shape[0]
+    wide, last = att_a.shape[1], att_b.shape[1]
+    all_rows = picks.shape[0]
     whole = lambda i, t: (0, 0)
     return pl.pallas_call(
         norm_kernel,
@@ -391,23 +414,24 @@
             in_specs=[
                 pl.BlockSpec((rows, half), whole),
                 pl.BlockSpec((rows, wide), whole),
-                pl.BlockSpec((rows, wide), whole),
+                pl.BlockSpec((rows, last), whole),
                 pl.BlockSpec((16, rows), whole),
                 pl.BlockSpec((16, rows), whole),
                 pl.BlockSpec((1, half), lambda i, t: (0, t[0])),
-                pl.BlockSpec((out_rows, rows), lambda i, t: (0, t[0])),
-                pl.BlockSpec((out_rows, rows), lambda i, t: (0, 1 - t[0])),
+                pl.BlockSpec((all_rows, rows), lambda i, t: (0, t[0])),
+                pl.BlockSpec((all_rows, rows), lambda i, t: (0, 1 - t[0])),
             ],
             out_specs=[
                 pl.BlockSpec((2 * rows, half), whole),
-                pl.BlockSpec((out_rows, wide + EXTRA), whole),
+                pl.BlockSpec((LATE_ROWS, half), whole),
+                pl.BlockSpec((LATE_ROWS, half), whole),
             ],
         ),
         out_shape=[
             jax.ShapeDtypeStruct((2 * rows, half), BF16),
-            jax.ShapeDtypeStruct((out_rows, wide + EXTRA), BF16),
+            jax.ShapeDtypeStruct((LATE_ROWS, half), BF16),
+            jax.ShapeDtypeStruct((LATE_ROWS, half), BF16),
         ],
-        cost_estimate=cost(2 * out_rows * 2 * rows * wide, 8 << 20),
         name="normalize",
     )(place, att_own, att_a, att_b, mine, theirs, norm_gain, picks, picks)
 
@@ -432,40 +456,42 @@
         in_specs=[VMEM_SPEC] * 3,
         out_specs=VMEM_SPEC,
         out_shape=jax.ShapeDtypeStruct((keys.shape[0], tokens), BF16),
-        cost_estimate=cost(4 * tokens * tokens, 1 << 20),
         name="class_picks",
     )(labels.reshape(tokens, 1), labels.reshape(1, tokens), keys)
 
 
 def gram_own_kernel(place, *refs):
-    a_refs = refs[0:BLOCKS]
-    b_refs = refs[BLOCKS : 2 * BLOCKS]
-    gain_ref, out_ref, turned_ref, extra_ref, rows_ref = refs[2 * BLOCKS :]
-    span = 2 * ROWS
-    wide = a_refs[0].shape[1]
+    own_refs, across_refs = refs[0:PIECES], refs[PIECES : PIECES + 2]
+    gain_ref, out_ref, turned_ref, extra_ref, rows_ref = refs[PIECES + 2 :]
     step = out_ref.shape[0]
 
     @pl.when(pl.program_id(0) == 0)
     def _():
-        for block in range(BLOCKS):
-            at = slice(block * span, (block + 1) * span)
-            extra = b_refs[block][:, wide:].astype(F32)
-            extra_ref[at, :] = extra
-            scale = extra[:, 0:1] + extra[:, 1:2] + extra[:, 2:3]
-            scaled = a_refs[block][...].astype(F32) * scale * gain_ref[:, 0:wide]
-            rows_ref[at, 0:wide] = scaled.astype(BF16)
-            rows_ref[at, wide:] = b_refs[block][:, 0:wide]
+        lane = lax.broadcasted_iota(jnp.int32, (SPAN, HD), 1)
+        for piece in range(PIECES):
+            at = slice(piece * SPAN, (piece + 1) * SPAN)
+            present = own_refs[piece][:, 0:1].astype(F32) < 0.5 * ABSENT
+            rows = jnp.where(present, own_refs[piece][...].astype(F32), 0.0)
+            if piece < 2:
+                other = jnp.where(present, across_refs[piece][...].astype(F32), 0.0)
+                squares = jnp.sum(rows * rows + other * other, axis=-1, keepdims=True)
+                scale = lax.rsqrt(squares * (1.0 / D) + EPSILON)
+                rows = rows * scale * gain_ref[...]
+            else:
+                scale = jnp.ones((SPAN, 1), F32)
+            rows_ref[at, :] = rows.astype(BF16)
+            flag = jnp.where(present, 1.0, 0.0)
+            extra_ref[at, :] = jnp.where(lane == 0, scale, jnp.where(lane == 1, flag, 0.0))
         turned_ref[...] = jnp.transpose(rows_ref[...])
 
-    count = jnp.sum(extra_ref[:, 3:4])
+    count = jnp.sum(extra_ref[:, 1:2])
     left = turned_ref[pl.ds(pl.multiple_of(pl.program_id(0) * step, step), step), :]
     out_ref[...] = (dot(left, rows_ref[...]) * (1.0 / count)).astype(BF16)
 
 
-def gram_own(place, pieces_a, pieces_b, norm_gain):
-    wide = pieces_a[0].shape[1]
-    half = 2 * wide
-    total = BLOCKS * 2 * ROWS
+def gram_own(place, pieces, across_pieces, norm_gain):
+    half = pieces[0].shape[1]
+    total = PIECES * SPAN
     step = 512
     whole = lambda i, t: (0, 0)
     return pl.pallas_call(
@@ -473,51 +499,44 @@
         grid_spec=pltpu.PrefetchScalarGridSpec(
             num_scalar_prefetch=1,
             grid=(half // step,),
-            in_specs=[pl.BlockSpec((2 * ROWS, wide), whole)] * BLOCKS
-            + [pl.BlockSpec((2 * ROWS, wide + EXTRA), whole)] * BLOCKS
+            in_specs=[pl.BlockSpec((SPAN, half), whole)] * (PIECES + 2)
             + [pl.BlockSpec((1, half), lambda i, t: (0, t[0]))],
             out_specs=[
                 pl.BlockSpec((step, half), lambda i, t: (i, t[0])),
                 pl.BlockSpec((half, total), whole),
-                pl.BlockSpec((total, EXTRA), whole),
+                pl.BlockSpec((total, HD), whole),
             ],
             scratch_shapes=[pltpu.VMEM((total, half), BF16)],
         ),
         out_shape=[
             jax.ShapeDtypeStruct((half, 2 * half), BF16),
             jax.ShapeDtypeStruct((half, total), BF16),
-            jax.ShapeDtypeStruct((total, EXTRA), F32),
+            jax.ShapeDtypeStruct((total, HD), F32),
         ],
-        cost_estimate=cost(2 * half * half * total, 14 << 20),
         name="gram_own",
-    )(place, *pieces_a, *pieces_b, norm_gain)
+    )(place, *pieces, *across_pieces, norm_gain)
 
 
 def gram_other_kernel(place, *refs):
-    a_refs = refs[0:BLOCKS]
-    b_refs = refs[BLOCKS : 2 * BLOCKS]
-    gain_ref, turned_ref, extra_ref, _, out_ref, rows_ref = refs[2 * BLOCKS :]
-    span = 2 * ROWS
-    wide = a_refs[0].shape[1]
+    other_refs = refs[0:PIECES]
+    gain_ref, turned_ref, extra_ref, _, out_ref, rows_ref = refs[PIECES:]
 
     @pl.when(pl.program_id(0) == 0)
     def _():
-        for block in range(BLOCKS):
-            at = slice(block * span, (block + 1) * span)
-            extra = extra_ref[at, :]
-            scale = extra[:, 0:1] + extra[:, 1:2] + extra[:, 2:3]
-            scaled = a_refs[block][...].astype(F32) * scale * gain_ref[:, 0:wide]
-            rows_ref[at, 0:wide] = scaled.astype(BF16)
-            rows_ref[at, wide:] = b_refs[block][...]
-
-    count = jnp.sum(extra_ref[:, 3:4])
+        for piece in range(PIECES):
+            at = slice(piece * SPAN, (piece + 1) * SPAN)
+            rows = other_refs[piece][...].astype(F32)
+            if piece < 2:
+                rows = rows * extra_ref[at, 0:1] * gain_ref[...]
+            rows_ref[at, :] = jnp.where(extra_ref[at, 1:2] > 0.5, rows, 0.0).astype(BF16)
+
+    count = jnp.sum(extra_ref[:, 1:2])
     out_ref[...] = (dot(turned_ref[...], rows_ref[...]) * (1.0 / count)).astype(BF16)
 
 
-def gram_other(place, pieces_a, pieces_b, norm_gain, turned, extra, partial):
-    wide = pieces_a[0].shape[1]
-    half = 2 * wide
-    total = BLOCKS * 2 * ROWS
+def gram_other(place, pieces, norm_gain, turned, extra, partial):
+    half = pieces[0].shape[1]
+    total = PIECES * SPAN
     step = 512
     whole = lambda i, t: (0, 0)
     return pl.pallas_call(
@@ -525,21 +544,24 @@
         grid_spec=pltpu.PrefetchScalarGridSpec(
             num_scalar_prefetch=1,
             grid=(half // step,),
-            in_specs=[pl.BlockSpec((2 * ROWS, wide), whole)] * (2 * BLOCKS)
+            in_specs=[pl.BlockSpec((SPAN, half), whole)] * PIECES
             + [
                 pl.BlockSpec((1, half), lambda i, t: (0, 1 - t[0])),
                 pl.BlockSpec((step, total), lambda i, t: (i, 0)),
-                pl.BlockSpec((total, EXTRA), whole),
+                pl.BlockSpec((total, HD), whole),
                 pl.BlockSpec(memory_space=pl.ANY),
             ],
             out_specs=pl.BlockSpec((step, half), lambda i, t: (i, 1 - t[0])),
             scratch_shapes=[pltpu.VMEM((total, half), BF16)],
         ),
         out_shape=jax.ShapeDtypeStruct((half, 2 * half), BF16),
-        input_output_aliases={2 * BLOCKS + 4: 0},
-        cost_estimate=cost(2 * half * half * total, 14 << 20),
+        input_output_aliases={PIECES + 4: 0},
         name="gram_other",
-    )(place, *pieces_a, *pieces_b, norm_gain, turned, extra, partial)
+    )(place, *pieces, norm_gain, turned, extra, partial)
+
+
+def after(value, *earlier):
+    return lax.optimization_barrier((value, *earlier))[0]
 
 
 def paired_local(queries, key_rows, value_rows, norm_gain, labels, pair_list, owner_map):
@@ -547,51 +569,73 @@
     my_tensor = lax.axis_index("tensor")
     my_group = lax.axis_index("dp")
     place = jnp.full((1,), my_tensor, jnp.int32)
-    wide = D // KVH
     swap = [(0, 1), (1, 0)]
 
-    def across(value):
-        return lax.ppermute(value, "tensor", swap)
-
-    def hop(value, offset):
-        return lax.ppermute(value, "dp", [(i, i ^ offset) for i in range(group_count)])
+    def across(value, name):
+        with jax.named_scope(name):
+            return lax.ppermute(value, "tensor", swap)
+
+    def hop(value, offset, name):
+        with jax.named_scope(name):
+            return lax.ppermute(value, "dp", [(i, i ^ offset) for i in range(group_count)])
 
     def theirs(rows, start, width):
         return lax.dynamic_slice_in_dim(rows, (1 - my_tensor) * start, width, 1)
 
     part = 2 * HD
     sent_kv = jnp.concatenate([theirs(key_rows, part, part), theirs(value_rows, part, part)], 1)
-    partner_kv = across(sent_kv)
-    other_half = (1 - my_tensor) * 2 * wide
-    query_a = across(lax.dynamic_slice_in_dim(queries, other_half, wide, 1))
-    query_b = across(lax.dynamic_slice_in_dim(queries, other_half + wide, wide, 1))
-
-    order = jnp.concatenate([jnp.arange(0, 16, 2), jnp.arange(1, 16, 2)]).astype(jnp.int32)
+    partner_kv = across(sent_kv, "x_kv")
+    other_half = (1 - my_tensor) * (D // 2)
+    last = D // 2 - WIDE_A
+    sent_a = lax.dynamic_slice_in_dim(queries, other_half, WIDE_A, 1)
+    sent_b = lax.dynamic_slice_in_dim(queries, other_half + WIDE_A, last, 1)
+    query_a = across(sent_a, "x_qa")
+    query_b = across(after(sent_b, partner_kv), "x_qb")
+
+    order = jnp.asarray(EARLY + LATE + tuple(j + 1 for j in LATE), jnp.int32)
     classes = pair_list[owner_map[my_group ^ order]]
     picks = class_picks(labels, classes)
     gain = norm_gain.reshape(1, D)
 
-    def spread(rows):
-        width = rows.shape[1]
-        stay, leave = rows[: BLOCKS * ROWS], rows[BLOCKS * ROWS :]
-        came = hop(leave, 1)
-        joined = jnp.concatenate(
-            [stay.reshape(BLOCKS, ROWS, width), came.reshape(BLOCKS, ROWS, width)], 1
-        )
-        return [joined[0]] + [hop(joined[m], 2 * m) for m in range(1, BLOCKS)]
-
     att_own, sq_own = attend_own(place, queries, key_rows, value_rows, partner_kv)
-    att_a, sq_a, rows_a = attend_partner_a(
+    att_a, sq_a, early_a = attend_partner_a(
         place, query_a, partner_kv, key_rows, value_rows, att_own, picks
     )
-    own_a = spread(rows_a)
-    other_a = [across(piece) for piece in own_a]
-    att_b, mine = attend_partner_b(place, query_b, partner_kv, key_rows, value_rows, sq_own, sq_a)
-    harvest, rows_b = normalize(place, att_own, att_a, att_b, mine, across(mine), gain, picks)
-    own_b = spread(rows_b)
-    other_b = [across(piece[:, :wide]) for piece in own_b]
-    partial, turned, extra = gram_own(place, own_a, own_b, gain)
-    gram = gram_other(place, other_a, other_b, gain, turned, extra, partial)
+    att_b, mine, *early = attend_partner_b(
+        place, query_b, partner_kv, key_rows, value_rows, sq_own, sq_a, picks, early_a
+    )
+    first = [hop(rows, j, f"far_e{j}") for rows, j in zip(early, EARLY)]
+    sums = after(across(mine, "x_sums"), first[0])
+    harvest, stay, leave = normalize(place, att_own, att_a, att_b, mine, sums, gain, picks)
+    came = hop(after(leave, first[1]), 1, "core")
+    shape = (len(LATE), ROWS, D // 2)
+    joined = jnp.concatenate([stay.reshape(shape), came.reshape(shape)], 1)
+    joined = {j: joined[index] for index, j in enumerate(LATE)}
+    own, other = {0: joined[0]}, {}
+    pairs = [jnp.concatenate(first[0:2]), jnp.concatenate(first[2:4])]
+
+    def far(j, *earlier):
+        own[j] = hop(after(joined[j], *earlier), j, f"far_{j}")
+
+    x_e0 = across(pairs[0], "x_e0")
+    other[0] = across(own[0], "x_0")
+    far(10, first[0])
+    far(2, first[1])
+    x_e1 = across(after(pairs[1], x_e0), "x_e1")
+    far(14, first[2], x_e0)
+    other[2] = across(after(own[2], other[0]), "x_2")
+    far(4, own[2], other[0])
+    other[10] = across(after(own[10], x_e1), "x_10")
+    far(6, own[10], x_e1)
+    other[4] = across(after(own[4], other[2]), "x_4")
+    other[6] = across(after(own[6], other[10]), "x_6")
+    other[14] = across(after(own[14], other[4]), "x_14")
+    partial, turned, extra = gram_own(
+        place, [*pairs, *[own[j] for j in LATE]], [x_e0, x_e1], gain
+    )
+    gram = gram_other(
+        place, [x_e0, x_e1, *[other[j] for j in LATE]], gain, turned, extra, partial
+    )
     return gram[None], harvest
 
 

time: 138 us -> 117 us (0.85)
  the two profiles are of different devices: /device:TPU:0 before, /device:TPU:8 now
where the time goes in v2:
time: 117 us
  Pallas kernels  40.6 us (35%)
  starting transfers between devices  34.6 us (30%)
  waiting for transfers between devices  30.5 us (26%)
  local copies, waits for them, and re-layouts  8.53 us (7%)
  other arithmetic  1.35 us (1%)
    ppermute x10, starting transfers between devices, hop(): lax.ppermute(value, 'dp', [(i, i ^ offset) for i in range(group_count)])  20.1 us
    ppermute x12, waiting for transfers between devices, across(): return lax.ppermute(value, 'tensor', swap)  17.1 us
    ppermute x12, starting transfers between devices, across(): return lax.ppermute(value, 'tensor', swap)  14.5 us
    ppermute x10, waiting for transfers between devices, hop(): lax.ppermute(value, 'dp', [(i, i ^ offset) for i in range(group_count)])  13.4 us
    pallas_call x1, Pallas kernels, gram_own(): pl.pallas_call(gram_own_kernel, grid_spec=pltpu.PrefetchScalarGridSpec(nu...  9.19 us
    pallas_call x1, Pallas kernels, gram_other(): pl.pallas_call(gram_other_kernel, grid_spec=pltpu.PrefetchScalarGridSpec(...  8.56 us
    pallas_call x1, Pallas kernels, attend_partner_a(): pl.pallas_call(partner_a_kernel, grid_spec=pltpu.PrefetchScalarGridSpec(n...  7.13 us
    pallas_call x1, Pallas kernels, normalize(): pl.pallas_call(norm_kernel, grid_spec=pltpu.PrefetchScalarGridSpec(num_sc...  5.09 us
  transfers between devices with their start and end apart: 22, of which 12 were waited for; matrix products, arithmetic and copies ran while one was open for 6% of the time, Pallas kernels for 24%

profile of v2, /device:TPU:8, one launch (start us, length us, event | category | flops | bytes accessed | tf_op | source)
XLA Modules:
  0.0 116.5 jit_solution(18406751070695232715)
XLA Ops:
  0.6 0.0 copy-start
  0.7 1.0 constant_dynamic-slice_fusion.1
  1.6 0.0 copy-start.23
  1.7 0.0 copy-start.22
  1.7 1.6 %collective-permute-start = (bf16[256,512]{1,0:T(8,128)(2,1)S(1)}, bf16[256,512]{1,0:T(8,128)(2,1)S(1)}, u32[]{:S(2)}, u32[]{:S(2)}) collective-permute-start(bf16[256,512]{1,0:T(8,128)(2,1)S(1)} %pad_maximum_fusion), channel_id=1, source_target_pairs={{0,1},{1,0},{2,3},{3,2},{4,5},{5,4},{6,7},{7,6},{8,9},{9,8},{10,11... | collective-permute-start | bytes 786440 | tf_op jit(solution)/shard_map/x_kv/ppermute | solution.py:576
  3.3 1.2 %constant_dynamic-slice_fusion = bf16[256,1536]{1,0:T(8,128)(2,1)S(1)} fusion(bf16[256,4096]{1,0:T(8,128)(2,1)} %q_ref.1, s32[]{:T(128)S(6)} %select_n.25), kind=kLoop, calls=%fused_computation.35 | loop fusion | bytes 1572868 | tf_op jit(solution)/shard_map/dynamic_slice | solution.py:590
  4.5 0.6 collective-permute-start.2
  5.1 0.7 gather_fusion
  5.8 0.1 copy.12
  5.8 0.6 gather_fusion.1
  6.4 1.0 constant_dynamic-slice_fusion.3
  7.4 3.5 %collective-permute-done.kp_ref.vp_ref.kd.vd = bf16[256,512]{1,0:T(8,128)(2,1)S(1)} collective-permute-done((bf16[256,512]{1,0:T(8,128)(2,1)S(1)}, bf16[256,512]{1,0:T(8,128)(2,1)S(1)}, u32[]{:S(2)}, u32[]{:S(2)}) %collective-permute-start) | collective-permute-done | bytes 262176 | tf_op jit(solution)/shard_map/x_kv/ppermute | solution.py:576
  10.9 1.5 %collective-permute-start.1 = (bf16[256,512]{1,0:T(8,128)(2,1)S(1)}, bf16[256,512]{1,0:T(8,128)(2,1)S(1)}, u32[]{:S(2)}, u32[]{:S(2)}) collective-permute-start(bf16[256,512]{1,0:T(8,128)(2,1)S(1)} %constant_dynamic-slice_fusion.3), channel_id=1, source_target_pairs={{0,1},{1,0},{2,3},{3,2},{4,5},{5,4},{6,7},{7,6},{8,9},{9,8},{10,11... | collective-permute-start | bytes 786440 | tf_op jit(solution)/shard_map/x_qb/ppermute | solution.py:576
  12.4 0.1 iota_add_fusion
  12.5 0.8 add.61.key_ref
  13.3 0.9 copy.13.col_ref
  14.2 2.0 %class_picks.1.so_ref.sp_ref = bf16[384,512]{1,0:T(8,128)(2,1)} custom-call(s32[512,1]{1,0:T(8,128)} %copy.13.col_ref, s32[1,512]{1,0:T(1,128)} %bitcast.29, s32[384,1]{1,0:T(8,128)} %add.61.key_ref), custom_call_target="tpu_custom_call" | custom-call | tf_op jit(solution)/shard_map/class_picks/pallas_call | solution.py:454
  16.2 4.5 %attend_own.1 = (f32[256,2048]{1,0:T(8,128)}, f32[2,256,128]{2,1,0:T(8,128)}) custom-call(s32[1]{0:T(128)} %bitcast.place, bf16[256,4096]{1,0:T(8,128)(2,1)} %q_ref.1, bf16[256,512]{1,0:T(8,128)(2,1)} %ko.3, bf16[256,512]{1,0:T(8,128)(2,1)} %vo.3, bf16[256,512]{1,0:T(8,128)(2,1)} %copy-done.1, bf16[256,512]{1,0:T(8,128)(2,1)} %copy-done.1), custom_call_target="tpu_custom_call" | custom-call | tf_op jit(solution)/shard_map/attend_own/pallas_call | solution.py:210
  20.7 7.1 %collective-permute-done.2.q_ref = bf16[256,1536]{1,0:T(8,128)(2,1)S(1)} collective-permute-done((bf16[256,1536]{1,0:T(8,128)(2,1)S(1)}, bf16[256,1536]{1,0:T(8,128)(2,1)S(1)}, u32[]{:S(2)}, u32[]{:S(2)}) %collective-permute-start.2) | collective-permute-done | bytes 786464 | tf_op jit(solution)/shard_map/x_qa/ppermute | solution.py:576
  27.8 0.9 copy-done.4
  28.7 7.1 %attend_partner_a.1 = (f32[256,1536]{1,0:T(8,128)}, f32[256,128]{1,0:T(8,128)}, bf16[96,2048]{1,0:T(8,128)(2,1)}) custom-call(s32[1]{0:T(128)} %bitcast.place, bf16[256,1536]{1,0:T(8,128)(2,1)} %copy-done.4, bf16[256,512]{1,0:T(8,128)(2,1)} %copy-done.1, bf16[256,512]{1,0:T(8,128)(2,1)} %copy-done.1, bf16[256,512]{1,0:T(8,128)(2,1)} %ko.3, ...), custom_call_target="tpu_custom_call" | custom-call | tf_op jit(solution)/shard_map/attend_partner_a/pallas_call | solution.py:270
  35.8 0.0 collective-permute-done.1.q_ref
  35.8 0.7 copy-done.8
  36.5 4.1 %attend_partner_b.1 = (f32[256,512]{1,0:T(8,128)}, f32[16,256]{1,0:T(8,128)}, bf16[24,2048]{1,0:T(8,128)(2,1)}, bf16[24,2048]{1,0:T(8,128)(2,1)}, bf16[24,2048]{1,0:T(8,128)(2,1)}, /*index=5*/bf16[24,2048]{1,0:T(8,128)(2,1)}) custom-call(s32[1]{0:T(128)} %bitcast.place, bf16[256,512]{1,0:T(8,128)(2,1)} %copy-done.8, bf16[256,512]{1,0:T(8,128)(2,1)} %copy-done.1, ...), custom_call_target="tpu_custom_call" | custom-call | tf_op jit(solution)/shard_map/attend_partner_b/pallas_call | solution.py:337
  40.6 2.6 %collective-permute-start.3 = (bf16[24,2048]{1,0:T(8,128)(2,1)}, bf16[24,2048]{1,0:T(8,128)(2,1)S(1)}, u32[]{:S(2)}, u32[]{:S(2)}) collective-permute-start(bf16[24,2048]{1,0:T(8,128)(2,1)} %get-tuple-element.38), channel_id=1, source_target_pairs={{0,16},{2,18},{4,20},{6,22},{8,24},{10,26},{12,28},{14,30},{16,0},... | collective-permute-start | bytes 294920 | tf_op jit(solution)/shard_map/far_e8/ppermute | solution.py:580
  43.2 0.0 collective-permute-start.4
  43.2 0.0 collective-permute-start.9
  43.2 0.0 collective-permute-start.6
  43.2 3.0 %collective-permute-start.7 = (bf16[24,2048]{1,0:T(8,128)(2,1)}, bf16[24,2048]{1,0:T(8,128)(2,1)S(1)}, u32[]{:S(2)}, u32[]{:S(2)}) collective-permute-start(bf16[24,2048]{1,0:T(8,128)(2,1)} %get-tuple-element.41), channel_id=1, source_target_pairs={{0,26},{2,24},{4,30},{6,28},{8,18},{10,16},{12,22},{14,20},{16,10}... | collective-permute-start | bytes 294920 | tf_op jit(solution)/shard_map/far_e13/ppermute | solution.py:580
  46.1 1.0 collective-permute-done.9.theirs_ref
  47.1 5.9 %collective-permute-done.3 = bf16[24,2048]{1,0:T(8,128)(2,1)S(1)} collective-permute-done((bf16[24,2048]{1,0:T(8,128)(2,1)}, bf16[24,2048]{1,0:T(8,128)(2,1)S(1)}, u32[]{:S(2)}, u32[]{:S(2)}) %collective-permute-start.3) | collective-permute-done | bytes 98336 | tf_op jit(solution)/shard_map/far_e8/ppermute | solution.py:580
  53.0 5.1 %normalize.1 = (bf16[512,2048]{1,0:T(8,128)(2,1)}, bf16[144,2048]{1,0:T(8,128)(2,1)}, bf16[144,2048]{1,0:T(8,128)(2,1)}) custom-call(s32[1]{0:T(128)} %bitcast.place, f32[256,2048]{1,0:T(8,128)} %get-tuple-element.35.own_ref, f32[256,1536]{1,0:T(8,128)} %get-tuple-element.43.pa_ref, f32[256,512]{1,0:T(8,128)} %get-tuple-element.44.pb_ref, ...), custom_call_target="tpu_custom_call" | custom-call | tf_op jit(solution)/shard_map/normalize/pallas_call | solution.py:409
  58.1 0.0 collective-permute-done.4
  58.1 0.0 collective-permute-start.10
  58.1 0.1 collective-permute-start.5
  58.2 0.0 collective-permute-done.6
  58.2 2.1 %collective-permute-done.10 = bf16[144,2048]{1,0:T(8,128)(2,1)S(1)} collective-permute-done((bf16[144,2048]{1,0:T(8,128)(2,1)}, bf16[144,2048]{1,0:T(8,128)(2,1)S(1)}, u32[]{:S(2)}, u32[]{:S(2)}) %collective-permute-start.10) | collective-permute-done | bytes 589856 | tf_op jit(solution)/shard_map/core/ppermute | solution.py:580
  60.3 1.2 %fusion.10 = (bf16[48,2048]{1,0:T(8,128)(2,1)S(1)}, bf16[48,2048]{1,0:T(8,128)(2,1)S(1)}, bf16[48,2048]{1,0:T(8,128)(2,1)S(1)}, bf16[48,2048]{1,0:T(8,128)(2,1)S...) fusion(bf16[6,24,2048]{2,1,0:T(8,128)(2,1)S(1)} %bitcast.25, bf16[6,24,2048]{2,1,0:T(8,128)(2,1)} %bitcast.24), kind=kLoop, calls=%fused_computation.24 | loop fusion | flops 2359296 | bytes 2359296 | tf_op jit(solution)/shard_map/squeeze | solution.py:613
  61.5 1.6 %collective-permute-start.12 = (bf16[48,2048]{1,0:T(8,128)(2,1)S(1)}, bf16[48,2048]{1,0:T(8,128)(2,1)S(1)}, u32[]{:S(2)}, u32[]{:S(2)}) collective-permute-start(bf16[48,2048]{1,0:T(8,128)(2,1)S(1)} %get-tuple-element.50), channel_id=1, source_target_pairs={{0,4},{2,6},{4,0},{6,2},{8,12},{10,14},{12,8},{14,10},{16,20},{18,... | collective-permute-start | bytes 589832 | tf_op jit(solution)/shard_map/far_2/ppermute | solution.py:580
  63.1 2.3 %collective-permute-done.5.refs_8_.refs_0_ = bf16[48,2048]{1,0:T(8,128)(2,1)S(1)} collective-permute-done((bf16[48,2048]{1,0:T(8,128)(2,1)S(1)}, bf16[48,2048]{1,0:T(8,128)(2,1)S(1)}, u32[]{:S(2)}, u32[]{:S(2)}) %collective-permute-start.5) | collective-permute-done | bytes 196640 | tf_op jit(solution)/shard_map/x_e0/ppermute | solution.py:576
  65.5 0.3 collective-permute-start.8
  65.8 4.4 %collective-permute-start.16 = (bf16[48,2048]{1,0:T(8,128)(2,1)S(1)}, bf16[48,2048]{1,0:T(8,128)(2,1)S(1)}, u32[]{:S(2)}, u32[]{:S(2)}) collective-permute-start(bf16[48,2048]{1,0:T(8,128)(2,1)S(1)} %get-tuple-element.54), channel_id=1, source_target_pairs={{0,20},{2,22},{4,16},{6,18},{8,28},{10,30},{12,24},{14,26},{16,4},... | collective-permute-start | bytes 589832 | tf_op jit(solution)/shard_map/far_10/ppermute | solution.py:580
  70.2 0.0 collective-permute-done.12.refs_3_
  70.2 0.7 collective-permute-done.11.refs_2_
  70.9 1.4 %collective-permute-start.13 = (bf16[48,2048]{1,0:T(8,128)(2,1)S(1)}, bf16[48,2048]{1,0:T(8,128)(2,1)S(1)}, u32[]{:S(2)}, u32[]{:S(2)}) collective-permute-start(bf16[48,2048]{1,0:T(8,128)(2,1)S(1)} %collective-permute-done.12.refs_3_), channel_id=1, source_target_pairs={{0,1},{1,0},{2,3},{3,2},{4,5},{5,4},{6,7},{7,6},{8,9},{9,8},{10,11... | collective-permute-start | bytes 589832 | tf_op jit(solution)/shard_map/x_2/ppermute | solution.py:576
  72.3 0.5 collective-permute-start.14
  72.8 2.2 %collective-permute-start.20 = (bf16[48,2048]{1,0:T(8,128)(2,1)S(1)}, bf16[48,2048]{1,0:T(8,128)(2,1)S(1)}, u32[]{:S(2)}, u32[]{:S(2)}) collective-permute-start(bf16[48,2048]{1,0:T(8,128)(2,1)S(1)} %get-tuple-element.58), channel_id=1, source_target_pairs={{0,28},{2,30},{4,24},{6,26},{8,20},{10,22},{12,16},{14,18},{16,12}... | collective-permute-start | bytes 589832 | tf_op jit(solution)/shard_map/far_14/ppermute | solution.py:580
  75.0 0.1 collective-permute-done.8.refs_9_.refs_1_
  75.1 1.4 %collective-permute-done.16.refs_6_ = bf16[48,2048]{1,0:T(8,128)(2,1)S(1)} collective-permute-done((bf16[48,2048]{1,0:T(8,128)(2,1)S(1)}, bf16[48,2048]{1,0:T(8,128)(2,1)S(1)}, u32[]{:S(2)}, u32[]{:S(2)}) %collective-permute-start.16) | collective-permute-done | bytes 196640 | tf_op jit(solution)/shard_map/far_10/ppermute | solution.py:580
  76.5 5.9 %collective-permute-start.17 = (bf16[48,2048]{1,0:T(8,128)(2,1)S(1)}, bf16[48,2048]{1,0:T(8,128)(2,1)S(1)}, u32[]{:S(2)}, u32[]{:S(2)}) collective-permute-start(bf16[48,2048]{1,0:T(8,128)(2,1)S(1)} %get-tuple-element.55), channel_id=1, source_target_pairs={{0,12},{2,14},{4,8},{6,10},{8,4},{10,6},{12,0},{14,2},{16,28},{18,... | collective-permute-start | bytes 589832 | tf_op jit(solution)/shard_map/far_6/ppermute | solution.py:580
  82.4 4.0 %collective-permute-start.18 = (bf16[48,2048]{1,0:T(8,128)(2,1)S(1)}, bf16[48,2048]{1,0:T(8,128)(2,1)S(1)}, u32[]{:S(2)}, u32[]{:S(2)}) collective-permute-start(bf16[48,2048]{1,0:T(8,128)(2,1)S(1)} %collective-permute-done.16.refs_6_), channel_id=1, source_target_pairs={{0,1},{1,0},{2,3},{3,2},{4,5},{5,4},{6,7},{7,6},{8,9},{9,8},{10,11... | collective-permute-start | bytes 589832 | tf_op jit(solution)/shard_map/x_10/ppermute | solution.py:576
  86.5 0.0 collective-permute-done.13.refs_3_
  86.5 0.0 collective-permute-done.14.refs_4_
  86.5 0.1 collective-permute-start.15
  86.6 4.1 %collective-permute-done.17.refs_5_ = bf16[48,2048]{1,0:T(8,128)(2,1)S(1)} collective-permute-done((bf16[48,2048]{1,0:T(8,128)(2,1)S(1)}, bf16[48,2048]{1,0:T(8,128)(2,1)S(1)}, u32[]{:S(2)}, u32[]{:S(2)}) %collective-permute-start.17) | collective-permute-done | bytes 196640 | tf_op jit(solution)/shard_map/far_6/ppermute | solution.py:580
  90.6 0.6 collective-permute-done.18.refs_6_
  91.2 2.5 %collective-permute-start.19 = (bf16[48,2048]{1,0:T(8,128)(2,1)S(1)}, bf16[48,2048]{1,0:T(8,128)(2,1)S(1)}, u32[]{:S(2)}, u32[]{:S(2)}) collective-permute-start(bf16[48,2048]{1,0:T(8,128)(2,1)S(1)} %collective-permute-done.17.refs_5_), channel_id=1, source_target_pairs={{0,1},{1,0},{2,3},{3,2},{4,5},{5,4},{6,7},{7,6},{8,9},{9,8},{10,11... | collective-permute-start | bytes 589832 | tf_op jit(solution)/shard_map/x_6/ppermute | solution.py:576
  93.7 0.0 collective-permute-done.20.refs_7_
  93.7 1.7 %collective-permute-done.15.refs_4_ = bf16[48,2048]{1,0:T(8,128)(2,1)S(1)} collective-permute-done((bf16[48,2048]{1,0:T(8,128)(2,1)S(1)}, bf16[48,2048]{1,0:T(8,128)(2,1)S(1)}, u32[]{:S(2)}, u32[]{:S(2)}) %collective-permute-start.15) | collective-permute-done | bytes 196640 | tf_op jit(solution)/shard_map/x_4/ppermute | solution.py:576
  95.5 2.5 %collective-permute-start.21 = (bf16[48,2048]{1,0:T(8,128)(2,1)S(1)}, bf16[48,2048]{1,0:T(8,128)(2,1)S(1)}, u32[]{:S(2)}, u32[]{:S(2)}) collective-permute-start(bf16[48,2048]{1,0:T(8,128)(2,1)S(1)} %collective-permute-done.20.refs_7_), channel_id=1, source_target_pairs={{0,1},{1,0},{2,3},{3,2},{4,5},{5,4},{6,7},{7,6},{8,9},{9,8},{10,11... | collective-permute-start | bytes 589832 | tf_op jit(solution)/shard_map/x_14/ppermute | solution.py:576
  98.0 9.2 %gram_own.1 = (bf16[2048,4096]{1,0:T(8,128)(2,1)}, bf16[2048,384]{1,0:T(8,128)(2,1)}, f32[384,128]{1,0:T(8,128)}) custom-call(s32[1]{0:T(128)} %bitcast.place, bf16[48,2048]{1,0:T(8,128)(2,1)} %copy-done.7, bf16[48,2048]{1,0:T(8,128)(2,1)} %copy-done.6, bf16[48,2048]{1,0:T(8,128)(2,1)} %copy-done.5, bf16[48,2048]{1,0:T(8,128)(2,1)} %copy-done.15, ...), custom_call_target="tpu_custom_call" | custom-call | tf_op jit(solution)/shard_map/gram_own/pallas_call | solution.py:497
  107.3 0.6 copy-done.13
  107.9 0.1 copy-done.14
  108.0 8.6 %gram_other.1 = bf16[2048,4096]{1,0:T(8,128)(2,1)} custom-call(s32[1]{0:T(128)} %bitcast.place, bf16[48,2048]{1,0:T(8,128)(2,1)} %copy-done.2, bf16[48,2048]{1,0:T(8,128)(2,1)} %copy-done.3, bf16[48,2048]{1,0:T(8,128)(2,1)} %copy-done.9, bf16[48,2048]{1,0:T(8,128)(2,1)} %copy-done.10, bf16[48,2048]{1,0:T(8,128)(2,1)} %copy-done.12, ...), custom_call_target="tpu_custom_call", output_to_operand_aliasing={{}: (12, {})} | custom-call | tf_op jit(solution)/shard_map/gram_other/pallas_call | solution.py:542
  (55 shorter events, 0.2 us)
Async XLA Ops:
  0.6 4.4 %copy-start = (s32[16]{0:T(128)S(1)}, s32[16]{0:T(128)}, u32[]{:S(2)}) copy-start(s32[16]{0:T(128)} %param.14) | copy-start | bytes 196
  1.6 3.4 %copy-start.23 = (s32[16]{0:T(128)S(1)}, s32[16]{0:T(128)}, u32[]{:S(2)}) copy-start(s32[16]{0:T(128)} %constant.30.clone) | copy-start | bytes 196
  1.7 4.1 %copy-start.22 = (s32[16,2]{0,1:T(2,128)S(1)}, s32[16,2]{0,1:T(2,128)}, u32[]{:S(2)}) copy-start(s32[16,2]{0,1:T(2,128)} %param.13) | copy-start | bytes 388
  1.7 9.2 %collective-permute-start = (bf16[256,512]{1,0:T(8,128)(2,1)S(1)}, bf16[256,512]{1,0:T(8,128)(2,1)S(1)}, u32[]{:S(2)}, u32[]{:S(2)}) collective-permute-start(bf16[256,512]{1,0:T(8,128)(2,1)S(1)} %pad_maximum_fusion), channel_id=1, source_target_pairs={{0,1},{1,0},{2,3},{3,2},{4,5},{5,4},{6,7},{7,6},{8,9},{9,8},{10,11... | collective-permute-start | bytes 786440 | tf_op jit(solution)/shard_map/x_kv/ppermute | solution.py:576
  3.3 10.1 %copy-start.21 = (s32[512]{0:T(512)S(1)}, s32[512]{0:T(512)}, u32[]{:S(2)}) copy-start(s32[512]{0:T(512)} %param.12) | copy-start | bytes 6148
  4.5 23.3 %collective-permute-start.2 = (bf16[256,1536]{1,0:T(8,128)(2,1)S(1)}, bf16[256,1536]{1,0:T(8,128)(2,1)S(1)}, u32[]{:S(2)}, u32[]{:S(2)}) collective-permute-start(bf16[256,1536]{1,0:T(8,128)(2,1)S(1)} %constant_dynamic-slice_fusion), channel_id=1, source_target_pairs={{0,1},{1,0},{2,3},{3,2},{4,5},{5,4},{6,7},{7,6},{8,9},{9,8},{10,11... | collective-permute-start | bytes 2359304 | tf_op jit(solution)/shard_map/x_qa/ppermute | solution.py:576
  10.9 5.3 %copy-start.1 = (bf16[256,512]{1,0:T(8,128)(2,1)}, bf16[256,512]{1,0:T(8,128)(2,1)S(1)}, u32[]{:S(2)}) copy-start(bf16[256,512]{1,0:T(8,128)(2,1)S(1)} %collective-permute-done.kp_ref.vp_ref.kd.vd) | copy-start | bytes 786436
  10.9 24.9 %collective-permute-start.1 = (bf16[256,512]{1,0:T(8,128)(2,1)S(1)}, bf16[256,512]{1,0:T(8,128)(2,1)S(1)}, u32[]{:S(2)}, u32[]{:S(2)}) collective-permute-start(bf16[256,512]{1,0:T(8,128)(2,1)S(1)} %constant_dynamic-slice_fusion.3), channel_id=1, source_target_pairs={{0,1},{1,0},{2,3},{3,2},{4,5},{5,4},{6,7},{7,6},{8,9},{9,8},{10,11... | collective-permute-start | bytes 786440 | tf_op jit(solution)/shard_map/x_qb/ppermute | solution.py:576
  27.8 0.9 copy-start.4
  35.8 0.7 copy-start.8
  40.6 12.4 %collective-permute-start.3 = (bf16[24,2048]{1,0:T(8,128)(2,1)}, bf16[24,2048]{1,0:T(8,128)(2,1)S(1)}, u32[]{:S(2)}, u32[]{:S(2)}) collective-permute-start(bf16[24,2048]{1,0:T(8,128)(2,1)} %get-tuple-element.38), channel_id=1, source_target_pairs={{0,16},{2,18},{4,20},{6,22},{8,24},{10,26},{12,28},{14,30},{16,0},... | collective-permute-start | bytes 294920 | tf_op jit(solution)/shard_map/far_e8/ppermute | solution.py:580
  43.2 14.9 %collective-permute-start.4 = (bf16[24,2048]{1,0:T(8,128)(2,1)}, bf16[24,2048]{1,0:T(8,128)(2,1)S(1)}, u32[]{:S(2)}, u32[]{:S(2)}) collective-permute-start(bf16[24,2048]{1,0:T(8,128)(2,1)} %get-tuple-element.39), channel_id=1, source_target_pairs={{0,24},{2,26},{4,28},{6,30},{8,16},{10,18},{12,20},{14,22},{16,8},... | collective-permute-start | bytes 294920 | tf_op jit(solution)/shard_map/far_e12/ppermute | solution.py:580
  43.2 3.9 %collective-permute-start.9 = (f32[16,256]{1,0:T(8,128)}, f32[16,256]{1,0:T(8,128)S(1)}, u32[]{:S(2)}, u32[]{:S(2)}) collective-permute-start(f32[16,256]{1,0:T(8,128)} %get-tuple-element.45.mine_ref), channel_id=1, source_target_pairs={{0,1},{1,0},{2,3},{3,2},{4,5},{5,4},{6,7},{7,6},{8,9},{9,8},{10,11... | collective-permute-start | bytes 49160 | tf_op jit(solution)/shard_map/x_sums/ppermute | solution.py:576
  43.2 15.0 %collective-permute-start.6 = (bf16[24,2048]{1,0:T(8,128)(2,1)}, bf16[24,2048]{1,0:T(8,128)(2,1)S(1)}, u32[]{:S(2)}, u32[]{:S(2)}) collective-permute-start(bf16[24,2048]{1,0:T(8,128)(2,1)} %get-tuple-element.40), channel_id=1, source_target_pairs={{0,18},{2,16},{4,22},{6,20},{8,26},{10,24},{12,30},{14,28},{16,2},... | collective-permute-start | bytes 294920 | tf_op jit(solution)/shard_map/far_e9/ppermute | solution.py:580
  43.2 19.9 %collective-permute-start.7 = (bf16[24,2048]{1,0:T(8,128)(2,1)}, bf16[24,2048]{1,0:T(8,128)(2,1)S(1)}, u32[]{:S(2)}, u32[]{:S(2)}) collective-permute-start(bf16[24,2048]{1,0:T(8,128)(2,1)} %get-tuple-element.41), channel_id=1, source_target_pairs={{0,26},{2,24},{4,30},{6,28},{8,18},{10,16},{12,22},{14,20},{16,10}... | collective-permute-start | bytes 294920 | tf_op jit(solution)/shard_map/far_e13/ppermute | solution.py:580
  47.1 5.9 %copy-start.20 = (f32[16,256]{1,0:T(8,128)}, f32[16,256]{1,0:T(8,128)S(1)}, u32[]{:S(2)}) copy-start(f32[16,256]{1,0:T(8,128)S(1)} %collective-permute-done.9.theirs_ref) | copy-start | bytes 49156
  58.1 2.2 %collective-permute-start.10 = (bf16[144,2048]{1,0:T(8,128)(2,1)}, bf16[144,2048]{1,0:T(8,128)(2,1)S(1)}, u32[]{:S(2)}, u32[]{:S(2)}) collective-permute-start(bf16[144,2048]{1,0:T(8,128)(2,1)} %get-tuple-element.49), channel_id=1, source_target_pairs={{0,2},{2,0},{4,6},{6,4},{8,10},{10,8},{12,14},{14,12},{16,18},{18,... | collective-permute-start | bytes 1769480 | tf_op jit(solution)/shard_map/core/ppermute | solution.py:580
  58.1 3.4 %copy-start.7 = (bf16[48,2048]{1,0:T(8,128)(2,1)}, bf16[48,2048]{1,0:T(8,128)(2,1)S(1)}, u32[]{:S(2)}) copy-start(bf16[48,2048]{1,0:T(8,128)(2,1)S(1)} %constant_dynamic-update-slice_fusion.refs_0_) | copy-start | bytes 589828
  58.1 7.4 %collective-permute-start.5 = (bf16[48,2048]{1,0:T(8,128)(2,1)S(1)}, bf16[48,2048]{1,0:T(8,128)(2,1)S(1)}, u32[]{:S(2)}, u32[]{:S(2)}) collective-permute-start(bf16[48,2048]{1,0:T(8,128)(2,1)S(1)} %constant_dynamic-update-slice_fusion.refs_0_), channel_id=1, source_target_pairs={{0,1},{1,0},{2,3},{3,2},{4,5},{5,4},{6,7},{7,6},{8,9},{9,8},{10,11... | collective-permute-start | bytes 589832 | tf_op jit(solution)/shard_map/x_e0/ppermute | solution.py:576
  61.5 36.4 %copy-start.5 = (bf16[48,2048]{1,0:T(8,128)(2,1)}, bf16[48,2048]{1,0:T(8,128)(2,1)S(1)}, u32[]{:S(2)}) copy-start(bf16[48,2048]{1,0:T(8,128)(2,1)S(1)} %get-tuple-element.65.refs_2_) | copy-start | bytes 589828
  61.5 8.7 %collective-permute-start.12 = (bf16[48,2048]{1,0:T(8,128)(2,1)S(1)}, bf16[48,2048]{1,0:T(8,128)(2,1)S(1)}, u32[]{:S(2)}, u32[]{:S(2)}) collective-permute-start(bf16[48,2048]{1,0:T(8,128)(2,1)S(1)} %get-tuple-element.50), channel_id=1, source_target_pairs={{0,4},{2,6},{4,0},{6,2},{8,12},{10,14},{12,8},{14,10},{16,20},{18,... | collective-permute-start | bytes 589832 | tf_op jit(solution)/shard_map/far_2/ppermute | solution.py:580
  63.1 7.8 %collective-permute-start.11 = (bf16[48,2048]{1,0:T(8,128)(2,1)S(1)}, bf16[48,2048]{1,0:T(8,128)(2,1)S(1)}, u32[]{:S(2)}, u32[]{:S(2)}) collective-permute-start(bf16[48,2048]{1,0:T(8,128)(2,1)S(1)} %get-tuple-element.65.refs_2_), channel_id=1, source_target_pairs={{0,1},{1,0},{2,3},{3,2},{4,5},{5,4},{6,7},{7,6},{8,9},{9,8},{10,11... | collective-permute-start | bytes 589832 | tf_op jit(solution)/shard_map/x_0/ppermute | solution.py:576
  63.1 34.8 %copy-start.6 = (bf16[48,2048]{1,0:T(8,128)(2,1)}, bf16[48,2048]{1,0:T(8,128)(2,1)S(1)}, u32[]{:S(2)}) copy-start(bf16[48,2048]{1,0:T(8,128)(2,1)S(1)} %constant_dynamic-update-slice_fusion.2.refs_1_) | copy-start | bytes 589828
  65.5 32.5 %copy-start.2 = (bf16[48,2048]{1,0:T(8,128)(2,1)}, bf16[48,2048]{1,0:T(8,128)(2,1)S(1)}, u32[]{:S(2)}) copy-start(bf16[48,2048]{1,0:T(8,128)(2,1)S(1)} %collective-permute-done.5.refs_8_.refs_0_) | copy-start | bytes 589828
  65.5 9.6 %collective-permute-start.8 = (bf16[48,2048]{1,0:T(8,128)(2,1)S(1)}, bf16[48,2048]{1,0:T(8,128)(2,1)S(1)}, u32[]{:S(2)}, u32[]{:S(2)}) collective-permute-start(bf16[48,2048]{1,0:T(8,128)(2,1)S(1)} %constant_dynamic-update-slice_fusion.2.refs_1_), channel_id=1, source_target_pairs={{0,1},{1,0},{2,3},{3,2},{4,5},{5,4},{6,7},{7,6},{8,9},{9,8},{10,11... | collective-permute-start | bytes 589832 | tf_op jit(solution)/shard_map/x_e1/ppermute | solution.py:576
  65.8 10.8 %collective-permute-start.16 = (bf16[48,2048]{1,0:T(8,128)(2,1)S(1)}, bf16[48,2048]{1,0:T(8,128)(2,1)S(1)}, u32[]{:S(2)}, u32[]{:S(2)}) collective-permute-start(bf16[48,2048]{1,0:T(8,128)(2,1)S(1)} %get-tuple-element.54), channel_id=1, source_target_pairs={{0,20},{2,22},{4,16},{6,18},{8,28},{10,30},{12,24},{14,26},{16,4},... | collective-permute-start | bytes 589832 | tf_op jit(solution)/shard_map/far_10/ppermute | solution.py:580
  70.2 27.8 %copy-start.15 = (bf16[48,2048]{1,0:T(8,128)(2,1)}, bf16[48,2048]{1,0:T(8,128)(2,1)S(1)}, u32[]{:S(2)}) copy-start(bf16[48,2048]{1,0:T(8,128)(2,1)S(1)} %collective-permute-done.12.refs_3_) | copy-start | bytes 589828
  70.9 36.3 %copy-start.9 = (bf16[48,2048]{1,0:T(8,128)(2,1)}, bf16[48,2048]{1,0:T(8,128)(2,1)S(1)}, u32[]{:S(2)}) copy-start(bf16[48,2048]{1,0:T(8,128)(2,1)S(1)} %collective-permute-done.11.refs_2_) | copy-start | bytes 589828
  70.9 15.6 %collective-permute-start.13 = (bf16[48,2048]{1,0:T(8,128)(2,1)S(1)}, bf16[48,2048]{1,0:T(8,128)(2,1)S(1)}, u32[]{:S(2)}, u32[]{:S(2)}) collective-permute-start(bf16[48,2048]{1,0:T(8,128)(2,1)S(1)} %collective-permute-done.12.refs_3_), channel_id=1, source_target_pairs={{0,1},{1,0},{2,3},{3,2},{4,5},{5,4},{6,7},{7,6},{8,9},{9,8},{10,11... | collective-permute-start | bytes 589832 | tf_op jit(solution)/shard_map/x_2/ppermute | solution.py:576
  72.3 14.2 %collective-permute-start.14 = (bf16[48,2048]{1,0:T(8,128)(2,1)S(1)}, bf16[48,2048]{1,0:T(8,128)(2,1)S(1)}, u32[]{:S(2)}, u32[]{:S(2)}) collective-permute-start(bf16[48,2048]{1,0:T(8,128)(2,1)S(1)} %get-tuple-element.52), channel_id=1, source_target_pairs={{0,8},{2,10},{4,12},{6,14},{8,0},{10,2},{12,4},{14,6},{16,24},{18,... | collective-permute-start | bytes 589832 | tf_op jit(solution)/shard_map/far_4/ppermute | solution.py:580
  72.8 20.9 %collective-permute-start.20 = (bf16[48,2048]{1,0:T(8,128)(2,1)S(1)}, bf16[48,2048]{1,0:T(8,128)(2,1)S(1)}, u32[]{:S(2)}, u32[]{:S(2)}) collective-permute-start(bf16[48,2048]{1,0:T(8,128)(2,1)S(1)} %get-tuple-element.58), channel_id=1, source_target_pairs={{0,28},{2,30},{4,24},{6,26},{8,20},{10,22},{12,16},{14,18},{16,12}... | collective-permute-start | bytes 589832 | tf_op jit(solution)/shard_map/far_14/ppermute | solution.py:580
  75.1 22.8 %copy-start.3 = (bf16[48,2048]{1,0:T(8,128)(2,1)}, bf16[48,2048]{1,0:T(8,128)(2,1)S(1)}, u32[]{:S(2)}) copy-start(bf16[48,2048]{1,0:T(8,128)(2,1)S(1)} %collective-permute-done.8.refs_9_.refs_1_) | copy-start | bytes 589828
  76.5 21.4 %copy-start.16 = (bf16[48,2048]{1,0:T(8,128)(2,1)}, bf16[48,2048]{1,0:T(8,128)(2,1)S(1)}, u32[]{:S(2)}) copy-start(bf16[48,2048]{1,0:T(8,128)(2,1)S(1)} %collective-permute-done.16.refs_6_) | copy-start | bytes 589828
  76.5 14.1 %collective-permute-start.17 = (bf16[48,2048]{1,0:T(8,128)(2,1)S(1)}, bf16[48,2048]{1,0:T(8,128)(2,1)S(1)}, u32[]{:S(2)}, u32[]{:S(2)}) collective-permute-start(bf16[48,2048]{1,0:T(8,128)(2,1)S(1)} %get-tuple-element.55), channel_id=1, source_target_pairs={{0,12},{2,14},{4,8},{6,10},{8,4},{10,6},{12,0},{14,2},{16,28},{18,... | collective-permute-start | bytes 589832 | tf_op jit(solution)/shard_map/far_6/ppermute | solution.py:580
  82.4 8.8 %collective-permute-start.18 = (bf16[48,2048]{1,0:T(8,128)(2,1)S(1)}, bf16[48,2048]{1,0:T(8,128)(2,1)S(1)}, u32[]{:S(2)}, u32[]{:S(2)}) collective-permute-start(bf16[48,2048]{1,0:T(8,128)(2,1)S(1)} %collective-permute-done.16.refs_6_), channel_id=1, source_target_pairs={{0,1},{1,0},{2,3},{3,2},{4,5},{5,4},{6,7},{7,6},{8,9},{9,8},{10,11... | collective-permute-start | bytes 589832 | tf_op jit(solution)/shard_map/x_10/ppermute | solution.py:576
  86.5 20.8 %copy-start.10 = (bf16[48,2048]{1,0:T(8,128)(2,1)}, bf16[48,2048]{1,0:T(8,128)(2,1)S(1)}, u32[]{:S(2)}) copy-start(bf16[48,2048]{1,0:T(8,128)(2,1)S(1)} %collective-permute-done.13.refs_3_) | copy-start | bytes 589828
  86.5 11.5 %copy-start.18 = (bf16[48,2048]{1,0:T(8,128)(2,1)}, bf16[48,2048]{1,0:T(8,128)(2,1)S(1)}, u32[]{:S(2)}) copy-start(bf16[48,2048]{1,0:T(8,128)(2,1)S(1)} %collective-permute-done.14.refs_4_) | copy-start | bytes 589828
  86.5 9.0 %collective-permute-start.15 = (bf16[48,2048]{1,0:T(8,128)(2,1)S(1)}, bf16[48,2048]{1,0:T(8,128)(2,1)S(1)}, u32[]{:S(2)}, u32[]{:S(2)}) collective-permute-start(bf16[48,2048]{1,0:T(8,128)(2,1)S(1)} %collective-permute-done.14.refs_4_), channel_id=1, source_target_pairs={{0,1},{1,0},{2,3},{3,2},{4,5},{5,4},{6,7},{7,6},{8,9},{9,8},{10,11... | collective-permute-start | bytes 589832 | tf_op jit(solution)/shard_map/x_4/ppermute | solution.py:576
  90.6 7.3 %copy-start.19 = (bf16[48,2048]{1,0:T(8,128)(2,1)}, bf16[48,2048]{1,0:T(8,128)(2,1)S(1)}, u32[]{:S(2)}) copy-start(bf16[48,2048]{1,0:T(8,128)(2,1)S(1)} %collective-permute-done.17.refs_5_) | copy-start | bytes 589828
  91.2 16.0 %copy-start.11 = (bf16[48,2048]{1,0:T(8,128)(2,1)}, bf16[48,2048]{1,0:T(8,128)(2,1)S(1)}, u32[]{:S(2)}) copy-start(bf16[48,2048]{1,0:T(8,128)(2,1)S(1)} %collective-permute-done.18.refs_6_) | copy-start | bytes 589828
  91.2 16.0 %collective-permute-start.19 = (bf16[48,2048]{1,0:T(8,128)(2,1)S(1)}, bf16[48,2048]{1,0:T(8,128)(2,1)S(1)}, u32[]{:S(2)}, u32[]{:S(2)}) collective-permute-start(bf16[48,2048]{1,0:T(8,128)(2,1)S(1)} %collective-permute-done.17.refs_5_), channel_id=1, source_target_pairs={{0,1},{1,0},{2,3},{3,2},{4,5},{5,4},{6,7},{7,6},{8,9},{9,8},{10,11... | collective-permute-start | bytes 589832 | tf_op jit(solution)/shard_map/x_6/ppermute | solution.py:576
  93.7 4.3 %copy-start.17 = (bf16[48,2048]{1,0:T(8,128)(2,1)}, bf16[48,2048]{1,0:T(8,128)(2,1)S(1)}, u32[]{:S(2)}) copy-start(bf16[48,2048]{1,0:T(8,128)(2,1)S(1)} %collective-permute-done.20.refs_7_) | copy-start | bytes 589828
  95.5 11.8 %copy-start.12 = (bf16[48,2048]{1,0:T(8,128)(2,1)}, bf16[48,2048]{1,0:T(8,128)(2,1)S(1)}, u32[]{:S(2)}) copy-start(bf16[48,2048]{1,0:T(8,128)(2,1)S(1)} %collective-permute-done.15.refs_4_) | copy-start | bytes 589828
  95.5 11.7 %collective-permute-start.21 = (bf16[48,2048]{1,0:T(8,128)(2,1)S(1)}, bf16[48,2048]{1,0:T(8,128)(2,1)S(1)}, u32[]{:S(2)}, u32[]{:S(2)}) collective-permute-start(bf16[48,2048]{1,0:T(8,128)(2,1)S(1)} %collective-permute-done.20.refs_7_), channel_id=1, source_target_pairs={{0,1},{1,0},{2,3},{3,2},{4,5},{5,4},{6,7},{7,6},{8,9},{9,8},{10,11... | collective-permute-start | bytes 589832 | tf_op jit(solution)/shard_map/x_14/ppermute | solution.py:576
  107.2 0.7 copy-start.13
  107.2 0.7 copy-start.14

commit v3 on v2

--- a/solution.py
+++ b/solution.py
@@ -139,12 +139,13 @@
 
 
 ROWS = 2 * SLOT
-EARLY = (8, 12, 9, 13)
-LATE = (0, 2, 4, 6, 10, 14)
+EARLY = (0, 1, 2, 3, 8, 9, 12, 13)
+LATE = (4, 6, 10, 14)
 EARLY_ROWS = len(EARLY) * ROWS
 LATE_ROWS = len(LATE) * ROWS
-PIECES = len(EARLY) // 2 + len(LATE)
 SPAN = 2 * ROWS
+PAIRS = len(EARLY) // 2
+PIECES = PAIRS + len(LATE)
 ABSENT = 2.0**100
 WIDE_A = 12 * HD
 VMEM_SPEC = pl.BlockSpec(memory_space=pltpu.VMEM)
@@ -158,32 +159,44 @@
     return lax.dot_general(left, right, (((1,), (0,)), ((), ())), preferred_element_type=F32)
 
 
-def attend_heads(q_ref, first, kd, vd, ko, vo, use_off, put):
+def attend_heads(q_ref, first, kd, vd, ko, vo, use_off, att_ref, put_squares):
     rows = q_ref.shape[0]
     heads = q_ref.shape[1] // HD
     factor = math.log2(math.e) / math.sqrt(HD)
+
+    def place_of(head):
+        key_head = (first + head) // (H // KVH)
+        return slice(key_head * HD, (key_head + 1) * HD)
 
     def run(with_off):
         row = lax.broadcasted_iota(jnp.int32, (rows, rows), 0)
         col = lax.broadcasted_iota(jnp.int32, (rows, rows), 1)
         allowed = col <= row
+
+        def scores_of(head):
+            query = q_ref[:, head * HD : (head + 1) * HD]
+            at = place_of(head)
+            return nt(query, kd[:, at]), nt(query, ko[:, at]) if with_off else None
+
+        following = scores_of(0)
+        squares = jnp.zeros((rows, HD), F32)
         for head in range(heads):
-            query = q_ref[:, head * HD : (head + 1) * HD]
-            key_head = (first + head) // (H // KVH)
-            at = slice(key_head * HD, (key_head + 1) * HD)
-            diag = jnp.where(allowed, nt(query, kd[:, at]), NEGATIVE)
-            peak = jnp.max(diag, axis=-1, keepdims=True)
+            (diag, off), at = following, place_of(head)
+            if head + 1 < heads:
+                following = scores_of(head + 1)
+            diag = jnp.where(allowed, diag, NEGATIVE)
+            both = jnp.maximum(diag, off) if with_off else diag
+            peak = jnp.max(both, axis=-1, keepdims=True)
+            weights = jnp.exp2((diag - peak) * factor)
+            mixed = dot(weights.astype(BF16), vd[:, at])
             if with_off:
-                off = nt(query, ko[:, at])
-                peak = jnp.maximum(peak, jnp.max(off, axis=-1, keepdims=True))
-            diag_w = jnp.exp2((diag - peak) * factor)
-            total = jnp.sum(diag_w, axis=-1, keepdims=True)
-            mixed = dot(diag_w.astype(BF16), vd[:, at])
-            if with_off:
-                off_w = jnp.exp2((off - peak) * factor)
-                total = total + jnp.sum(off_w, axis=-1, keepdims=True)
-                mixed = mixed + dot(off_w.astype(BF16), vo[:, at])
-            put(head, mixed * (1.0 / total))
+                off_weights = jnp.exp2((off - peak) * factor)
+                mixed = mixed + dot(off_weights.astype(BF16), vo[:, at])
+                weights = weights + off_weights
+            value = mixed * (1.0 / jnp.sum(weights, axis=-1, keepdims=True))
+            att_ref[:, head * HD : (head + 1) * HD] = value
+            squares = squares + value * value
+        put_squares(squares)
 
     @pl.when(use_off)
     def _():
@@ -195,13 +208,10 @@
 
 
 def own_kernel(place, q_ref, k_ref, v_ref, kp_ref, vp_ref, att_ref, sq_ref):
-    sq_ref[...] = jnp.zeros_like(sq_ref)
-
-    def put(head, value):
-        att_ref[:, head * HD : (head + 1) * HD] = value
-        sq_ref[0] += value * value
-
-    attend_heads(q_ref, 0, k_ref, v_ref, kp_ref, vp_ref, place[0] == 1, put)
+    def put(squares):
+        sq_ref[0] = squares
+
+    attend_heads(q_ref, 0, k_ref, v_ref, kp_ref, vp_ref, place[0] == 1, att_ref, put)
 
 
 def attend_own(place, queries, key_rows, value_rows, partner_kv):
@@ -241,13 +251,11 @@
     place, q_ref, kd, vd, ko, vo, own_ref, so_ref, sp_ref, att_ref, sq_ref, out_ref
 ):
     wide = q_ref.shape[1]
-    sq_ref[...] = jnp.zeros_like(sq_ref)
-
-    def put(head, value):
-        att_ref[:, head * HD : (head + 1) * HD] = value
-        sq_ref[...] += value * value
-
-    attend_heads(q_ref, 0, kd, vd, ko, vo, place[0] == 0, put)
+
+    def put(squares):
+        sq_ref[...] = squares
+
+    attend_heads(q_ref, 0, kd, vd, ko, vo, place[0] == 0, att_ref, put)
     picked = dot(so_ref[...], own_ref[...].astype(BF16))
     out_ref[:, wide:] = picked[:, wide:].astype(BF16)
     picked = picked[:, 0:wide] + dot(sp_ref[...], att_ref[...].astype(BF16))
@@ -297,14 +305,12 @@
     att_ref, sum_ref = refs[0:2]
     out_refs, sq_ref = refs[2:-1], refs[-1]
     wide = early_ref.shape[1] - q_ref.shape[1]
-    sq_ref[...] = sqa_ref[...]
-
-    def put(head, value):
-        att_ref[:, head * HD : (head + 1) * HD] = value
-        sq_ref[...] += value * value
+
+    def put(squares):
+        sq_ref[...] = sqa_ref[...] + squares
 
     first = H // 2 - q_ref.shape[1] // HD
-    attend_heads(q_ref, first, kd, vd, ko, vo, place[0] == 0, put)
+    attend_heads(q_ref, first, kd, vd, ko, vo, place[0] == 0, att_ref, put)
     absent = absent_of(so_ref[...], sp_ref[...])
     picked = dot(sp_ref[...], att_ref[...].astype(BF16)) + early_ref[:, wide:].astype(F32)
     picked = (picked + absent).astype(BF16)
@@ -366,48 +372,42 @@
     )
 
 
-def norm_kernel(
+def row_scale(first, second):
+    total = lax.dot_general(
+        first + second,
+        jnp.full((8, HD), 0.125, F32),
+        (((0,), (0,)), ((), ())),
+        precision=lax.Precision.HIGHEST,
+        preferred_element_type=F32,
+    )
+    return lax.rsqrt(total * (1.0 / D) + EPSILON)[:, 0:1]
+
+
+def late_kernel(
     place, own_ref, pa_ref, pb_ref, mine_ref, theirs_ref, gain_ref, so_ref, sp_ref,
-    h_ref, stay_ref, leave_ref,
+    stay_ref, leave_ref, first_ref, second_ref,
 ):
-    rows = own_ref.shape[0]
     wide = pa_ref.shape[1]
-    ones = jnp.full((8, HD), 0.125, F32)
-
-    def scale_of(first, second):
-        total = lax.dot_general(
-            first + second,
-            ones,
-            (((0,), (0,)), ((), ())),
-            precision=lax.Precision.HIGHEST,
-            preferred_element_type=F32,
-        )
-        return lax.rsqrt(total * (1.0 / D) + EPSILON)[:, 0:1]
-
-    own_scale = scale_of(mine_ref[8:16, :], theirs_ref[0:8, :])
-    other_scale = scale_of(mine_ref[0:8, :], theirs_ref[8:16, :])
-    own_at = pl.ds(pl.multiple_of(place[0] * rows, rows), rows)
-    other_at = pl.ds(pl.multiple_of((1 - place[0]) * rows, rows), rows)
+    own_scale = row_scale(mine_ref[8:16, :], theirs_ref[0:8, :])
+    other_scale = row_scale(mine_ref[0:8, :], theirs_ref[8:16, :])
     gain = gain_ref[...]
-    h_ref[own_at, :] = (own_ref[...] * own_scale * gain).astype(BF16)
-    h_ref[other_at, 0:wide] = (pa_ref[...] * other_scale * gain[:, 0:wide]).astype(BF16)
-    h_ref[other_at, wide:] = (pb_ref[...] * other_scale * gain[:, wide:]).astype(BF16)
-    start = EARLY_ROWS
-    for out_ref in (stay_ref, leave_ref):
-        first = so_ref[start : start + LATE_ROWS, :]
-        second = sp_ref[start : start + LATE_ROWS, :]
-        picked = dot(first, h_ref[own_at, :]) + dot(second, h_ref[other_at, :])
-        out_ref[...] = (picked + absent_of(first, second)).astype(BF16)
-        start += LATE_ROWS
-
-
-def normalize(place, att_own, att_a, att_b, mine, theirs, norm_gain, picks):
+    first_ref[...] = (own_ref[...] * own_scale * gain).astype(BF16)
+    second_ref[:, 0:wide] = (pa_ref[...] * other_scale * gain[:, 0:wide]).astype(BF16)
+    second_ref[:, wide:] = (pb_ref[...] * other_scale * gain[:, wide:]).astype(BF16)
+    first, second = so_ref[EARLY_ROWS:, :], sp_ref[EARLY_ROWS:, :]
+    picked = dot(first, first_ref[...]) + dot(second, second_ref[...])
+    picked = (picked + absent_of(first, second)).astype(BF16)
+    stay_ref[...] = picked[0:LATE_ROWS]
+    leave_ref[...] = picked[LATE_ROWS:]
+
+
+def late_rows(place, att_own, att_a, att_b, mine, theirs, norm_gain, picks):
     rows, half = att_own.shape
     wide, last = att_a.shape[1], att_b.shape[1]
     all_rows = picks.shape[0]
     whole = lambda i, t: (0, 0)
     return pl.pallas_call(
-        norm_kernel,
+        late_kernel,
         grid_spec=pltpu.PrefetchScalarGridSpec(
             num_scalar_prefetch=1,
             grid=(1,),
@@ -421,19 +421,51 @@
                 pl.BlockSpec((all_rows, rows), lambda i, t: (0, t[0])),
                 pl.BlockSpec((all_rows, rows), lambda i, t: (0, 1 - t[0])),
             ],
-            out_specs=[
-                pl.BlockSpec((2 * rows, half), whole),
-                pl.BlockSpec((LATE_ROWS, half), whole),
-                pl.BlockSpec((LATE_ROWS, half), whole),
-            ],
-        ),
-        out_shape=[
-            jax.ShapeDtypeStruct((2 * rows, half), BF16),
-            jax.ShapeDtypeStruct((LATE_ROWS, half), BF16),
-            jax.ShapeDtypeStruct((LATE_ROWS, half), BF16),
-        ],
-        name="normalize",
+            out_specs=[pl.BlockSpec((LATE_ROWS, half), whole)] * 2,
+            scratch_shapes=[pltpu.VMEM((rows, half), BF16)] * 2,
+        ),
+        out_shape=[jax.ShapeDtypeStruct((LATE_ROWS, half), BF16)] * 2,
+        name="late_rows",
     )(place, att_own, att_a, att_b, mine, theirs, norm_gain, picks, picks)
+
+
+def harvest_kernel(place, own_ref, pa_ref, pb_ref, mine_ref, theirs_ref, gain_ref, out_ref):
+    wide = pa_ref.shape[1]
+    gain = gain_ref[...]
+
+    @pl.when(pl.program_id(0) == place[0])
+    def _():
+        scale = row_scale(mine_ref[8:16, :], theirs_ref[0:8, :])
+        out_ref[...] = (own_ref[...] * scale * gain).astype(BF16)
+
+    @pl.when(pl.program_id(0) != place[0])
+    def _():
+        scale = row_scale(mine_ref[0:8, :], theirs_ref[8:16, :])
+        out_ref[:, 0:wide] = (pa_ref[...] * scale * gain[:, 0:wide]).astype(BF16)
+        out_ref[:, wide:] = (pb_ref[...] * scale * gain[:, wide:]).astype(BF16)
+
+
+def harvest_rows(place, att_own, att_a, att_b, mine, theirs, norm_gain):
+    rows, half = att_own.shape
+    whole = lambda i, t: (0, 0)
+    return pl.pallas_call(
+        harvest_kernel,
+        grid_spec=pltpu.PrefetchScalarGridSpec(
+            num_scalar_prefetch=1,
+            grid=(2,),
+            in_specs=[
+                pl.BlockSpec(att_own.shape, whole),
+                pl.BlockSpec(att_a.shape, whole),
+                pl.BlockSpec(att_b.shape, whole),
+                pl.BlockSpec((16, rows), whole),
+                pl.BlockSpec((16, rows), whole),
+                pl.BlockSpec((1, half), lambda i, t: (0, t[0])),
+            ],
+            out_specs=pl.BlockSpec((rows, half), lambda i, t: (i, 0)),
+        ),
+        out_shape=jax.ShapeDtypeStruct((2 * rows, half), BF16),
+        name="harvest_rows",
+    )(place, att_own, att_a, att_b, mine, theirs, norm_gain)
 
 
 def picks_kernel(col_ref, row_ref, key_ref, out_ref):
@@ -460,37 +492,74 @@
     )(labels.reshape(tokens, 1), labels.reshape(1, tokens), keys)
 
 
+def present_of(rows):
+    return rows[:, 0:1].astype(F32) < 0.5 * ABSENT
+
+
+def scale_kernel(place, *refs):
+    own_refs, other_refs = refs[0:PAIRS], refs[PAIRS : 2 * PAIRS]
+    gain_ref, other_gain_ref, own_out, other_out, flag_ref = refs[2 * PAIRS :]
+    for piece in range(PAIRS):
+        at = slice(piece * SPAN, (piece + 1) * SPAN)
+        present = present_of(own_refs[piece])
+        rows = jnp.where(present, own_refs[piece][...].astype(F32), 0.0)
+        other = jnp.where(present, other_refs[piece][...].astype(F32), 0.0)
+        squares = jnp.sum(rows * rows + other * other, axis=-1, keepdims=True)
+        scale = lax.rsqrt(squares * (1.0 / D) + EPSILON)
+        own_out[at, :] = (rows * scale * gain_ref[...]).astype(BF16)
+        other_out[at, :] = (other * scale * other_gain_ref[...]).astype(BF16)
+        flag_ref[at, :] = jnp.broadcast_to(jnp.where(present, 1.0, 0.0), (SPAN, HD))
+
+
+def scale_early(place, own, other, norm_gain):
+    half = own[0].shape[1]
+    whole = lambda i, t: (0, 0)
+    return pl.pallas_call(
+        scale_kernel,
+        grid_spec=pltpu.PrefetchScalarGridSpec(
+            num_scalar_prefetch=1,
+            grid=(1,),
+            in_specs=[pl.BlockSpec((SPAN, half), whole)] * (2 * PAIRS)
+            + [
+                pl.BlockSpec((1, half), lambda i, t: (0, t[0])),
+                pl.BlockSpec((1, half), lambda i, t: (0, 1 - t[0])),
+            ],
+            out_specs=[pl.BlockSpec((EARLY_ROWS, half), whole)] * 2
+            + [pl.BlockSpec((EARLY_ROWS, HD), whole)],
+        ),
+        out_shape=[jax.ShapeDtypeStruct((EARLY_ROWS, half), BF16)] * 2
+        + [jax.ShapeDtypeStruct((EARLY_ROWS, HD), F32)],
+        name="scale_early",
+    )(place, *own, *other, norm_gain, norm_gain)
+
+
+def tdot(left, right):
+    return lax.dot_general(left, right, (((0,), (0,)), ((), ())), preferred_element_type=F32)
+
+
 def gram_own_kernel(place, *refs):
-    own_refs, across_refs = refs[0:PIECES], refs[PIECES : PIECES + 2]
-    gain_ref, out_ref, turned_ref, extra_ref, rows_ref = refs[PIECES + 2 :]
+    early_ref, early_flag_ref = refs[0:2]
+    late_refs = refs[2 : 2 + len(LATE)]
+    out_ref, rows_ref, flag_ref = refs[2 + len(LATE) :]
     step = out_ref.shape[0]
 
     @pl.when(pl.program_id(0) == 0)
     def _():
-        lane = lax.broadcasted_iota(jnp.int32, (SPAN, HD), 1)
-        for piece in range(PIECES):
-            at = slice(piece * SPAN, (piece + 1) * SPAN)
-            present = own_refs[piece][:, 0:1].astype(F32) < 0.5 * ABSENT
-            rows = jnp.where(present, own_refs[piece][...].astype(F32), 0.0)
-            if piece < 2:
-                other = jnp.where(present, across_refs[piece][...].astype(F32), 0.0)
-                squares = jnp.sum(rows * rows + other * other, axis=-1, keepdims=True)
-                scale = lax.rsqrt(squares * (1.0 / D) + EPSILON)
-                rows = rows * scale * gain_ref[...]
-            else:
-                scale = jnp.ones((SPAN, 1), F32)
-            rows_ref[at, :] = rows.astype(BF16)
-            flag = jnp.where(present, 1.0, 0.0)
-            extra_ref[at, :] = jnp.where(lane == 0, scale, jnp.where(lane == 1, flag, 0.0))
-        turned_ref[...] = jnp.transpose(rows_ref[...])
-
-    count = jnp.sum(extra_ref[:, 1:2])
-    left = turned_ref[pl.ds(pl.multiple_of(pl.program_id(0) * step, step), step), :]
-    out_ref[...] = (dot(left, rows_ref[...]) * (1.0 / count)).astype(BF16)
-
-
-def gram_own(place, pieces, across_pieces, norm_gain):
-    half = pieces[0].shape[1]
+        rows_ref[0:EARLY_ROWS, :] = early_ref[...]
+        flag_ref[0:EARLY_ROWS, :] = early_flag_ref[...]
+        for piece in range(len(LATE)):
+            at = slice(EARLY_ROWS + piece * SPAN, EARLY_ROWS + (piece + 1) * SPAN)
+            present = present_of(late_refs[piece])
+            rows_ref[at, :] = jnp.where(present, late_refs[piece][...].astype(F32), 0.0).astype(BF16)
+            flag_ref[at, :] = jnp.broadcast_to(jnp.where(present, 1.0, 0.0), (SPAN, HD))
+
+    count = jnp.sum(flag_ref[:, 0:1])
+    left = rows_ref[:, pl.ds(pl.multiple_of(pl.program_id(0) * step, step), step)]
+    out_ref[...] = (tdot(left, rows_ref[...]) * (1.0 / count)).astype(BF16)
+
+
+def gram_own(place, early, early_flags, late):
+    half = early.shape[1]
     total = PIECES * SPAN
     step = 512
     whole = lambda i, t: (0, 0)
@@ -499,43 +568,45 @@
         grid_spec=pltpu.PrefetchScalarGridSpec(
             num_scalar_prefetch=1,
             grid=(half // step,),
-            in_specs=[pl.BlockSpec((SPAN, half), whole)] * (PIECES + 2)
-            + [pl.BlockSpec((1, half), lambda i, t: (0, t[0]))],
+            in_specs=[
+                pl.BlockSpec((EARLY_ROWS, half), whole),
+                pl.BlockSpec((EARLY_ROWS, HD), whole),
+            ]
+            + [pl.BlockSpec((SPAN, half), whole)] * len(LATE),
             out_specs=[
                 pl.BlockSpec((step, half), lambda i, t: (i, t[0])),
-                pl.BlockSpec((half, total), whole),
+                pl.BlockSpec((total, half), whole),
                 pl.BlockSpec((total, HD), whole),
             ],
-            scratch_shapes=[pltpu.VMEM((total, half), BF16)],
         ),
         out_shape=[
             jax.ShapeDtypeStruct((half, 2 * half), BF16),
-            jax.ShapeDtypeStruct((half, total), BF16),
+            jax.ShapeDtypeStruct((total, half), BF16),
             jax.ShapeDtypeStruct((total, HD), F32),
         ],
         name="gram_own",
-    )(place, *pieces, *across_pieces, norm_gain)
+    )(place, early, early_flags, *late)
 
 
 def gram_other_kernel(place, *refs):
-    other_refs = refs[0:PIECES]
-    gain_ref, turned_ref, extra_ref, _, out_ref, rows_ref = refs[PIECES:]
+    early_ref = refs[0]
+    late_refs = refs[1 : 1 + len(LATE)]
+    left_ref, flag_ref, _, out_ref, rows_ref = refs[1 + len(LATE) :]
 
     @pl.when(pl.program_id(0) == 0)
     def _():
-        for piece in range(PIECES):
-            at = slice(piece * SPAN, (piece + 1) * SPAN)
-            rows = other_refs[piece][...].astype(F32)
-            if piece < 2:
-                rows = rows * extra_ref[at, 0:1] * gain_ref[...]
-            rows_ref[at, :] = jnp.where(extra_ref[at, 1:2] > 0.5, rows, 0.0).astype(BF16)
-
-    count = jnp.sum(extra_ref[:, 1:2])
-    out_ref[...] = (dot(turned_ref[...], rows_ref[...]) * (1.0 / count)).astype(BF16)
-
-
-def gram_other(place, pieces, norm_gain, turned, extra, partial):
-    half = pieces[0].shape[1]
+        rows_ref[0:EARLY_ROWS, :] = early_ref[...]
+        for piece in range(len(LATE)):
+            at = slice(EARLY_ROWS + piece * SPAN, EARLY_ROWS + (piece + 1) * SPAN)
+            present = flag_ref[at, 0:1] > 0.5
+            rows_ref[at, :] = jnp.where(present, late_refs[piece][...].astype(F32), 0.0).astype(BF16)
+
+    count = jnp.sum(flag_ref[:, 0:1])
+    out_ref[...] = (tdot(left_ref[...], rows_ref[...]) * (1.0 / count)).astype(BF16)
+
+
+def gram_other(place, early, late, rows, flags, partial):
+    half = early.shape[1]
     total = PIECES * SPAN
     step = 512
     whole = lambda i, t: (0, 0)
@@ -544,10 +615,10 @@
         grid_spec=pltpu.PrefetchScalarGridSpec(
             num_scalar_prefetch=1,
             grid=(half // step,),
-            in_specs=[pl.BlockSpec((SPAN, half), whole)] * PIECES
+            in_specs=[pl.BlockSpec((EARLY_ROWS, half), whole)]
+            + [pl.BlockSpec((SPAN, half), whole)] * len(LATE)
             + [
-                pl.BlockSpec((1, half), lambda i, t: (0, 1 - t[0])),
-                pl.BlockSpec((step, total), lambda i, t: (i, 0)),
+                pl.BlockSpec((total, step), lambda i, t: (0, i)),
                 pl.BlockSpec((total, HD), whole),
                 pl.BlockSpec(memory_space=pl.ANY),
             ],
@@ -555,9 +626,9 @@
             scratch_shapes=[pltpu.VMEM((total, half), BF16)],
         ),
         out_shape=jax.ShapeDtypeStruct((half, 2 * half), BF16),
-        input_output_aliases={PIECES + 4: 0},
+        input_output_aliases={len(LATE) + 4: 0},
         name="gram_other",
-    )(place, *pieces, norm_gain, turned, extra, partial)
+    )(place, early, *late, rows, flags, partial)
 
 
 def after(value, *earlier):
@@ -604,37 +675,55 @@
     att_b, mine, *early = attend_partner_b(
         place, query_b, partner_kv, key_rows, value_rows, sq_own, sq_a, picks, early_a
     )
-    first = [hop(rows, j, f"far_e{j}") for rows, j in zip(early, EARLY)]
-    sums = after(across(mine, "x_sums"), first[0])
-    harvest, stay, leave = normalize(place, att_own, att_a, att_b, mine, sums, gain, picks)
-    came = hop(after(leave, first[1]), 1, "core")
+    early = dict(zip(EARLY, early))
+    came, own, other, crossed = {0: early[0]}, {}, {}, []
+
+    def send_early(j, *earlier):
+        came[j] = hop(after(early[j], *earlier), j, f"far_e{j}")
+
+    def send_late(j, *earlier):
+        own[j] = hop(after(joined[j], *earlier), j, f"far_{j}")
+
+    def cross(j, *earlier):
+        other[j] = across(after(own[j], *earlier, *crossed[-2:-1]), f"x_{j}")
+        crossed.append(other[j])
+
+    for j in (8, 12, 1, 2):
+        send_early(j)
+    sums = across(mine, "x_sums")
+    send_early(3, came[2])
+    send_early(9, came[1])
+    own[0] = jnp.concatenate([came[0], came[1]])
+    cross(0)
+    ready = after(sums, came[1], came[2])
+    stay, leave = late_rows(place, att_own, att_a, att_b, mine, ready, gain, picks)
+    send_early(13, leave)
+    swapped = hop(after(leave, came[3], came[8], other[0]), 1, "far_core")
     shape = (len(LATE), ROWS, D // 2)
-    joined = jnp.concatenate([stay.reshape(shape), came.reshape(shape)], 1)
+    joined = jnp.concatenate([stay.reshape(shape), swapped.reshape(shape)], 1)
     joined = {j: joined[index] for index, j in enumerate(LATE)}
-    own, other = {0: joined[0]}, {}
-    pairs = [jnp.concatenate(first[0:2]), jnp.concatenate(first[2:4])]
-
-    def far(j, *earlier):
-        own[j] = hop(after(joined[j], *earlier), j, f"far_{j}")
-
-    x_e0 = across(pairs[0], "x_e0")
-    other[0] = across(own[0], "x_0")
-    far(10, first[0])
-    far(2, first[1])
-    x_e1 = across(after(pairs[1], x_e0), "x_e1")
-    far(14, first[2], x_e0)
-    other[2] = across(after(own[2], other[0]), "x_2")
-    far(4, own[2], other[0])
-    other[10] = across(after(own[10], x_e1), "x_10")
-    far(6, own[10], x_e1)
-    other[4] = across(after(own[4], other[2]), "x_4")
-    other[6] = across(after(own[6], other[10]), "x_6")
-    other[14] = across(after(own[14], other[4]), "x_14")
-    partial, turned, extra = gram_own(
-        place, [*pairs, *[own[j] for j in LATE]], [x_e0, x_e1], gain
-    )
+    own[2] = jnp.concatenate([came[2], came[3]])
+    cross(2)
+    send_late(10, came[12])
+    own[8] = jnp.concatenate([came[8], came[9]])
+    cross(8)
+    send_late(14, came[9], other[2])
+    send_late(4, came[13], other[2])
+    own[12] = jnp.concatenate([came[12], came[13]])
+    cross(12)
+    send_late(6, own[4], other[8])
+    cross(4)
+    harvest = harvest_rows(place, att_own, att_a, att_b, mine, ready, gain)
+    cross(10, harvest)
+    cross(6)
+    pairs = EARLY[0::2]
+    own_early, other_early, early_flags = scale_early(
+        place, [own[j] for j in pairs], [other[j] for j in pairs], gain
+    )
+    cross(14, own_early)
+    partial, rows, flags = gram_own(place, own_early, early_flags, [own[j] for j in LATE])
     gram = gram_other(
-        place, [x_e0, x_e1, *[other[j] for j in LATE]], gain, turned, extra, partial
+        place, other_early, [other[j] for j in LATE], rows, flags, partial
     )
     return gram[None], harvest
 

time: 117 us -> 113 us (0.966)
  the two profiles are of different devices: /device:TPU:8 before, /device:TPU:0 now
where the time goes in v3:
time: 113 us; the launch traced here: 112 us
  Pallas kernels  44.9 us (40%)
  starting transfers between devices  34.1 us (30%)
  waiting for transfers between devices  21.2 us (19%)
  local copies, waits for them, and re-layouts  9.81 us (9%)
  other arithmetic  1.21 us (1%)
    ppermute x12, starting transfers between devices, hop(): lax.ppermute(value, 'dp', [(i, i ^ offset) for i in range(group_count)])  19.1 us
    ppermute x12, starting transfers between devices, across(): return lax.ppermute(value, 'tensor', swap)  15 us
    ppermute x12, waiting for transfers between devices, across(): return lax.ppermute(value, 'tensor', swap)  12.1 us
    ppermute x12, waiting for transfers between devices, hop(): lax.ppermute(value, 'dp', [(i, i ^ offset) for i in range(group_count)])  9.09 us
    pallas_call x1, Pallas kernels, gram_other(): pl.pallas_call(gram_other_kernel, grid_spec=pltpu.PrefetchScalarGridSpec(...  8.38 us
    pallas_call x1, Pallas kernels, gram_own(): pl.pallas_call(gram_own_kernel, grid_spec=pltpu.PrefetchScalarGridSpec(nu...  8.28 us
    pallas_call x1, Pallas kernels, attend_partner_a(): pl.pallas_call(partner_a_kernel, grid_spec=pltpu.PrefetchScalarGridSpec(n...  5.83 us
    pallas_call x1, Pallas kernels, late_rows(): pl.pallas_call(late_kernel, grid_spec=pltpu.PrefetchScalarGridSpec(num_sc...  4.31 us
  transfers between devices with their start and end apart: 24, of which 7 were waited for; matrix products, arithmetic and copies ran while one was open for 6% of the time, Pallas kernels for 29%

profile of v3, /device:TPU:0, one launch (start us, length us, event | category | flops | bytes accessed | tf_op | source)
XLA Modules:
  0.0 112.3 jit_solution(4978203802127488706)
XLA Ops:
  0.6 0.0 copy-start
  0.6 0.0 copy-start.24
  0.7 0.0 copy-start.21
  0.7 1.0 constant_dynamic-slice_fusion.1
  1.7 3.0 %collective-permute-start = (bf16[256,512]{1,0:T(8,128)(2,1)S(1)}, bf16[256,512]{1,0:T(8,128)(2,1)S(1)}, u32[]{:S(2)}, u32[]{:S(2)}) collective-permute-start(bf16[256,512]{1,0:T(8,128)(2,1)S(1)} %pad_maximum_fusion), channel_id=1, source_target_pairs={{0,1},{1,0},{2,3},{3,2},{4,5},{5,4},{6,7},{7,6},{8,9},{9,8},{10,11... | collective-permute-start | bytes 786440 | tf_op jit(solution)/shard_map/x_kv/ppermute | solution.py:647
  4.7 1.2 %constant_dynamic-slice_fusion = bf16[256,1536]{1,0:T(8,128)(2,1)S(1)} fusion(bf16[256,4096]{1,0:T(8,128)(2,1)} %q_ref.1, s32[]{:T(128)S(6)} %select_n.25), kind=kLoop, calls=%fused_computation.31 | loop fusion | bytes 1572868 | tf_op jit(solution)/shard_map/dynamic_slice | solution.py:661
  5.9 0.1 collective-permute-start.2
  6.1 0.7 gather_fusion
  6.7 0.1 copy.12
  6.8 0.6 gather_fusion.1
  7.4 1.0 constant_dynamic-slice_fusion.3
  8.4 3.5 %collective-permute-done.kp_ref.vp_ref.kd.vd = bf16[256,512]{1,0:T(8,128)(2,1)S(1)} collective-permute-done((bf16[256,512]{1,0:T(8,128)(2,1)S(1)}, bf16[256,512]{1,0:T(8,128)(2,1)S(1)}, u32[]{:S(2)}, u32[]{:S(2)}) %collective-permute-start) | collective-permute-done | bytes 262176 | tf_op jit(solution)/shard_map/x_kv/ppermute | solution.py:647
  11.9 2.0 %collective-permute-start.1 = (bf16[256,512]{1,0:T(8,128)(2,1)S(1)}, bf16[256,512]{1,0:T(8,128)(2,1)S(1)}, u32[]{:S(2)}, u32[]{:S(2)}) collective-permute-start(bf16[256,512]{1,0:T(8,128)(2,1)S(1)} %constant_dynamic-slice_fusion.3), channel_id=1, source_target_pairs={{0,1},{1,0},{2,3},{3,2},{4,5},{5,4},{6,7},{7,6},{8,9},{9,8},{10,11... | collective-permute-start | bytes 786440 | tf_op jit(solution)/shard_map/x_qb/ppermute | solution.py:647
  13.9 0.1 iota_add_fusion
  14.0 0.8 add.61.key_ref
  14.8 0.9 copy.13.col_ref
  15.7 2.0 %class_picks.1.so_ref.sp_ref = bf16[384,512]{1,0:T(8,128)(2,1)} custom-call(s32[512,1]{1,0:T(8,128)} %copy.13.col_ref, s32[1,512]{1,0:T(1,128)} %bitcast.26, s32[384,1]{1,0:T(8,128)} %add.61.key_ref), custom_call_target="tpu_custom_call" | custom-call | tf_op jit(solution)/shard_map/class_picks/pallas_call | solution.py:486
  17.7 4.1 %attend_own.1 = (f32[256,2048]{1,0:T(8,128)}, f32[2,256,128]{2,1,0:T(8,128)}) custom-call(s32[1]{0:T(128)} %bitcast.place, bf16[256,4096]{1,0:T(8,128)(2,1)} %q_ref.1, bf16[256,512]{1,0:T(8,128)(2,1)} %ko.3, bf16[256,512]{1,0:T(8,128)(2,1)} %vo.3, bf16[256,512]{1,0:T(8,128)(2,1)} %copy-done.1, bf16[256,512]{1,0:T(8,128)(2,1)} %copy-done.1), custom_call_target="tpu_custom_call" | custom-call | tf_op jit(solution)/shard_map/attend_own/pallas_call | solution.py:220
  21.8 7.0 %collective-permute-done.2.q_ref = bf16[256,1536]{1,0:T(8,128)(2,1)S(1)} collective-permute-done((bf16[256,1536]{1,0:T(8,128)(2,1)S(1)}, bf16[256,1536]{1,0:T(8,128)(2,1)S(1)}, u32[]{:S(2)}, u32[]{:S(2)}) %collective-permute-start.2) | collective-permute-done | bytes 786464 | tf_op jit(solution)/shard_map/x_qa/ppermute | solution.py:647
  28.8 0.9 copy-done.2
  29.6 5.8 %attend_partner_a.1 = (f32[256,1536]{1,0:T(8,128)}, f32[256,128]{1,0:T(8,128)}, bf16[192,2048]{1,0:T(8,128)(2,1)}) custom-call(s32[1]{0:T(128)} %bitcast.place, bf16[256,1536]{1,0:T(8,128)(2,1)} %copy-done.2, bf16[256,512]{1,0:T(8,128)(2,1)} %copy-done.1, bf16[256,512]{1,0:T(8,128)(2,1)} %copy-done.1, bf16[256,512]{1,0:T(8,128)(2,1)} %ko.3, ...), custom_call_target="tpu_custom_call" | custom-call | tf_op jit(solution)/shard_map/attend_partner_a/pallas_call | solution.py:278
  35.5 0.0 collective-permute-done.1.q_ref
  35.5 0.7 copy-done.7
  36.2 4.1 %attend_partner_b.1 = (f32[256,512]{1,0:T(8,128)}, f32[16,256]{1,0:T(8,128)}, bf16[24,2048]{1,0:T(8,128)(2,1)}, bf16[24,2048]{1,0:T(8,128)(2,1)}, bf16[24,2048]{...) custom-call(s32[1]{0:T(128)} %bitcast.place, ...), custom_call_target="tpu_custom_call" | custom-call | tf_op jit(solution)/shard_map/attend_partner_b/pallas_call | solution.py:343
  40.2 0.1 collective-permute-start.3
  40.3 2.1 %collective-permute-start.4 = (bf16[24,2048]{1,0:T(8,128)(2,1)}, bf16[24,2048]{1,0:T(8,128)(2,1)S(1)}, u32[]{:S(2)}, u32[]{:S(2)}) collective-permute-start(bf16[24,2048]{1,0:T(8,128)(2,1)} %get-tuple-element.48), channel_id=1, source_target_pairs={{0,4},{2,6},{4,0},{6,2},{8,12},{10,14},{12,8},{14,10},{16,20},{18,... | collective-permute-start | bytes 294920 | tf_op jit(solution)/shard_map/far_e2/ppermute | solution.py:651
  42.4 0.9 constant_dynamic-update-slice_fusion.1
  43.3 0.1 collective-permute-start.9
  43.4 2.6 %collective-permute-start.6 = (bf16[24,2048]{1,0:T(8,128)(2,1)}, bf16[24,2048]{1,0:T(8,128)(2,1)S(1)}, u32[]{:S(2)}, u32[]{:S(2)}) collective-permute-start(bf16[24,2048]{1,0:T(8,128)(2,1)} %get-tuple-element.51), channel_id=1, source_target_pairs={{0,16},{2,18},{4,20},{6,22},{8,24},{10,26},{12,28},{14,30},{16,0},... | collective-permute-start | bytes 294920 | tf_op jit(solution)/shard_map/far_e8/ppermute | solution.py:651
  46.0 1.3 %collective-permute-start.8 = (bf16[24,2048]{1,0:T(8,128)(2,1)}, bf16[24,2048]{1,0:T(8,128)(2,1)S(1)}, u32[]{:S(2)}, u32[]{:S(2)}) collective-permute-start(bf16[24,2048]{1,0:T(8,128)(2,1)} %get-tuple-element.54), channel_id=1, source_target_pairs={{0,24},{2,26},{4,28},{6,30},{8,16},{10,18},{12,20},{14,22},{16,8},... | collective-permute-start | bytes 294920 | tf_op jit(solution)/shard_map/far_e12/ppermute | solution.py:651
  47.3 0.0 collective-permute-done.3
  47.3 0.9 collective-permute-start.7
  48.2 0.0 collective-permute-done.4
  48.2 1.0 collective-permute-start.5
  49.3 2.0 %collective-permute-start.11 = (bf16[48,2048]{1,0:T(8,128)(2,1)S(1)}, bf16[48,2048]{1,0:T(8,128)(2,1)S(1)}, u32[]{:S(2)}, u32[]{:S(2)}) collective-permute-start(bf16[48,2048]{1,0:T(8,128)(2,1)S(1)} %constant_dynamic-update-slice_fusion.refs_0_), channel_id=1, source_target_pairs={{0,1},{1,0},{2,3},{3,2},{4,5},{5,4},{6,7},{7,6},{8,9},{9,8},{10,11... | collective-permute-start | bytes 589832 | tf_op jit(solution)/shard_map/x_0/ppermute | solution.py:647
  51.3 4.3 %late_rows.1 = (bf16[96,2048]{1,0:T(8,128)(2,1)}, bf16[96,2048]{1,0:T(8,128)(2,1)}) custom-call(s32[1]{0:T(128)} %bitcast.place, f32[256,2048]{1,0:T(8,128)} %get-tuple-element.43.own_ref, f32[256,1536]{1,0:T(8,128)} %get-tuple-element.56.pa_ref, f32[256,512]{1,0:T(8,128)} %get-tuple-element.57.pb_ref, f32[16,256]{1,0:T(8,128)} %get-tuple-element.58.mine_ref, ...), custom_call_target="tpu_custom_call" | custom-call | tf_op jit(solution)/shard_map/late_rows/pallas_call | solution.py:409
  55.7 0.6 collective-permute-start.10
  56.3 0.2 collective-permute-done.6
  56.5 0.0 collective-permute-done.5
  56.5 0.0 collective-permute-done.11.refs_4_
  56.5 0.3 collective-permute-start.15
  56.9 1.7 %collective-permute-start.12 = (bf16[48,2048]{1,0:T(8,128)(2,1)S(1)}, bf16[48,2048]{1,0:T(8,128)(2,1)S(1)}, u32[]{:S(2)}, u32[]{:S(2)}) collective-permute-start(bf16[48,2048]{1,0:T(8,128)(2,1)S(1)} %constant_dynamic-update-slice_fusion.2.refs_1_), channel_id=1, source_target_pairs={{0,1},{1,0},{2,3},{3,2},{4,5},{5,4},{6,7},{7,6},{8,9},{9,8},{10,11... | collective-permute-start | bytes 589832 | tf_op jit(solution)/shard_map/x_2/ppermute | solution.py:647
  58.6 0.5 collective-permute-done.7
  59.1 1.6 %collective-permute-start.13 = (bf16[48,2048]{1,0:T(8,128)(2,1)S(1)}, bf16[48,2048]{1,0:T(8,128)(2,1)S(1)}, u32[]{:S(2)}, u32[]{:S(2)}) collective-permute-start(bf16[48,2048]{1,0:T(8,128)(2,1)S(1)} %constant_dynamic-update-slice_fusion.4.refs_2_), channel_id=1, source_target_pairs={{0,1},{1,0},{2,3},{3,2},{4,5},{5,4},{6,7},{7,6},{8,9},{9,8},{10,11... | collective-permute-start | bytes 589832 | tf_op jit(solution)/shard_map/x_8/ppermute | solution.py:647
  60.6 0.0 collective-permute-done.15
  60.7 1.1 fusion.6
  61.7 0.8 collective-permute-done.10
  62.5 1.6 %collective-permute-done.12.refs_5_ = bf16[48,2048]{1,0:T(8,128)(2,1)S(1)} collective-permute-done((bf16[48,2048]{1,0:T(8,128)(2,1)S(1)}, bf16[48,2048]{1,0:T(8,128)(2,1)S(1)}, u32[]{:S(2)}, u32[]{:S(2)}) %collective-permute-start.12) | collective-permute-done | bytes 196640 | tf_op jit(solution)/shard_map/x_2/ppermute | solution.py:647
  64.1 6.8 %collective-permute-start.16 = (bf16[48,2048]{1,0:T(8,128)(2,1)S(1)}, bf16[48,2048]{1,0:T(8,128)(2,1)S(1)}, u32[]{:S(2)}, u32[]{:S(2)}) collective-permute-start(bf16[48,2048]{1,0:T(8,128)(2,1)S(1)} %get-tuple-element.67), channel_id=1, source_target_pairs={{0,8},{2,10},{4,12},{6,14},{8,0},{10,2},{12,4},{14,6},{16,24},{18,... | collective-permute-start | bytes 589832 | tf_op jit(solution)/shard_map/far_4/ppermute | solution.py:651
  70.9 2.1 %collective-permute-start.14 = (bf16[48,2048]{1,0:T(8,128)(2,1)S(1)}, bf16[48,2048]{1,0:T(8,128)(2,1)S(1)}, u32[]{:S(2)}, u32[]{:S(2)}) collective-permute-start(bf16[48,2048]{1,0:T(8,128)(2,1)S(1)} %constant_dynamic-update-slice_fusion.6.refs_3_), channel_id=1, source_target_pairs={{0,1},{1,0},{2,3},{3,2},{4,5},{5,4},{6,7},{7,6},{8,9},{9,8},{10,11... | collective-permute-start | bytes 589832 | tf_op jit(solution)/shard_map/x_12/ppermute | solution.py:647
  73.0 4.3 %harvest_rows.1 = bf16[512,2048]{1,0:T(8,128)(2,1)} custom-call(s32[1]{0:T(128)} %bitcast.place, f32[256,2048]{1,0:T(8,128)} %get-tuple-element.43.own_ref, f32[256,1536]{1,0:T(8,128)} %get-tuple-element.56.pa_ref, f32[256,512]{1,0:T(8,128)} %get-tuple-element.57.pb_ref, f32[16,256]{1,0:T(8,128)} %get-tuple-element.58.mine_ref, f32[16,256]{1,0:T(8,128)} %copy-done.20, ...), custom_call_target="tpu_custom_call" | custom-call | tf_op jit(solution)/shard_map/harvest_rows/pallas_call | solution.py:451
  77.3 3.3 %collective-permute-start.22 = (bf16[48,2048]{1,0:T(8,128)(2,1)S(1)}, bf16[48,2048]{1,0:T(8,128)(2,1)S(1)}, u32[]{:S(2)}, u32[]{:S(2)}) collective-permute-start(bf16[48,2048]{1,0:T(8,128)(2,1)S(1)} %get-tuple-element.73), channel_id=1, source_target_pairs={{0,28},{2,30},{4,24},{6,26},{8,20},{10,22},{12,16},{14,18},{16,12}... | collective-permute-start | bytes 589832 | tf_op jit(solution)/shard_map/far_14/ppermute | solution.py:651
  80.7 0.1 collective-permute-start.17
  80.8 0.0 collective-permute-start.18
  80.8 0.0 collective-permute-done.14.refs_7_
  80.9 7.6 %collective-permute-done.20.refs_4_ = bf16[48,2048]{1,0:T(8,128)(2,1)S(1)} collective-permute-done((bf16[48,2048]{1,0:T(8,128)(2,1)S(1)}, bf16[48,2048]{1,0:T(8,128)(2,1)S(1)}, u32[]{:S(2)}, u32[]{:S(2)}) %collective-permute-start.20) | collective-permute-done | bytes 196640 | tf_op jit(solution)/shard_map/far_10/ppermute | solution.py:651
  88.5 3.6 %scale_early.1 = (bf16[192,2048]{1,0:T(8,128)(2,1)}, bf16[192,2048]{1,0:T(8,128)(2,1)}, f32[192,128]{1,0:T(8,128)}) custom-call(s32[1]{0:T(128)} %bitcast.place, bf16[48,2048]{1,0:T(8,128)(2,1)} %copy-done.5, bf16[48,2048]{1,0:T(8,128)(2,1)} %copy-done.4, bf16[48,2048]{1,0:T(8,128)(2,1)} %copy-done.6, bf16[48,2048]{1,0:T(8,128)(2,1)} %copy-done.3, ...), custom_call_target="tpu_custom_call" | custom-call | tf_op jit(solution)/shard_map/scale_early/pallas_call | solution.py:517
  92.1 2.0 %collective-permute-start.19 = (bf16[48,2048]{1,0:T(8,128)(2,1)S(1)}, bf16[48,2048]{1,0:T(8,128)(2,1)S(1)}, u32[]{:S(2)}, u32[]{:S(2)}) collective-permute-start(bf16[48,2048]{1,0:T(8,128)(2,1)S(1)} %collective-permute-done.18.refs_3_), channel_id=1, source_target_pairs={{0,1},{1,0},{2,3},{3,2},{4,5},{5,4},{6,7},{7,6},{8,9},{9,8},{10,11... | collective-permute-start | bytes 589832 | tf_op jit(solution)/shard_map/x_6/ppermute | solution.py:647
  94.2 0.3 collective-permute-start.23
  94.5 0.4 copy-done.14
  94.8 8.3 %gram_own.1 = (bf16[2048,4096]{1,0:T(8,128)(2,1)}, bf16[384,2048]{1,0:T(8,128)(2,1)}, f32[384,128]{1,0:T(8,128)}) custom-call(s32[1]{0:T(128)} %bitcast.place, bf16[192,2048]{1,0:T(8,128)(2,1)} %get-tuple-element.74.refs_0_, f32[192,128]{1,0:T(8,128)} %get-tuple-element.76.refs_1_, bf16[48,2048]{1,0:T(8,128)(2,1)} %copy-done.12, ...), custom_call_target="tpu_custom_call" | custom-call | tf_op jit(solution)/shard_map/gram_own/pallas_call | solution.py:566
  103.2 0.6 copy-done.10
  103.8 0.1 copy-done.11
  103.9 8.4 %gram_other.1 = bf16[2048,4096]{1,0:T(8,128)(2,1)} custom-call(s32[1]{0:T(128)} %bitcast.place, bf16[192,2048]{1,0:T(8,128)(2,1)} %get-tuple-element.64.refs_0_, bf16[48,2048]{1,0:T(8,128)(2,1)} %copy-done.8, bf16[48,2048]{1,0:T(8,128)(2,1)} %copy-done.10, bf16[48,2048]{1,0:T(8,128)(2,1)} %copy-done.9, ...), custom_call_target="tpu_custom_call", output_to_operand_aliasing={{}: (8, {})} | custom-call | tf_op jit(solution)/shard_map/gram_other/pallas_call | solution.py:613
  (67 shorter events, 0.2 us)
Async XLA Ops:
  0.6 5.4 %copy-start = (s32[16]{0:T(128)S(1)}, s32[16]{0:T(128)}, u32[]{:S(2)}) copy-start(s32[16]{0:T(128)} %param.14) | copy-start | bytes 196
  0.6 5.4 %copy-start.24 = (s32[16]{0:T(128)S(1)}, s32[16]{0:T(128)}, u32[]{:S(2)}) copy-start(s32[16]{0:T(128)} %constant.30.clone) | copy-start | bytes 196
  0.7 6.1 %copy-start.22 = (s32[16,2]{0,1:T(2,128)S(1)}, s32[16,2]{0,1:T(2,128)}, u32[]{:S(2)}) copy-start(s32[16,2]{0,1:T(2,128)} %param.13) | copy-start | bytes 388
  0.7 14.2 %copy-start.21 = (s32[512]{0:T(512)S(1)}, s32[512]{0:T(512)}, u32[]{:S(2)}) copy-start(s32[512]{0:T(512)} %param.12) | copy-start | bytes 6148
  1.7 10.2 %collective-permute-start = (bf16[256,512]{1,0:T(8,128)(2,1)S(1)}, bf16[256,512]{1,0:T(8,128)(2,1)S(1)}, u32[]{:S(2)}, u32[]{:S(2)}) collective-permute-start(bf16[256,512]{1,0:T(8,128)(2,1)S(1)} %pad_maximum_fusion), channel_id=1, source_target_pairs={{0,1},{1,0},{2,3},{3,2},{4,5},{5,4},{6,7},{7,6},{8,9},{9,8},{10,11... | collective-permute-start | bytes 786440 | tf_op jit(solution)/shard_map/x_kv/ppermute | solution.py:647
  5.9 22.8 %collective-permute-start.2 = (bf16[256,1536]{1,0:T(8,128)(2,1)S(1)}, bf16[256,1536]{1,0:T(8,128)(2,1)S(1)}, u32[]{:S(2)}, u32[]{:S(2)}) collective-permute-start(bf16[256,1536]{1,0:T(8,128)(2,1)S(1)} %constant_dynamic-slice_fusion), channel_id=1, source_target_pairs={{0,1},{1,0},{2,3},{3,2},{4,5},{5,4},{6,7},{7,6},{8,9},{9,8},{10,11... | collective-permute-start | bytes 2359304 | tf_op jit(solution)/shard_map/x_qa/ppermute | solution.py:647
  11.9 5.8 %copy-start.1 = (bf16[256,512]{1,0:T(8,128)(2,1)}, bf16[256,512]{1,0:T(8,128)(2,1)S(1)}, u32[]{:S(2)}) copy-start(bf16[256,512]{1,0:T(8,128)(2,1)S(1)} %collective-permute-done.kp_ref.vp_ref.kd.vd) | copy-start | bytes 786436
  11.9 23.6 %collective-permute-start.1 = (bf16[256,512]{1,0:T(8,128)(2,1)S(1)}, bf16[256,512]{1,0:T(8,128)(2,1)S(1)}, u32[]{:S(2)}, u32[]{:S(2)}) collective-permute-start(bf16[256,512]{1,0:T(8,128)(2,1)S(1)} %constant_dynamic-slice_fusion.3), channel_id=1, source_target_pairs={{0,1},{1,0},{2,3},{3,2},{4,5},{5,4},{6,7},{7,6},{8,9},{9,8},{10,11... | collective-permute-start | bytes 786440 | tf_op jit(solution)/shard_map/x_qb/ppermute | solution.py:647
  28.8 0.9 copy-start.2
  35.5 0.7 copy-start.7
  40.2 7.1 %collective-permute-start.3 = (bf16[24,2048]{1,0:T(8,128)(2,1)}, bf16[24,2048]{1,0:T(8,128)(2,1)S(1)}, u32[]{:S(2)}, u32[]{:S(2)}) collective-permute-start(bf16[24,2048]{1,0:T(8,128)(2,1)} %get-tuple-element.47), channel_id=1, source_target_pairs={{0,2},{2,0},{4,6},{6,4},{8,10},{10,8},{12,14},{14,12},{16,18},{18,... | collective-permute-start | bytes 294920 | tf_op jit(solution)/shard_map/far_e1/ppermute | solution.py:651
  40.3 7.9 %collective-permute-start.4 = (bf16[24,2048]{1,0:T(8,128)(2,1)}, bf16[24,2048]{1,0:T(8,128)(2,1)S(1)}, u32[]{:S(2)}, u32[]{:S(2)}) collective-permute-start(bf16[24,2048]{1,0:T(8,128)(2,1)} %get-tuple-element.48), channel_id=1, source_target_pairs={{0,4},{2,6},{4,0},{6,2},{8,12},{10,14},{12,8},{14,10},{16,20},{18,... | collective-permute-start | bytes 294920 | tf_op jit(solution)/shard_map/far_e2/ppermute | solution.py:651
  43.3 6.0 %collective-permute-start.9 = (f32[16,256]{1,0:T(8,128)}, f32[16,256]{1,0:T(8,128)S(1)}, u32[]{:S(2)}, u32[]{:S(2)}) collective-permute-start(f32[16,256]{1,0:T(8,128)} %get-tuple-element.58.mine_ref), channel_id=1, source_target_pairs={{0,1},{1,0},{2,3},{3,2},{4,5},{5,4},{6,7},{7,6},{8,9},{9,8},{10,11... | collective-permute-start | bytes 49160 | tf_op jit(solution)/shard_map/x_sums/ppermute | solution.py:647
  43.4 13.1 %collective-permute-start.6 = (bf16[24,2048]{1,0:T(8,128)(2,1)}, bf16[24,2048]{1,0:T(8,128)(2,1)S(1)}, u32[]{:S(2)}, u32[]{:S(2)}) collective-permute-start(bf16[24,2048]{1,0:T(8,128)(2,1)} %get-tuple-element.51), channel_id=1, source_target_pairs={{0,16},{2,18},{4,20},{6,22},{8,24},{10,26},{12,28},{14,30},{16,0},... | collective-permute-start | bytes 294920 | tf_op jit(solution)/shard_map/far_e8/ppermute | solution.py:651
  46.0 9.7 %collective-permute-start.8 = (bf16[24,2048]{1,0:T(8,128)(2,1)}, bf16[24,2048]{1,0:T(8,128)(2,1)S(1)}, u32[]{:S(2)}, u32[]{:S(2)}) collective-permute-start(bf16[24,2048]{1,0:T(8,128)(2,1)} %get-tuple-element.54), channel_id=1, source_target_pairs={{0,24},{2,26},{4,28},{6,30},{8,16},{10,18},{12,20},{14,22},{16,8},... | collective-permute-start | bytes 294920 | tf_op jit(solution)/shard_map/far_e12/ppermute | solution.py:651
  47.3 11.7 %collective-permute-start.7 = (bf16[24,2048]{1,0:T(8,128)(2,1)}, bf16[24,2048]{1,0:T(8,128)(2,1)S(1)}, u32[]{:S(2)}, u32[]{:S(2)}) collective-permute-start(bf16[24,2048]{1,0:T(8,128)(2,1)} %get-tuple-element.53), channel_id=1, source_target_pairs={{0,18},{2,16},{4,22},{6,20},{8,26},{10,24},{12,30},{14,28},{16,2},... | collective-permute-start | bytes 294920 | tf_op jit(solution)/shard_map/far_e9/ppermute | solution.py:651
  48.2 8.3 %collective-permute-start.5 = (bf16[24,2048]{1,0:T(8,128)(2,1)}, bf16[24,2048]{1,0:T(8,128)(2,1)S(1)}, u32[]{:S(2)}, u32[]{:S(2)}) collective-permute-start(bf16[24,2048]{1,0:T(8,128)(2,1)} %get-tuple-element.50), channel_id=1, source_target_pairs={{0,6},{2,4},{4,2},{6,0},{8,14},{10,12},{12,10},{14,8},{16,22},{18,... | collective-permute-start | bytes 294920 | tf_op jit(solution)/shard_map/far_e3/ppermute | solution.py:651
  49.3 6.4 %copy-start.5 = (bf16[48,2048]{1,0:T(8,128)(2,1)}, bf16[48,2048]{1,0:T(8,128)(2,1)S(1)}, u32[]{:S(2)}) copy-start(bf16[48,2048]{1,0:T(8,128)(2,1)S(1)} %constant_dynamic-update-slice_fusion.refs_0_) | copy-start | bytes 589828
  49.3 2.0 %copy-start.20 = (f32[16,256]{1,0:T(8,128)}, f32[16,256]{1,0:T(8,128)S(1)}, u32[]{:S(2)}) copy-start(f32[16,256]{1,0:T(8,128)S(1)} %collective-permute-done.9.theirs_ref) | copy-start | bytes 49156
  49.3 7.2 %collective-permute-start.11 = (bf16[48,2048]{1,0:T(8,128)(2,1)S(1)}, bf16[48,2048]{1,0:T(8,128)(2,1)S(1)}, u32[]{:S(2)}, u32[]{:S(2)}) collective-permute-start(bf16[48,2048]{1,0:T(8,128)(2,1)S(1)} %constant_dynamic-update-slice_fusion.refs_0_), channel_id=1, source_target_pairs={{0,1},{1,0},{2,3},{3,2},{4,5},{5,4},{6,7},{7,6},{8,9},{9,8},{10,11... | collective-permute-start | bytes 589832 | tf_op jit(solution)/shard_map/x_0/ppermute | solution.py:647
  51.3 4.3 %copy-start.23 = (bf16[24,2048]{1,0:T(8,128)(2,1)S(1)}, bf16[24,2048]{1,0:T(8,128)(2,1)}, u32[]{:S(2)}) copy-start(bf16[24,2048]{1,0:T(8,128)(2,1)} %get-tuple-element.61) | copy-start | bytes 294916
  55.7 6.8 %collective-permute-start.10 = (bf16[24,2048]{1,0:T(8,128)(2,1)S(1)}, bf16[24,2048]{1,0:T(8,128)(2,1)S(1)}, u32[]{:S(2)}, u32[]{:S(2)}) collective-permute-start(bf16[24,2048]{1,0:T(8,128)(2,1)S(1)} %copy-done.23), channel_id=1, source_target_pairs={{0,26},{2,24},{4,30},{6,28},{8,18},{10,16},{12,22},{14,20},{16,10}... | collective-permute-start | bytes 294920 | tf_op jit(solution)/shard_map/far_e13/ppermute | solution.py:651
  56.5 20.8 %copy-start.16 = (bf16[48,2048]{1,0:T(8,128)(2,1)}, bf16[48,2048]{1,0:T(8,128)(2,1)S(1)}, u32[]{:S(2)}) copy-start(bf16[48,2048]{1,0:T(8,128)(2,1)S(1)} %collective-permute-done.11.refs_4_) | copy-start | bytes 589828
  56.5 4.1 %collective-permute-start.15 = (bf16[96,2048]{1,0:T(8,128)(2,1)}, bf16[96,2048]{1,0:T(8,128)(2,1)S(1)}, u32[]{:S(2)}, u32[]{:S(2)}) collective-permute-start(bf16[96,2048]{1,0:T(8,128)(2,1)} %get-tuple-element.66), channel_id=1, source_target_pairs={{0,2},{2,0},{4,6},{6,4},{8,10},{10,8},{12,14},{14,12},{16,18},{18,... | collective-permute-start | bytes 1179656 | tf_op jit(solution)/shard_map/far_core/ppermute | solution.py:651
  56.9 20.4 %copy-start.4 = (bf16[48,2048]{1,0:T(8,128)(2,1)}, bf16[48,2048]{1,0:T(8,128)(2,1)S(1)}, u32[]{:S(2)}) copy-start(bf16[48,2048]{1,0:T(8,128)(2,1)S(1)} %constant_dynamic-update-slice_fusion.2.refs_1_) | copy-start | bytes 589828
  56.9 7.2 %collective-permute-start.12 = (bf16[48,2048]{1,0:T(8,128)(2,1)S(1)}, bf16[48,2048]{1,0:T(8,128)(2,1)S(1)}, u32[]{:S(2)}, u32[]{:S(2)}) collective-permute-start(bf16[48,2048]{1,0:T(8,128)(2,1)S(1)} %constant_dynamic-update-slice_fusion.2.refs_1_), channel_id=1, source_target_pairs={{0,1},{1,0},{2,3},{3,2},{4,5},{5,4},{6,7},{7,6},{8,9},{9,8},{10,11... | collective-permute-start | bytes 589832 | tf_op jit(solution)/shard_map/x_2/ppermute | solution.py:647
  59.1 18.2 %copy-start.6 = (bf16[48,2048]{1,0:T(8,128)(2,1)}, bf16[48,2048]{1,0:T(8,128)(2,1)S(1)}, u32[]{:S(2)}) copy-start(bf16[48,2048]{1,0:T(8,128)(2,1)S(1)} %constant_dynamic-update-slice_fusion.4.refs_2_) | copy-start | bytes 589828
  59.1 21.6 %collective-permute-start.13 = (bf16[48,2048]{1,0:T(8,128)(2,1)S(1)}, bf16[48,2048]{1,0:T(8,128)(2,1)S(1)}, u32[]{:S(2)}, u32[]{:S(2)}) collective-permute-start(bf16[48,2048]{1,0:T(8,128)(2,1)S(1)} %constant_dynamic-update-slice_fusion.4.refs_2_), channel_id=1, source_target_pairs={{0,1},{1,0},{2,3},{3,2},{4,5},{5,4},{6,7},{7,6},{8,9},{9,8},{10,11... | collective-permute-start | bytes 589832 | tf_op jit(solution)/shard_map/x_8/ppermute | solution.py:647
  64.1 13.2 %copy-start.17 = (bf16[48,2048]{1,0:T(8,128)(2,1)}, bf16[48,2048]{1,0:T(8,128)(2,1)S(1)}, u32[]{:S(2)}) copy-start(bf16[48,2048]{1,0:T(8,128)(2,1)S(1)} %collective-permute-done.12.refs_5_) | copy-start | bytes 589828
  64.1 16.6 %collective-permute-start.16 = (bf16[48,2048]{1,0:T(8,128)(2,1)S(1)}, bf16[48,2048]{1,0:T(8,128)(2,1)S(1)}, u32[]{:S(2)}, u32[]{:S(2)}) collective-permute-start(bf16[48,2048]{1,0:T(8,128)(2,1)S(1)} %get-tuple-element.67), channel_id=1, source_target_pairs={{0,8},{2,10},{4,12},{6,14},{8,0},{10,2},{12,4},{14,6},{16,24},{18,... | collective-permute-start | bytes 589832 | tf_op jit(solution)/shard_map/far_4/ppermute | solution.py:651
  70.9 6.4 %copy-start.3 = (bf16[48,2048]{1,0:T(8,128)(2,1)}, bf16[48,2048]{1,0:T(8,128)(2,1)S(1)}, u32[]{:S(2)}) copy-start(bf16[48,2048]{1,0:T(8,128)(2,1)S(1)} %constant_dynamic-update-slice_fusion.6.refs_3_) | copy-start | bytes 589828
  70.9 9.9 %collective-permute-start.14 = (bf16[48,2048]{1,0:T(8,128)(2,1)S(1)}, bf16[48,2048]{1,0:T(8,128)(2,1)S(1)}, u32[]{:S(2)}, u32[]{:S(2)}) collective-permute-start(bf16[48,2048]{1,0:T(8,128)(2,1)S(1)} %constant_dynamic-update-slice_fusion.6.refs_3_), channel_id=1, source_target_pairs={{0,1},{1,0},{2,3},{3,2},{4,5},{5,4},{6,7},{7,6},{8,9},{9,8},{10,11... | collective-permute-start | bytes 589832 | tf_op jit(solution)/shard_map/x_12/ppermute | solution.py:647
  73.0 15.5 %collective-permute-start.20 = (bf16[48,2048]{1,0:T(8,128)(2,1)S(1)}, bf16[48,2048]{1,0:T(8,128)(2,1)S(1)}, u32[]{:S(2)}, u32[]{:S(2)}) collective-permute-start(bf16[48,2048]{1,0:T(8,128)(2,1)S(1)} %get-tuple-element.71), channel_id=1, source_target_pairs={{0,20},{2,22},{4,16},{6,18},{8,28},{10,30},{12,24},{14,26},{16,4},... | collective-permute-start | bytes 589832 | tf_op jit(solution)/shard_map/far_10/ppermute | solution.py:651
  77.3 16.8 %collective-permute-start.22 = (bf16[48,2048]{1,0:T(8,128)(2,1)S(1)}, bf16[48,2048]{1,0:T(8,128)(2,1)S(1)}, u32[]{:S(2)}, u32[]{:S(2)}) collective-permute-start(bf16[48,2048]{1,0:T(8,128)(2,1)S(1)} %get-tuple-element.73), channel_id=1, source_target_pairs={{0,28},{2,30},{4,24},{6,26},{8,20},{10,22},{12,16},{14,18},{16,12}... | collective-permute-start | bytes 589832 | tf_op jit(solution)/shard_map/far_14/ppermute | solution.py:651
  80.7 7.8 %copy-start.18 = (bf16[48,2048]{1,0:T(8,128)(2,1)}, bf16[48,2048]{1,0:T(8,128)(2,1)S(1)}, u32[]{:S(2)}) copy-start(bf16[48,2048]{1,0:T(8,128)(2,1)S(1)} %collective-permute-done.13.refs_6_) | copy-start | bytes 589828
  80.7 13.8 %copy-start.12 = (bf16[48,2048]{1,0:T(8,128)(2,1)}, bf16[48,2048]{1,0:T(8,128)(2,1)S(1)}, u32[]{:S(2)}) copy-start(bf16[48,2048]{1,0:T(8,128)(2,1)S(1)} %collective-permute-done.16.refs_2_) | copy-start | bytes 589828
  80.7 11.4 %collective-permute-start.17 = (bf16[48,2048]{1,0:T(8,128)(2,1)S(1)}, bf16[48,2048]{1,0:T(8,128)(2,1)S(1)}, u32[]{:S(2)}, u32[]{:S(2)}) collective-permute-start(bf16[48,2048]{1,0:T(8,128)(2,1)S(1)} %collective-permute-done.16.refs_2_), channel_id=1, source_target_pairs={{0,1},{1,0},{2,3},{3,2},{4,5},{5,4},{6,7},{7,6},{8,9},{9,8},{10,11... | collective-permute-start | bytes 589832 | tf_op jit(solution)/shard_map/x_4/ppermute | solution.py:647
  80.8 11.3 %collective-permute-start.18 = (bf16[48,2048]{1,0:T(8,128)(2,1)S(1)}, bf16[48,2048]{1,0:T(8,128)(2,1)S(1)}, u32[]{:S(2)}, u32[]{:S(2)}) collective-permute-start(bf16[48,2048]{1,0:T(8,128)(2,1)S(1)} %get-tuple-element.69), channel_id=1, source_target_pairs={{0,12},{2,14},{4,8},{6,10},{8,4},{10,6},{12,0},{14,2},{16,28},{18,... | collective-permute-start | bytes 589832 | tf_op jit(solution)/shard_map/far_6/ppermute | solution.py:651
  80.8 7.6 %copy-start.19 = (bf16[48,2048]{1,0:T(8,128)(2,1)}, bf16[48,2048]{1,0:T(8,128)(2,1)S(1)}, u32[]{:S(2)}) copy-start(bf16[48,2048]{1,0:T(8,128)(2,1)S(1)} %collective-permute-done.14.refs_7_) | copy-start | bytes 589828
  88.5 6.0 %copy-start.13 = (bf16[48,2048]{1,0:T(8,128)(2,1)}, bf16[48,2048]{1,0:T(8,128)(2,1)S(1)}, u32[]{:S(2)}) copy-start(bf16[48,2048]{1,0:T(8,128)(2,1)S(1)} %collective-permute-done.20.refs_4_) | copy-start | bytes 589828
  88.5 5.7 %collective-permute-start.21 = (bf16[48,2048]{1,0:T(8,128)(2,1)S(1)}, bf16[48,2048]{1,0:T(8,128)(2,1)S(1)}, u32[]{:S(2)}, u32[]{:S(2)}) collective-permute-start(bf16[48,2048]{1,0:T(8,128)(2,1)S(1)} %collective-permute-done.20.refs_4_), channel_id=1, source_target_pairs={{0,1},{1,0},{2,3},{3,2},{4,5},{5,4},{6,7},{7,6},{8,9},{9,8},{10,11... | collective-permute-start | bytes 589832 | tf_op jit(solution)/shard_map/x_10/ppermute | solution.py:647
  92.1 11.0 %copy-start.8 = (bf16[48,2048]{1,0:T(8,128)(2,1)}, bf16[48,2048]{1,0:T(8,128)(2,1)S(1)}, u32[]{:S(2)}) copy-start(bf16[48,2048]{1,0:T(8,128)(2,1)S(1)} %collective-permute-done.17.refs_1_) | copy-start | bytes 589828
  92.1 2.3 %copy-start.15 = (bf16[48,2048]{1,0:T(8,128)(2,1)}, bf16[48,2048]{1,0:T(8,128)(2,1)S(1)}, u32[]{:S(2)}) copy-start(bf16[48,2048]{1,0:T(8,128)(2,1)S(1)} %collective-permute-done.18.refs_3_) | copy-start | bytes 589828
  92.1 11.0 %collective-permute-start.19 = (bf16[48,2048]{1,0:T(8,128)(2,1)S(1)}, bf16[48,2048]{1,0:T(8,128)(2,1)S(1)}, u32[]{:S(2)}, u32[]{:S(2)}) collective-permute-start(bf16[48,2048]{1,0:T(8,128)(2,1)S(1)} %collective-permute-done.18.refs_3_), channel_id=1, source_target_pairs={{0,1},{1,0},{2,3},{3,2},{4,5},{5,4},{6,7},{7,6},{8,9},{9,8},{10,11... | collective-permute-start | bytes 589832 | tf_op jit(solution)/shard_map/x_6/ppermute | solution.py:647
  94.2 0.7 copy-start.14
  94.2 9.0 %copy-start.9 = (bf16[48,2048]{1,0:T(8,128)(2,1)}, bf16[48,2048]{1,0:T(8,128)(2,1)S(1)}, u32[]{:S(2)}) copy-start(bf16[48,2048]{1,0:T(8,128)(2,1)S(1)} %collective-permute-done.21.refs_3_) | copy-start | bytes 589828
  94.2 8.9 %collective-permute-start.23 = (bf16[48,2048]{1,0:T(8,128)(2,1)S(1)}, bf16[48,2048]{1,0:T(8,128)(2,1)S(1)}, u32[]{:S(2)}, u32[]{:S(2)}) collective-permute-start(bf16[48,2048]{1,0:T(8,128)(2,1)S(1)} %collective-permute-done.22.refs_5_), channel_id=1, source_target_pairs={{0,1},{1,0},{2,3},{3,2},{4,5},{5,4},{6,7},{7,6},{8,9},{9,8},{10,11... | collective-permute-start | bytes 589832 | tf_op jit(solution)/shard_map/x_14/ppermute | solution.py:647
  103.1 0.7 copy-start.10
  103.1 0.7 copy-start.11
